TPU v7x, 512 devices: a whole 4x8x8 slice. The times are simulated.
512 devices in a mesh: gz: 32 (over z_hi, x, core), gy: 16 (over z_lo, y).
Axes of the slice: x: 4, y: 8, z: 8 (z_hi: 4, z_lo: 2; z = z_hi * 2 + z_lo), core: 2. Of those that a mesh axis runs over, the one named last changes fastest.
Arguments:
- filtered: bfloat16 [16, 256, 4096], P(None, 'gz', 'gy'), may hold values from -6 to 6
- angle_index: int32 [16], replicated, may hold values from 0 to 3599
- band_offset: int32 [16, 32], P(None, 'gz'), may hold values from 0 to 12, as said below
- band_length: int32 [16, 32], P(None, 'gz'), may hold values from 4 to 12
- foot_block: int32 [16, 64, 64], P(None, 'gy'), may hold values from 0 to 62, as said below
Outputs:
- denoised: float32 [64, 256, 4096], P('gy', 'gz')
Inputs may be any that keep to these rules, and one draw needn't show every extreme that they name: band_offset + band_length <= 16 for every projection and group. foot_block[p, y, b] is b plus a shift of -2 to 2 that depends only on p and y, clipped to the range.
All inputs are finite; a program needn't handle non-finite values.
Results may differ from a plain program's by a relative error of at most 0.0041.
Values may be sent and summed in bfloat16 or wider, within the bound.
A program may use at most 64 MiB of HBM per device.

v0:
```python
import math

import jax
import jax.numpy as jnp
from jax import lax
from jax.sharding import PartitionSpec as P

X = 4096
P_SIZE = 16
NANG = 3600
BLOCK = 64
ITERS = 2


step_length = 0.25
smooth_weight = 0.3
gradient_floor = 0.01
shift_reach = 8.0


def with_halo(cells, sides, width):
    for axis, dim in sides:
        count = lax.axis_size(axis)
        ends = count - 1
        head = lax.slice_in_dim(cells, 0, width, axis=dim)
        tail = lax.slice_in_dim(cells, cells.shape[dim] - width, cells.shape[dim], axis=dim)
        cells = jnp.concatenate(
            [
                lax.ppermute(tail, axis, [(i, (i + 1) % count) for i in range(ends)]),
                cells,
                lax.ppermute(head, axis, [((i + 1) % count, i) for i in range(ends)]),
            ],
            axis=dim,
        )
    return cells


def geometry(angle_value):
    radians = 2.0 * math.pi * angle_value.astype(jnp.float32) / NANG
    stretch = 0.5 + 0.5 * jnp.abs(jnp.cos(radians))
    spread = 1.0 + jnp.abs(jnp.sin(radians))
    return (radians, stretch, spread)


def footprint(radians, stretch, spread, row_global, rows_total, block_size):
    shifted = shift_reach * jnp.sin(radians + 2.0 * math.pi * row_global / rows_total)
    inside = jnp.arange(block_size).astype(jnp.float32) - 0.5 * (block_size - 1)
    centre = block_size + inside[None, :] * stretch + shifted[:, None]
    places = jnp.arange(2 * block_size).astype(jnp.float32) + 0.5
    weights = (
        jnp.maximum(0.0, 1.0 - jnp.abs(places[None, None, :] - centre[:, :, None]) / spread)
        / spread
    )
    return weights.astype(jnp.bfloat16)


def axial_table(offsets, lengths, depth_count):
    offset_real = offsets.astype(jnp.float32)[..., None]
    length_real = lengths.astype(jnp.float32)[..., None]
    depth_place = jnp.arange(depth_count).astype(jnp.float32) + 0.5
    centre = offset_real + depth_place * length_real / depth_count
    row_number = jnp.arange(2 * depth_count)
    row_place = row_number.astype(jnp.float32) + 0.5
    triangle = jnp.maximum(0.0, 1.0 - jnp.abs(row_place - centre[..., None]))
    inside = (row_number >= offsets[..., None, None]) & (
        row_number < (offsets + lengths)[..., None, None]
    )
    return jnp.where(inside, triangle, 0.0).astype(jnp.bfloat16)


def smooth_update(current, fidelity, row_first, depth_first, rows_total, depth_total):
    row_index = row_first + jnp.arange(current.shape[0])
    depth_index = depth_first + jnp.arange(current.shape[1])
    keep_rows = ((row_index >= 0) & (row_index < rows_total - 1)).astype(jnp.float32)[:, None, None]
    keep_depth = ((depth_index >= 0) & (depth_index < depth_total - 1)).astype(jnp.float32)[
        None, :, None
    ]
    forward_rows = (
        jnp.concatenate([current[1:] - current[:-1], jnp.zeros_like(current[:1])], 0) * keep_rows
    )
    forward_depth = (
        jnp.concatenate([current[:, 1:] - current[:, :-1], jnp.zeros_like(current[:, :1])], 1)
        * keep_depth
    )
    forward_width = jnp.concatenate(
        [current[:, :, 1:] - current[:, :, :-1], jnp.zeros_like(current[:, :, :1])], 2
    )
    magnitude = jnp.sqrt(
        forward_rows * forward_rows
        + forward_depth * forward_depth
        + forward_width * forward_width
        + gradient_floor
    )
    normal_rows = forward_rows / magnitude
    normal_depth = forward_depth / magnitude
    normal_width = forward_width / magnitude
    divergence = normal_rows - jnp.concatenate(
        [jnp.zeros_like(normal_rows[:1]), normal_rows[:-1]], 0
    )
    divergence = (
        divergence
        + normal_depth
        - jnp.concatenate([jnp.zeros_like(normal_depth[:, :1]), normal_depth[:, :-1]], 1)
    )
    divergence = (
        divergence
        + normal_width
        - jnp.concatenate([jnp.zeros_like(normal_width[:, :, :1]), normal_width[:, :, :-1]], 2)
    )
    return current + step_length * (smooth_weight * divergence - (current - fidelity))


def per_device(filtered, angle_index, band_offset, band_length, foot_block):
    depth_count = filtered.shape[1]
    row_count = foot_block.shape[1]
    extended_band = with_halo(filtered, (("gz", 1),), depth_count // 2)
    axial_weights = axial_table(band_offset[:, 0], band_length[:, 0], depth_count)
    summed_rows = jnp.einsum(
        "pzv,pvu->pzu",
        axial_weights,
        lax.all_gather(extended_band, "gy", axis=2, tiled=True),
        preferred_element_type=jnp.float32,
    )
    columns = summed_rows.astype(jnp.bfloat16)
    column_count = columns.shape[2]
    row_base = lax.axis_index("gy") * row_count
    depth_base = lax.axis_index("gz") * depth_count
    rows_total = lax.axis_size("gy") * row_count
    depth_total = lax.axis_size("gz") * depth_count
    row_global = (row_base + jnp.arange(row_count)).astype(jnp.float32)

    def one_projection(running, inputs):
        projected, angle_value, blocks = inputs
        radians, stretch, spread = geometry(angle_value)
        weights = footprint(radians, stretch, spread, row_global, rows_total, BLOCK)
        column_tiles = projected.reshape(depth_count, column_count // BLOCK, BLOCK)
        window = jnp.concatenate([column_tiles[:, blocks], column_tiles[:, blocks + 1]], axis=-1)
        product = jnp.einsum("yiu,zybu->yzbi", weights, window, preferred_element_type=jnp.float32)
        return (running + product.reshape(running.shape), None)

    initial = jnp.zeros((row_count, depth_count, X), jnp.float32)
    summed, _unused = lax.scan(one_projection, initial, (columns, angle_index, foot_block))
    backprojection = math.pi / P_SIZE * summed
    current = backprojection
    padded_fidelity = jnp.pad(backprojection, ((1, 1), (1, 1), (0, 0)))
    for turn_index in range(ITERS):
        extended = with_halo(current, (("gz", 1), ("gy", 0)), 1)
        updated = smooth_update(
            extended, padded_fidelity, row_base - 1, depth_base - 1, rows_total, depth_total
        )
        current = updated[1:-1, 1:-1]
    return current


def solution(mesh):
    return jax.shard_map(
        per_device,
        mesh=mesh,
        in_specs=(P(None, "gz", "gy"), P(), P(None, "gz"), P(None, "gz"), P(None, "gy", None)),
        out_specs=P("gy", "gz", None),
        check_vma=False,
    )
```

profile of v0, /device:TPU:191, one launch (start us, length us, event | category | flops | bytes accessed | tf_op | source)
XLA Modules:
  0.0 257.0 jit_solution(1076519616723766050)
XLA Ops:
  7.5 7.5 %collective-permute-start = (bf16[16,4,256]{2,1,0:T(4,128)(2,1)S(1)}, bf16[16,4,256]{2,1,0:T(4,128)(2,1)S(1)}, u32[]{:S(2)}, u32[]{:S(2)}) collective-permute-start(bf16[16,4,256]{2,1,0:T(4,128)(2,1)S(1)} %get-tuple-element.140), channel_id=1, source_target_pairs={{0,16},{16,32},{32,48},{48,64},{64,80},{80,96},{96,112},{112,128},... | collective-permute-start | bytes 98312 | tf_op jit(solution)/shard_map/ppermute | solution.py:29
  15.0 1.9 collective-permute-start.1
  16.9 7.5 %collective-permute-done.1 = bf16[16,4,256]{2,1,0:T(4,128)(2,1)S(1)} collective-permute-done((bf16[16,4,256]{2,1,0:T(4,128)(2,1)S(1)}, bf16[16,4,256]{2,1,0:T(4,128)(2,1)S(1)}, u32[]{:S(2)}, u32[]{:S(2)}) %collective-permute-start.1) | collective-permute-done | bytes 32800 | tf_op jit(solution)/shard_map/ppermute | solution.py:31
  24.4 1.6 pad_maximum_fusion.8
  28.2 60.6 %all-gather.2.cloned.1.call-done = bf16[16,16,4096]{2,1,0:T(8,128)(2,1)} async-done(((bf16[16,16,256]{2,1,0:T(8,128)(2,1)}), bf16[16,16,4096]{2,1,0:T(8,128)(2,1)}) %all-gather.2.cloned.1.call-update) | async-done | bytes 2097168 | tf_op jit(solution)/shard_map/all_gather | solution.py:121
  88.8 2.1 convolution_convert_fusion
  90.9 90.2 %while.13 = (s32[]{:T(128)}, f32[4,8,4096]{2,1,0:T(8,128)S(1)}, bf16[16,8,4096]{2,1,0:T(8,128)(2,1)S(1)}, s32[16,4,64]{2,1,0:T(4,128)}, s32[16]{0:T(128)S(1)}, /...) while((s32[]{:T(128)}, f32[4,8,4096]{2,1,0:T(8,128)S(1)}, ...), condition=%wide.region_1.2_spmd.clone, body=%wide.region_0.1_spmd.clone.sunk | while | flops 35099164 | bytes 6183707 | solution.py:142
  181.3 15.5 %collective-permute-start.2 = (f32[4,1,4096]{2,1,0:T(1,128)S(1)}, f32[4,1,4096]{2,1,0:T(1,128)S(1)}, u32[]{:S(2)}, u32[]{:S(2)}) collective-permute-start(f32[4,1,4096]{2,1,0:T(1,128)S(1)} %get-tuple-element.138), channel_id=1, source_target_pairs={{0,16},{16,32},{32,48},{48,64},{64,80},{80,96},{96,112},{112,128},... | collective-permute-start | bytes 196616 | tf_op jit(solution)/shard_map/ppermute | solution.py:29
  196.8 1.9 collective-permute-start.3
  198.8 8.6 %collective-permute-done.3 = f32[4,1,4096]{2,1,0:T(1,128)S(1)} collective-permute-done((f32[4,1,4096]{2,1,0:T(1,128)S(1)}, f32[4,1,4096]{2,1,0:T(1,128)S(1)}, u32[]{:S(2)}, u32[]{:S(2)}) %collective-permute-start.3) | collective-permute-done | bytes 65568 | tf_op jit(solution)/shard_map/ppermute | solution.py:31
  207.4 1.9 collective-permute-start.4
  209.4 3.4 %collective-permute-start.5 = (f32[1,10,4096]{2,1,0:T(8,128)S(1)}, f32[1,10,4096]{2,1,0:T(8,128)S(1)}, u32[]{:S(2)}, u32[]{:S(2)}) collective-permute-start(f32[1,10,4096]{2,1,0:T(8,128)S(1)} %get-tuple-element.137), channel_id=1, source_target_pairs={{1,0},{2,1},{3,2},{4,3},{5,4},{6,5},{7,6},{8,7},{9,8},{10,9},{11,1... | collective-permute-start | bytes 491528 | tf_op jit(solution)/shard_map/ppermute | solution.py:31
  212.8 1.8 collective-permute-done.4
  214.5 4.0 %collective-permute-done.5 = f32[1,10,4096]{2,1,0:T(8,128)S(1)} collective-permute-done((f32[1,10,4096]{2,1,0:T(8,128)S(1)}, f32[1,10,4096]{2,1,0:T(8,128)S(1)}, u32[]{:S(2)}, u32[]{:S(2)}) %collective-permute-start.5) | collective-permute-done | bytes 163872 | tf_op jit(solution)/shard_map/ppermute | solution.py:31
  220.9 1.2 multiply_add_fusion.1
  222.2 2.9 %collective-permute-start.6 = (f32[4,1,4096]{2,1,0:T(1,128)S(1)}, f32[4,1,4096]{2,1,0:T(1,128)S(1)}, u32[]{:S(2)}, u32[]{:S(2)}) collective-permute-start(f32[4,1,4096]{2,1,0:T(1,128)S(1)} %get-tuple-element.132), channel_id=1, source_target_pairs={{0,16},{16,32},{32,48},{48,64},{64,80},{80,96},{96,112},{112,128},... | collective-permute-start | bytes 196616 | tf_op jit(solution)/shard_map/ppermute | solution.py:29
  225.1 1.9 collective-permute-start.7
  227.1 7.8 %collective-permute-done.7 = f32[4,1,4096]{2,1,0:T(1,128)S(1)} collective-permute-done((f32[4,1,4096]{2,1,0:T(1,128)S(1)}, f32[4,1,4096]{2,1,0:T(1,128)S(1)}, u32[]{:S(2)}, u32[]{:S(2)}) %collective-permute-start.7) | collective-permute-done | bytes 65568 | tf_op jit(solution)/shard_map/ppermute | solution.py:31
  235.0 1.9 collective-permute-start.8
  237.0 3.4 %collective-permute-start.9 = (f32[1,10,4096]{2,1,0:T(8,128)S(1)}, f32[1,10,4096]{2,1,0:T(8,128)S(1)}, u32[]{:S(2)}, u32[]{:S(2)}) collective-permute-start(f32[1,10,4096]{2,1,0:T(8,128)S(1)} %get-tuple-element.135), channel_id=1, source_target_pairs={{1,0},{2,1},{3,2},{4,3},{5,4},{6,5},{7,6},{8,7},{9,8},{10,9},{11,1... | collective-permute-start | bytes 491528 | tf_op jit(solution)/shard_map/ppermute | solution.py:31
  240.3 1.8 collective-permute-done.8
  242.2 4.0 %collective-permute-done.9 = f32[1,10,4096]{2,1,0:T(8,128)S(1)} collective-permute-done((f32[1,10,4096]{2,1,0:T(8,128)S(1)}, f32[1,10,4096]{2,1,0:T(8,128)S(1)}, u32[]{:S(2)}, u32[]{:S(2)}) %collective-permute-start.9) | collective-permute-done | bytes 163872 | tf_op jit(solution)/shard_map/ppermute | solution.py:31
  247.3 1.1 fusion.20
  249.0 1.2 fusion.25
  (339 shorter events, 83.4 us)
Async XLA Ops:
  6.5 82.3 %all-gather.2.cloned.1.call-start = ((), (), s32[]{:S(2)}) async-start(), calls=%async_computation | async-start | bytes 2228224 | tf_op jit(solution)/shard_map/all_gather | solution.py:121
  7.5 9.4 %collective-permute-start = (bf16[16,4,256]{2,1,0:T(4,128)(2,1)S(1)}, bf16[16,4,256]{2,1,0:T(4,128)(2,1)S(1)}, u32[]{:S(2)}, u32[]{:S(2)}) collective-permute-start(bf16[16,4,256]{2,1,0:T(4,128)(2,1)S(1)} %get-tuple-element.140), channel_id=1, source_target_pairs={{0,16},{16,32},{32,48},{48,64},{64,80},{80,96},{96,112},{112,128},... | collective-permute-start | bytes 98312 | tf_op jit(solution)/shard_map/ppermute | solution.py:29
  15.0 9.5 %collective-permute-start.1 = (bf16[16,4,256]{2,1,0:T(4,128)(2,1)S(1)}, bf16[16,4,256]{2,1,0:T(4,128)(2,1)S(1)}, u32[]{:S(2)}, u32[]{:S(2)}) collective-permute-start(bf16[16,4,256]{2,1,0:T(4,128)(2,1)S(1)} %get-tuple-element.141), channel_id=1, source_target_pairs={{16,0},{32,16},{48,32},{64,48},{80,64},{96,80},{112,96},{128,112},... | collective-permute-start | bytes 98312 | tf_op jit(solution)/shard_map/ppermute | solution.py:31
  28.2 62.7 %copy-start = (s32[16]{0:T(128)S(1)}, s32[16]{0:T(128)}, u32[]{:S(2)}) copy-start(s32[16]{0:T(128)} %param.8) | copy-start | bytes 196
  181.3 17.5 %collective-permute-start.2 = (f32[4,1,4096]{2,1,0:T(1,128)S(1)}, f32[4,1,4096]{2,1,0:T(1,128)S(1)}, u32[]{:S(2)}, u32[]{:S(2)}) collective-permute-start(f32[4,1,4096]{2,1,0:T(1,128)S(1)} %get-tuple-element.138), channel_id=1, source_target_pairs={{0,16},{16,32},{32,48},{48,64},{64,80},{80,96},{96,112},{112,128},... | collective-permute-start | bytes 196616 | tf_op jit(solution)/shard_map/ppermute | solution.py:29
  196.8 10.5 %collective-permute-start.3 = (f32[4,1,4096]{2,1,0:T(1,128)S(1)}, f32[4,1,4096]{2,1,0:T(1,128)S(1)}, u32[]{:S(2)}, u32[]{:S(2)}) collective-permute-start(f32[4,1,4096]{2,1,0:T(1,128)S(1)} %get-tuple-element.139), channel_id=1, source_target_pairs={{16,0},{32,16},{48,32},{64,48},{80,64},{96,80},{112,96},{128,112},... | collective-permute-start | bytes 196616 | tf_op jit(solution)/shard_map/ppermute | solution.py:31
  207.4 7.1 %collective-permute-start.4 = (f32[1,10,4096]{2,1,0:T(8,128)S(1)}, f32[1,10,4096]{2,1,0:T(8,128)S(1)}, u32[]{:S(2)}, u32[]{:S(2)}) collective-permute-start(f32[1,10,4096]{2,1,0:T(8,128)S(1)} %get-tuple-element.136), channel_id=1, source_target_pairs={{0,1},{1,2},{2,3},{3,4},{4,5},{5,6},{6,7},{7,8},{8,9},{9,10},{10,1... | collective-permute-start | bytes 491528 | tf_op jit(solution)/shard_map/ppermute | solution.py:29
  209.4 9.2 %collective-permute-start.5 = (f32[1,10,4096]{2,1,0:T(8,128)S(1)}, f32[1,10,4096]{2,1,0:T(8,128)S(1)}, u32[]{:S(2)}, u32[]{:S(2)}) collective-permute-start(f32[1,10,4096]{2,1,0:T(8,128)S(1)} %get-tuple-element.137), channel_id=1, source_target_pairs={{1,0},{2,1},{3,2},{4,3},{5,4},{6,5},{7,6},{8,7},{9,8},{10,9},{11,1... | collective-permute-start | bytes 491528 | tf_op jit(solution)/shard_map/ppermute | solution.py:31
  222.2 4.9 %collective-permute-start.6 = (f32[4,1,4096]{2,1,0:T(1,128)S(1)}, f32[4,1,4096]{2,1,0:T(1,128)S(1)}, u32[]{:S(2)}, u32[]{:S(2)}) collective-permute-start(f32[4,1,4096]{2,1,0:T(1,128)S(1)} %get-tuple-element.132), channel_id=1, source_target_pairs={{0,16},{16,32},{32,48},{48,64},{64,80},{80,96},{96,112},{112,128},... | collective-permute-start | bytes 196616 | tf_op jit(solution)/shard_map/ppermute | solution.py:29
  225.1 9.8 %collective-permute-start.7 = (f32[4,1,4096]{2,1,0:T(1,128)S(1)}, f32[4,1,4096]{2,1,0:T(1,128)S(1)}, u32[]{:S(2)}, u32[]{:S(2)}) collective-permute-start(f32[4,1,4096]{2,1,0:T(1,128)S(1)} %get-tuple-element.133), channel_id=1, source_target_pairs={{16,0},{32,16},{48,32},{64,48},{80,64},{96,80},{112,96},{128,112},... | collective-permute-start | bytes 196616 | tf_op jit(solution)/shard_map/ppermute | solution.py:31
  235.0 7.1 %collective-permute-start.8 = (f32[1,10,4096]{2,1,0:T(8,128)S(1)}, f32[1,10,4096]{2,1,0:T(8,128)S(1)}, u32[]{:S(2)}, u32[]{:S(2)}) collective-permute-start(f32[1,10,4096]{2,1,0:T(8,128)S(1)} %get-tuple-element.134), channel_id=1, source_target_pairs={{0,1},{1,2},{2,3},{3,4},{4,5},{5,6},{6,7},{7,8},{8,9},{9,10},{10,1... | collective-permute-start | bytes 491528 | tf_op jit(solution)/shard_map/ppermute | solution.py:29
  237.0 9.2 %collective-permute-start.9 = (f32[1,10,4096]{2,1,0:T(8,128)S(1)}, f32[1,10,4096]{2,1,0:T(8,128)S(1)}, u32[]{:S(2)}, u32[]{:S(2)}) collective-permute-start(f32[1,10,4096]{2,1,0:T(8,128)S(1)} %get-tuple-element.135), channel_id=1, source_target_pairs={{1,0},{2,1},{3,2},{4,3},{5,4},{6,5},{7,6},{8,7},{9,8},{10,9},{11,1... | collective-permute-start | bytes 491528 | tf_op jit(solution)/shard_map/ppermute | solution.py:31
Sparse Core Ops, SparseCore 0:
  26.1 62.6 all-gather.1
where the time goes:
time: 258 us; the launch traced here: 257 us
  waiting for transfers between devices  96.2 us (37%)
  local copies, waits for them, and re-layouts  54.1 us (21%)
  starting transfers between devices  42.3 us (16%)
  other arithmetic  26.9 us (10%)
  loops' own time  14.3 us (6%)
  between operations  13.7 us (5%)
  matrix products  9.54 us (4%)
    all_gather x1, waiting for transfers between devices, per_device(): lax.all_gather(extended_band, 'gy', axis=2, tiled=True)  60.6 us
    ppermute x5, waiting for transfers between devices, with_halo(): lax.ppermute(head, axis, [((i + 1) % count, i) for i in range(ends)])  32 us
    ppermute x5, starting transfers between devices, with_halo(): lax.ppermute(tail, axis, [(i, (i + 1) % count) for i in range(ends)])  29.8 us
    gather x32, local copies, waits for them, and re-layouts, one_projection(): column_tiles[:, blocks + 1]  17.4 us
    another operation x1, loops' own time, per_device(): lax.scan(one_projection, initial, (columns, angle_index, foot_block))  14.3 us
    gather x16, local copies, waits for them, and re-layouts, one_projection(): column_tiles[:, blocks]  13.1 us
    ppermute x5, starting transfers between devices, with_halo(): lax.ppermute(head, axis, [((i + 1) % count, i) for i in range(ends)])  12.5 us
    select_n x16, other arithmetic, one_projection(): column_tiles[:, blocks]  11 us
  transfers between devices with their start and end apart: 11, of which 8 were waited for; matrix products, arithmetic and copies ran while one was open for 1% of the time, Pallas kernels for 0%

commit v1 on v0

--- a/solution.py
+++ b/solution.py
@@ -118,10 +118,10 @@
     summed_rows = jnp.einsum(
         "pzv,pvu->pzu",
         axial_weights,
-        lax.all_gather(extended_band, "gy", axis=2, tiled=True),
+        extended_band,
         preferred_element_type=jnp.float32,
     )
-    columns = summed_rows.astype(jnp.bfloat16)
+    columns = lax.all_gather(summed_rows.astype(jnp.bfloat16), "gy", axis=2, tiled=True)
     column_count = columns.shape[2]
     row_base = lax.axis_index("gy") * row_count
     depth_base = lax.axis_index("gz") * depth_count

time: 258 us -> 274 us (1.062)
  local copies, waits for them, and re-layouts: 54.1 us -> 77.9 us
  waiting for transfers between devices: 96.2 us -> 89 us
    dynamic_slice x32, local copies, waits for them, and re-layouts: 9.64 us -> 33.5 us  [per_device(): lax.scan(one_projection, initial, (columns, angle_index, foot_block))]
    all_gather x1, waiting for transfers between devices: 60.6 us -> 55.3 us  [per_device(): lax.all_gather(summed_rows.astype(jnp.bfloat16), 'gy', axis=2, tiled=True)]
where the time goes in v1:
time: 274 us; the launch traced here: 272 us
  waiting for transfers between devices  89 us (32%)
  local copies, waits for them, and re-layouts  77.9 us (28%)
  starting transfers between devices  43 us (16%)
  other arithmetic  25.3 us (9%)
  loops' own time  14.1 us (5%)
  between operations  13.7 us (5%)
  matrix products  9.14 us (3%)
    all_gather x1, waiting for transfers between devices, per_device(): lax.all_gather(summed_rows.astype(jnp.bfloat16), 'gy', axis=2, tiled=True)  55.3 us
    dynamic_slice x32, local copies, waits for them, and re-layouts, per_device(): lax.scan(one_projection, initial, (columns, angle_index, foot_block))  33.5 us
    ppermute x5, starting transfers between devices, with_halo(): lax.ppermute(tail, axis, [(i, (i + 1) % count) for i in range(ends)])  31.6 us
    ppermute x5, waiting for transfers between devices, with_halo(): lax.ppermute(head, axis, [((i + 1) % count, i) for i in range(ends)])  30.1 us
    gather x32, local copies, waits for them, and re-layouts, one_projection(): column_tiles[:, blocks + 1]  17.4 us
    another operation x1, loops' own time, per_device(): lax.scan(one_projection, initial, (columns, angle_index, foot_block))  14.1 us
    gather x16, local copies, waits for them, and re-layouts, one_projection(): column_tiles[:, blocks]  13.1 us
    ppermute x5, starting transfers between devices, with_halo(): lax.ppermute(head, axis, [((i + 1) % count, i) for i in range(ends)])  11.4 us
  transfers between devices with their start and end apart: 11, of which 8 were waited for; matrix products, arithmetic and copies ran while one was open for 1% of the time, Pallas kernels for 0%

profile of v1, /device:TPU:191, one launch (start us, length us, event | category | flops | bytes accessed | tf_op | source)
XLA Modules:
  0.0 272.3 jit_solution(10231032295771682402)
XLA Ops:
  7.5 7.5 %collective-permute-start = (bf16[16,4,256]{2,1,0:T(4,128)(2,1)S(1)}, bf16[16,4,256]{2,1,0:T(4,128)(2,1)S(1)}, u32[]{:S(2)}, u32[]{:S(2)}) collective-permute-start(bf16[16,4,256]{2,1,0:T(4,128)(2,1)S(1)} %get-tuple-element.140), channel_id=1, source_target_pairs={{0,16},{16,32},{32,48},{48,64},{64,80},{80,96},{96,112},{112,128},... | collective-permute-start | bytes 98312 | tf_op jit(solution)/shard_map/ppermute | solution.py:29
  15.0 1.9 collective-permute-start.1
  19.1 5.4 %collective-permute-done.1 = bf16[16,4,256]{2,1,0:T(4,128)(2,1)S(1)} collective-permute-done((bf16[16,4,256]{2,1,0:T(4,128)(2,1)S(1)}, bf16[16,4,256]{2,1,0:T(4,128)(2,1)S(1)}, u32[]{:S(2)}, u32[]{:S(2)}) %collective-permute-start.1) | collective-permute-done | bytes 32800 | tf_op jit(solution)/shard_map/ppermute | solution.py:31
  24.4 1.7 convolution_convert_fusion
  26.2 55.3 %all-gather.2.cloned.1.call-done = bf16[16,8,4096]{2,1,0:T(8,128)(2,1)} async-done(((bf16[16,8,256]{2,1,0:T(8,128)(2,1)}), bf16[16,8,4096]{2,1,0:T(8,128)(2,1)}) %all-gather.2.cloned.1.call-update) | async-done | bytes 1048592 | tf_op jit(solution)/shard_map/all_gather | solution.py:124
  81.4 113.9 %while.13 = (s32[]{:T(128)}, f32[4,8,4096]{2,1,0:T(8,128)S(1)}, bf16[16,8,4096]{2,1,0:T(8,128)(2,1)}, s32[16,4,64]{2,1,0:T(4,128)}, s32[16]{0:T(128)}, /*index=5...) while((s32[]{:T(128)}, f32[4,8,4096]{2,1,0:T(8,128)S(1)}, ...), condition=%wide.region_1.2_spmd.clone, body=%wide.region_0.1_spmd.clone.sunk | while | flops 35099164 | bytes 6183707 | solution.py:142
  102.8 1.2 dynamic_slice.32
  138.4 1.2 dynamic_slice.32
  152.6 1.2 dynamic_slice.32
  159.8 1.2 dynamic_slice.32
  195.5 15.9 %collective-permute-start.2 = (f32[4,1,4096]{2,1,0:T(1,128)S(1)}, f32[4,1,4096]{2,1,0:T(1,128)S(1)}, u32[]{:S(2)}, u32[]{:S(2)}) collective-permute-start(f32[4,1,4096]{2,1,0:T(1,128)S(1)} %get-tuple-element.138), channel_id=1, source_target_pairs={{0,16},{16,32},{32,48},{48,64},{64,80},{80,96},{96,112},{112,128},... | collective-permute-start | bytes 196616 | tf_op jit(solution)/shard_map/ppermute | solution.py:29
  211.4 1.9 collective-permute-start.3
  213.3 7.9 %collective-permute-done.3 = f32[4,1,4096]{2,1,0:T(1,128)S(1)} collective-permute-done((f32[4,1,4096]{2,1,0:T(1,128)S(1)}, f32[4,1,4096]{2,1,0:T(1,128)S(1)}, u32[]{:S(2)}, u32[]{:S(2)}) %collective-permute-start.3) | collective-permute-done | bytes 65568 | tf_op jit(solution)/shard_map/ppermute | solution.py:31
  221.3 3.0 %collective-permute-start.4 = (f32[1,10,4096]{2,1,0:T(8,128)S(1)}, f32[1,10,4096]{2,1,0:T(8,128)S(1)}, u32[]{:S(2)}, u32[]{:S(2)}) collective-permute-start(f32[1,10,4096]{2,1,0:T(8,128)S(1)} %get-tuple-element.136), channel_id=1, source_target_pairs={{0,1},{1,2},{2,3},{3,4},{4,5},{5,6},{6,7},{7,8},{8,9},{9,10},{10,1... | collective-permute-start | bytes 491528 | tf_op jit(solution)/shard_map/ppermute | solution.py:29
  224.3 2.3 collective-permute-start.5
  226.6 1.8 collective-permute-done.4
  228.4 5.1 %collective-permute-done.5 = f32[1,10,4096]{2,1,0:T(8,128)S(1)} collective-permute-done((f32[1,10,4096]{2,1,0:T(8,128)S(1)}, f32[1,10,4096]{2,1,0:T(8,128)S(1)}, u32[]{:S(2)}, u32[]{:S(2)}) %collective-permute-start.5) | collective-permute-done | bytes 163872 | tf_op jit(solution)/shard_map/ppermute | solution.py:31
  237.1 3.3 %collective-permute-start.6 = (f32[4,1,4096]{2,1,0:T(1,128)S(1)}, f32[4,1,4096]{2,1,0:T(1,128)S(1)}, u32[]{:S(2)}, u32[]{:S(2)}) collective-permute-start(f32[4,1,4096]{2,1,0:T(1,128)S(1)} %get-tuple-element.132), channel_id=1, source_target_pairs={{0,16},{16,32},{32,48},{48,64},{64,80},{80,96},{96,112},{112,128},... | collective-permute-start | bytes 196616 | tf_op jit(solution)/shard_map/ppermute | solution.py:29
  240.4 1.9 collective-permute-start.7
  242.4 7.8 %collective-permute-done.7 = f32[4,1,4096]{2,1,0:T(1,128)S(1)} collective-permute-done((f32[4,1,4096]{2,1,0:T(1,128)S(1)}, f32[4,1,4096]{2,1,0:T(1,128)S(1)}, u32[]{:S(2)}, u32[]{:S(2)}) %collective-permute-start.7) | collective-permute-done | bytes 65568 | tf_op jit(solution)/shard_map/ppermute | solution.py:31
  250.3 1.9 collective-permute-start.8
  252.2 3.4 %collective-permute-start.9 = (f32[1,10,4096]{2,1,0:T(8,128)S(1)}, f32[1,10,4096]{2,1,0:T(8,128)S(1)}, u32[]{:S(2)}, u32[]{:S(2)}) collective-permute-start(f32[1,10,4096]{2,1,0:T(8,128)S(1)} %get-tuple-element.135), channel_id=1, source_target_pairs={{1,0},{2,1},{3,2},{4,3},{5,4},{6,5},{7,6},{8,7},{9,8},{10,9},{11,1... | collective-permute-start | bytes 491528 | tf_op jit(solution)/shard_map/ppermute | solution.py:31
  255.6 1.8 collective-permute-done.8
  257.4 4.0 %collective-permute-done.9 = f32[1,10,4096]{2,1,0:T(8,128)S(1)} collective-permute-done((f32[1,10,4096]{2,1,0:T(8,128)S(1)}, f32[1,10,4096]{2,1,0:T(8,128)S(1)}, u32[]{:S(2)}, u32[]{:S(2)}) %collective-permute-start.9) | collective-permute-done | bytes 163872 | tf_op jit(solution)/shard_map/ppermute | solution.py:31
  (336 shorter events, 105.8 us)
Async XLA Ops:
  6.5 74.9 %all-gather.2.cloned.1.call-start = ((), (), s32[]{:S(2)}) async-start(), calls=%async_computation | async-start | bytes 1114112 | tf_op jit(solution)/shard_map/all_gather | solution.py:124
  7.5 11.6 %collective-permute-start = (bf16[16,4,256]{2,1,0:T(4,128)(2,1)S(1)}, bf16[16,4,256]{2,1,0:T(4,128)(2,1)S(1)}, u32[]{:S(2)}, u32[]{:S(2)}) collective-permute-start(bf16[16,4,256]{2,1,0:T(4,128)(2,1)S(1)} %get-tuple-element.140), channel_id=1, source_target_pairs={{0,16},{16,32},{32,48},{48,64},{64,80},{80,96},{96,112},{112,128},... | collective-permute-start | bytes 98312 | tf_op jit(solution)/shard_map/ppermute | solution.py:29
  15.0 9.5 %collective-permute-start.1 = (bf16[16,4,256]{2,1,0:T(4,128)(2,1)S(1)}, bf16[16,4,256]{2,1,0:T(4,128)(2,1)S(1)}, u32[]{:S(2)}, u32[]{:S(2)}) collective-permute-start(bf16[16,4,256]{2,1,0:T(4,128)(2,1)S(1)} %get-tuple-element.141), channel_id=1, source_target_pairs={{16,0},{32,16},{48,32},{64,48},{80,64},{96,80},{112,96},{128,112},... | collective-permute-start | bytes 98312 | tf_op jit(solution)/shard_map/ppermute | solution.py:31
  195.5 17.8 %collective-permute-start.2 = (f32[4,1,4096]{2,1,0:T(1,128)S(1)}, f32[4,1,4096]{2,1,0:T(1,128)S(1)}, u32[]{:S(2)}, u32[]{:S(2)}) collective-permute-start(f32[4,1,4096]{2,1,0:T(1,128)S(1)} %get-tuple-element.138), channel_id=1, source_target_pairs={{0,16},{16,32},{32,48},{48,64},{64,80},{80,96},{96,112},{112,128},... | collective-permute-start | bytes 196616 | tf_op jit(solution)/shard_map/ppermute | solution.py:29
  211.4 9.8 %collective-permute-start.3 = (f32[4,1,4096]{2,1,0:T(1,128)S(1)}, f32[4,1,4096]{2,1,0:T(1,128)S(1)}, u32[]{:S(2)}, u32[]{:S(2)}) collective-permute-start(f32[4,1,4096]{2,1,0:T(1,128)S(1)} %get-tuple-element.139), channel_id=1, source_target_pairs={{16,0},{32,16},{48,32},{64,48},{80,64},{96,80},{112,96},{128,112},... | collective-permute-start | bytes 196616 | tf_op jit(solution)/shard_map/ppermute | solution.py:31
  221.3 7.1 %collective-permute-start.4 = (f32[1,10,4096]{2,1,0:T(8,128)S(1)}, f32[1,10,4096]{2,1,0:T(8,128)S(1)}, u32[]{:S(2)}, u32[]{:S(2)}) collective-permute-start(f32[1,10,4096]{2,1,0:T(8,128)S(1)} %get-tuple-element.136), channel_id=1, source_target_pairs={{0,1},{1,2},{2,3},{3,4},{4,5},{5,6},{6,7},{7,8},{8,9},{9,10},{10,1... | collective-permute-start | bytes 491528 | tf_op jit(solution)/shard_map/ppermute | solution.py:29
  224.3 9.2 %collective-permute-start.5 = (f32[1,10,4096]{2,1,0:T(8,128)S(1)}, f32[1,10,4096]{2,1,0:T(8,128)S(1)}, u32[]{:S(2)}, u32[]{:S(2)}) collective-permute-start(f32[1,10,4096]{2,1,0:T(8,128)S(1)} %get-tuple-element.137), channel_id=1, source_target_pairs={{1,0},{2,1},{3,2},{4,3},{5,4},{6,5},{7,6},{8,7},{9,8},{10,9},{11,1... | collective-permute-start | bytes 491528 | tf_op jit(solution)/shard_map/ppermute | solution.py:31
  237.1 5.3 %collective-permute-start.6 = (f32[4,1,4096]{2,1,0:T(1,128)S(1)}, f32[4,1,4096]{2,1,0:T(1,128)S(1)}, u32[]{:S(2)}, u32[]{:S(2)}) collective-permute-start(f32[4,1,4096]{2,1,0:T(1,128)S(1)} %get-tuple-element.132), channel_id=1, source_target_pairs={{0,16},{16,32},{32,48},{48,64},{64,80},{80,96},{96,112},{112,128},... | collective-permute-start | bytes 196616 | tf_op jit(solution)/shard_map/ppermute | solution.py:29
  240.4 9.8 %collective-permute-start.7 = (f32[4,1,4096]{2,1,0:T(1,128)S(1)}, f32[4,1,4096]{2,1,0:T(1,128)S(1)}, u32[]{:S(2)}, u32[]{:S(2)}) collective-permute-start(f32[4,1,4096]{2,1,0:T(1,128)S(1)} %get-tuple-element.133), channel_id=1, source_target_pairs={{16,0},{32,16},{48,32},{64,48},{80,64},{96,80},{112,96},{128,112},... | collective-permute-start | bytes 196616 | tf_op jit(solution)/shard_map/ppermute | solution.py:31
  250.3 7.1 %collective-permute-start.8 = (f32[1,10,4096]{2,1,0:T(8,128)S(1)}, f32[1,10,4096]{2,1,0:T(8,128)S(1)}, u32[]{:S(2)}, u32[]{:S(2)}) collective-permute-start(f32[1,10,4096]{2,1,0:T(8,128)S(1)} %get-tuple-element.134), channel_id=1, source_target_pairs={{0,1},{1,2},{2,3},{3,4},{4,5},{5,6},{6,7},{7,8},{8,9},{9,10},{10,1... | collective-permute-start | bytes 491528 | tf_op jit(solution)/shard_map/ppermute | solution.py:29
  252.2 9.2 %collective-permute-start.9 = (f32[1,10,4096]{2,1,0:T(8,128)S(1)}, f32[1,10,4096]{2,1,0:T(8,128)S(1)}, u32[]{:S(2)}, u32[]{:S(2)}) collective-permute-start(f32[1,10,4096]{2,1,0:T(8,128)S(1)} %get-tuple-element.135), channel_id=1, source_target_pairs={{1,0},{2,1},{3,2},{4,3},{5,4},{6,5},{7,6},{8,7},{9,8},{10,9},{11,1... | collective-permute-start | bytes 491528 | tf_op jit(solution)/shard_map/ppermute | solution.py:31
Sparse Core Ops, SparseCore 0:
  26.3 55.1 all-gather.1

commit v2 on v1

--- a/solution.py
+++ b/solution.py
@@ -1,8 +1,11 @@
+import functools
 import math
 
 import jax
 import jax.numpy as jnp
 from jax import lax
+from jax.experimental import pallas as pl
+from jax.experimental.pallas import tpu as pltpu
 from jax.sharding import PartitionSpec as P
 
 X = 4096
@@ -35,6 +38,67 @@
     return cells
 
 
+def gather_kernel(count, local_ref, out_ref, send_sem, recv_sem, own_sem):
+    me = lax.axis_index("gy")
+    depth_index = lax.axis_index("gz")
+    width = local_ref.shape[2]
+    barrier = pltpu.get_barrier_semaphore()
+    for step in range(1, count):
+        peer = lax.rem(me + step, count)
+        pl.semaphore_signal(
+            barrier, inc=1, device_id=(depth_index, peer), device_id_type=pl.DeviceIdType.MESH
+        )
+    pl.semaphore_wait(barrier, count - 1)
+    own_slot = pl.ds(pl.multiple_of(me * width, width), width)
+    own = pltpu.make_async_copy(local_ref, out_ref.at[:, :, own_slot], own_sem)
+    own.start()
+    sends = []
+    for step in range(1, count):
+        peer = lax.rem(me + step, count)
+        copy = pltpu.make_async_remote_copy(
+            src_ref=local_ref,
+            dst_ref=out_ref.at[:, :, own_slot],
+            send_sem=send_sem.at[step],
+            recv_sem=recv_sem.at[step],
+            device_id=(depth_index, peer),
+            device_id_type=pl.DeviceIdType.MESH,
+        )
+        copy.start()
+        sends.append(copy)
+    own.wait()
+    for copy in sends:
+        copy.wait_send()
+    for step in range(1, count):
+        sender = lax.rem(me + count - step, count)
+        slot = pl.ds(pl.multiple_of(sender * width, width), width)
+        arriving = pltpu.make_async_remote_copy(
+            src_ref=local_ref,
+            dst_ref=out_ref.at[:, :, slot],
+            send_sem=send_sem.at[step],
+            recv_sem=recv_sem.at[step],
+            device_id=(depth_index, sender),
+            device_id_type=pl.DeviceIdType.MESH,
+        )
+        arriving.wait_recv()
+
+
+def gather_columns(local):
+    count = lax.axis_size("gy")
+    rows, depth, width = local.shape
+    return pl.pallas_call(
+        functools.partial(gather_kernel, count),
+        out_shape=jax.ShapeDtypeStruct((rows, depth, width * count), local.dtype),
+        in_specs=[pl.BlockSpec(memory_space=pl.ANY)],
+        out_specs=pl.BlockSpec(memory_space=pl.ANY),
+        scratch_shapes=[
+            pltpu.SemaphoreType.DMA((count,)),
+            pltpu.SemaphoreType.DMA((count,)),
+            pltpu.SemaphoreType.DMA(()),
+        ],
+        compiler_params=pltpu.CompilerParams(collective_id=0, has_side_effects=True),
+    )(local)
+
+
 def geometry(angle_value):
     radians = 2.0 * math.pi * angle_value.astype(jnp.float32) / NANG
     stretch = 0.5 + 0.5 * jnp.abs(jnp.cos(radians))
@@ -121,7 +185,7 @@
         extended_band,
         preferred_element_type=jnp.float32,
     )
-    columns = lax.all_gather(summed_rows.astype(jnp.bfloat16), "gy", axis=2, tiled=True)
+    columns = gather_columns(summed_rows.astype(jnp.bfloat16))
     column_count = columns.shape[2]
     row_base = lax.axis_index("gy") * row_count
     depth_base = lax.axis_index("gz") * depth_count

time: 274 us -> 196 us (0.72)
  the two profiles are of different devices: /device:TPU:191 before, /device:TPU:151 now
where the time goes in v2:
time: 196 us; the launch traced here: 195 us
  local copies, waits for them, and re-layouts  54.1 us (28%)
  starting transfers between devices  34 us (17%)
  waiting for transfers between devices  32.1 us (16%)
  other arithmetic  25.4 us (13%)
  Pallas kernels  25.4 us (13%)
  loops' own time  14.3 us (7%)
  matrix products  9.15 us (5%)
    ppermute x5, waiting for transfers between devices, with_halo(): lax.ppermute(head, axis, [((i + 1) % count, i) for i in range(ends)])  29 us
    pallas_call x1, Pallas kernels, gather_columns(): pl.pallas_call(functools.partial(gather_kernel, count), out_shape=jax.Sha...  25.4 us
    ppermute x5, starting transfers between devices, with_halo(): lax.ppermute(tail, axis, [(i, (i + 1) % count) for i in range(ends)])  22.9 us
    gather x32, local copies, waits for them, and re-layouts, one_projection(): column_tiles[:, blocks + 1]  17.4 us
    another operation x1, loops' own time, per_device(): lax.scan(one_projection, initial, (columns, angle_index, foot_block))  14.3 us
    gather x16, local copies, waits for them, and re-layouts, one_projection(): column_tiles[:, blocks]  13.1 us
    ppermute x5, starting transfers between devices, with_halo(): lax.ppermute(head, axis, [((i + 1) % count, i) for i in range(ends)])  11 us
    select_n x16, other arithmetic, one_projection(): column_tiles[:, blocks]  11 us
  transfers between devices with their start and end apart: 10, of which 7 were waited for; matrix products, arithmetic and copies ran while one was open for 1% of the time, Pallas kernels for 0%

profile of v2, /device:TPU:151, one launch (start us, length us, event | category | flops | bytes accessed | tf_op | source)
XLA Modules:
  0.0 194.7 jit_solution(6746326531100843357)
XLA Ops:
  0.9 7.5 %collective-permute-start = (bf16[16,4,256]{2,1,0:T(4,128)(2,1)S(1)}, bf16[16,4,256]{2,1,0:T(4,128)(2,1)S(1)}, u32[]{:S(2)}, u32[]{:S(2)}) collective-permute-start(bf16[16,4,256]{2,1,0:T(4,128)(2,1)S(1)} %get-tuple-element.140), channel_id=1, source_target_pairs={{0,16},{16,32},{32,48},{48,64},{64,80},{80,96},{96,112},{112,128},... | collective-permute-start | bytes 98312 | tf_op jit(solution)/shard_map/ppermute | solution.py:32
  8.5 1.9 collective-permute-start.1
  12.6 5.3 %collective-permute-done.1 = bf16[16,4,256]{2,1,0:T(4,128)(2,1)S(1)} collective-permute-done((bf16[16,4,256]{2,1,0:T(4,128)(2,1)S(1)}, bf16[16,4,256]{2,1,0:T(4,128)(2,1)S(1)}, u32[]{:S(2)}, u32[]{:S(2)}) %collective-permute-start.1) | collective-permute-done | bytes 32800 | tf_op jit(solution)/shard_map/ppermute | solution.py:34
  17.9 1.7 convolution_convert_fusion.local_ref
  19.6 25.4 %shard_map.55 = bf16[16,8,4096]{2,1,0:T(8,128)(2,1)S(1)} custom-call(bf16[16,8,256]{2,1,0:T(8,128)(2,1)} %convolution_convert_fusion.local_ref), custom_call_target="tpu_custom_call" | custom-call | tf_op jit(solution)/shard_map/pallas_call | solution.py:88
  45.0 90.2 %while.13 = (s32[]{:T(128)}, f32[4,8,4096]{2,1,0:T(8,128)S(1)}, bf16[16,8,4096]{2,1,0:T(8,128)(2,1)S(1)}, s32[16,4,64]{2,1,0:T(4,128)}, s32[16]{0:T(128)S(1)}, /...) while((s32[]{:T(128)}, f32[4,8,4096]{2,1,0:T(8,128)S(1)}, ...), condition=%wide.region_1.2_spmd.clone, body=%wide.region_0.1_spmd.clone.sunk | while | flops 35099164 | bytes 6183707 | solution.py:206
  135.4 5.7 %collective-permute-start.2 = (f32[4,1,4096]{2,1,0:T(1,128)S(1)}, f32[4,1,4096]{2,1,0:T(1,128)S(1)}, u32[]{:S(2)}, u32[]{:S(2)}) collective-permute-start(f32[4,1,4096]{2,1,0:T(1,128)S(1)} %get-tuple-element.138), channel_id=1, source_target_pairs={{0,16},{16,32},{32,48},{48,64},{64,80},{80,96},{96,112},{112,128},... | collective-permute-start | bytes 196616 | tf_op jit(solution)/shard_map/ppermute | solution.py:32
  141.0 1.9 collective-permute-start.3
  143.0 8.6 %collective-permute-done.3 = f32[4,1,4096]{2,1,0:T(1,128)S(1)} collective-permute-done((f32[4,1,4096]{2,1,0:T(1,128)S(1)}, f32[4,1,4096]{2,1,0:T(1,128)S(1)}, u32[]{:S(2)}, u32[]{:S(2)}) %collective-permute-start.3) | collective-permute-done | bytes 65568 | tf_op jit(solution)/shard_map/ppermute | solution.py:34
  151.6 1.9 collective-permute-start.4
  153.6 3.4 %collective-permute-start.5 = (f32[1,10,4096]{2,1,0:T(8,128)S(1)}, f32[1,10,4096]{2,1,0:T(8,128)S(1)}, u32[]{:S(2)}, u32[]{:S(2)}) collective-permute-start(f32[1,10,4096]{2,1,0:T(8,128)S(1)} %get-tuple-element.137), channel_id=1, source_target_pairs={{1,0},{2,1},{3,2},{4,3},{5,4},{6,5},{7,6},{8,7},{9,8},{10,9},{11,1... | collective-permute-start | bytes 491528 | tf_op jit(solution)/shard_map/ppermute | solution.py:34
  157.0 1.8 collective-permute-done.4
  158.7 3.4 %collective-permute-done.5 = f32[1,10,4096]{2,1,0:T(8,128)S(1)} collective-permute-done((f32[1,10,4096]{2,1,0:T(8,128)S(1)}, f32[1,10,4096]{2,1,0:T(8,128)S(1)}, u32[]{:S(2)}, u32[]{:S(2)}) %collective-permute-start.5) | collective-permute-done | bytes 163872 | tf_op jit(solution)/shard_map/ppermute | solution.py:34
  163.3 1.1 fusion.19
  164.5 1.2 multiply_add_fusion.1
  165.8 3.0 %collective-permute-start.6 = (f32[4,1,4096]{2,1,0:T(1,128)S(1)}, f32[4,1,4096]{2,1,0:T(1,128)S(1)}, u32[]{:S(2)}, u32[]{:S(2)}) collective-permute-start(f32[4,1,4096]{2,1,0:T(1,128)S(1)} %get-tuple-element.132), channel_id=1, source_target_pairs={{0,16},{16,32},{32,48},{48,64},{64,80},{80,96},{96,112},{112,128},... | collective-permute-start | bytes 196616 | tf_op jit(solution)/shard_map/ppermute | solution.py:32
  168.8 1.9 collective-permute-start.7
  170.8 7.8 %collective-permute-done.7 = f32[4,1,4096]{2,1,0:T(1,128)S(1)} collective-permute-done((f32[4,1,4096]{2,1,0:T(1,128)S(1)}, f32[4,1,4096]{2,1,0:T(1,128)S(1)}, u32[]{:S(2)}, u32[]{:S(2)}) %collective-permute-start.7) | collective-permute-done | bytes 65568 | tf_op jit(solution)/shard_map/ppermute | solution.py:34
  178.7 4.9 %collective-permute-start.8 = (f32[1,10,4096]{2,1,0:T(8,128)S(1)}, f32[1,10,4096]{2,1,0:T(8,128)S(1)}, u32[]{:S(2)}, u32[]{:S(2)}) collective-permute-start(f32[1,10,4096]{2,1,0:T(8,128)S(1)} %get-tuple-element.134), channel_id=1, source_target_pairs={{0,1},{1,2},{2,3},{3,4},{4,5},{5,6},{6,7},{7,8},{8,9},{9,10},{10,1... | collective-permute-start | bytes 491528 | tf_op jit(solution)/shard_map/ppermute | solution.py:32
  183.6 1.9 collective-permute-start.9
  185.5 1.4 collective-permute-done.8
  186.9 3.8 %collective-permute-done.9 = f32[1,10,4096]{2,1,0:T(8,128)S(1)} collective-permute-done((f32[1,10,4096]{2,1,0:T(8,128)S(1)}, f32[1,10,4096]{2,1,0:T(8,128)S(1)}, u32[]{:S(2)}, u32[]{:S(2)}) %collective-permute-start.9) | collective-permute-done | bytes 163872 | tf_op jit(solution)/shard_map/ppermute | solution.py:34
  191.9 1.1 fusion.20
  193.5 1.2 fusion.25
  (336 shorter events, 82.3 us)
Async XLA Ops:
  0.0 45.0 %copy-start = (s32[16]{0:T(128)S(1)}, s32[16]{0:T(128)}, u32[]{:S(2)}) copy-start(s32[16]{0:T(128)} %param.8) | copy-start | bytes 196
  0.9 11.6 %collective-permute-start = (bf16[16,4,256]{2,1,0:T(4,128)(2,1)S(1)}, bf16[16,4,256]{2,1,0:T(4,128)(2,1)S(1)}, u32[]{:S(2)}, u32[]{:S(2)}) collective-permute-start(bf16[16,4,256]{2,1,0:T(4,128)(2,1)S(1)} %get-tuple-element.140), channel_id=1, source_target_pairs={{0,16},{16,32},{32,48},{48,64},{64,80},{80,96},{96,112},{112,128},... | collective-permute-start | bytes 98312 | tf_op jit(solution)/shard_map/ppermute | solution.py:32
  8.5 9.5 %collective-permute-start.1 = (bf16[16,4,256]{2,1,0:T(4,128)(2,1)S(1)}, bf16[16,4,256]{2,1,0:T(4,128)(2,1)S(1)}, u32[]{:S(2)}, u32[]{:S(2)}) collective-permute-start(bf16[16,4,256]{2,1,0:T(4,128)(2,1)S(1)} %get-tuple-element.141), channel_id=1, source_target_pairs={{16,0},{32,16},{48,32},{64,48},{80,64},{96,80},{112,96},{128,112},... | collective-permute-start | bytes 98312 | tf_op jit(solution)/shard_map/ppermute | solution.py:34
  135.4 7.6 %collective-permute-start.2 = (f32[4,1,4096]{2,1,0:T(1,128)S(1)}, f32[4,1,4096]{2,1,0:T(1,128)S(1)}, u32[]{:S(2)}, u32[]{:S(2)}) collective-permute-start(f32[4,1,4096]{2,1,0:T(1,128)S(1)} %get-tuple-element.138), channel_id=1, source_target_pairs={{0,16},{16,32},{32,48},{48,64},{64,80},{80,96},{96,112},{112,128},... | collective-permute-start | bytes 196616 | tf_op jit(solution)/shard_map/ppermute | solution.py:32
  141.0 10.5 %collective-permute-start.3 = (f32[4,1,4096]{2,1,0:T(1,128)S(1)}, f32[4,1,4096]{2,1,0:T(1,128)S(1)}, u32[]{:S(2)}, u32[]{:S(2)}) collective-permute-start(f32[4,1,4096]{2,1,0:T(1,128)S(1)} %get-tuple-element.139), channel_id=1, source_target_pairs={{16,0},{32,16},{48,32},{64,48},{80,64},{96,80},{112,96},{128,112},... | collective-permute-start | bytes 196616 | tf_op jit(solution)/shard_map/ppermute | solution.py:34
  151.6 7.1 %collective-permute-start.4 = (f32[1,10,4096]{2,1,0:T(8,128)S(1)}, f32[1,10,4096]{2,1,0:T(8,128)S(1)}, u32[]{:S(2)}, u32[]{:S(2)}) collective-permute-start(f32[1,10,4096]{2,1,0:T(8,128)S(1)} %get-tuple-element.136), channel_id=1, source_target_pairs={{0,1},{1,2},{2,3},{3,4},{4,5},{5,6},{6,7},{7,8},{8,9},{9,10},{10,1... | collective-permute-start | bytes 491528 | tf_op jit(solution)/shard_map/ppermute | solution.py:32
  153.6 8.6 %collective-permute-start.5 = (f32[1,10,4096]{2,1,0:T(8,128)S(1)}, f32[1,10,4096]{2,1,0:T(8,128)S(1)}, u32[]{:S(2)}, u32[]{:S(2)}) collective-permute-start(f32[1,10,4096]{2,1,0:T(8,128)S(1)} %get-tuple-element.137), channel_id=1, source_target_pairs={{1,0},{2,1},{3,2},{4,3},{5,4},{6,5},{7,6},{8,7},{9,8},{10,9},{11,1... | collective-permute-start | bytes 491528 | tf_op jit(solution)/shard_map/ppermute | solution.py:34
  165.8 5.0 %collective-permute-start.6 = (f32[4,1,4096]{2,1,0:T(1,128)S(1)}, f32[4,1,4096]{2,1,0:T(1,128)S(1)}, u32[]{:S(2)}, u32[]{:S(2)}) collective-permute-start(f32[4,1,4096]{2,1,0:T(1,128)S(1)} %get-tuple-element.132), channel_id=1, source_target_pairs={{0,16},{16,32},{32,48},{48,64},{64,80},{80,96},{96,112},{112,128},... | collective-permute-start | bytes 196616 | tf_op jit(solution)/shard_map/ppermute | solution.py:32
  168.8 9.8 %collective-permute-start.7 = (f32[4,1,4096]{2,1,0:T(1,128)S(1)}, f32[4,1,4096]{2,1,0:T(1,128)S(1)}, u32[]{:S(2)}, u32[]{:S(2)}) collective-permute-start(f32[4,1,4096]{2,1,0:T(1,128)S(1)} %get-tuple-element.133), channel_id=1, source_target_pairs={{16,0},{32,16},{48,32},{64,48},{80,64},{96,80},{112,96},{128,112},... | collective-permute-start | bytes 196616 | tf_op jit(solution)/shard_map/ppermute | solution.py:34
  178.7 8.2 %collective-permute-start.8 = (f32[1,10,4096]{2,1,0:T(8,128)S(1)}, f32[1,10,4096]{2,1,0:T(8,128)S(1)}, u32[]{:S(2)}, u32[]{:S(2)}) collective-permute-start(f32[1,10,4096]{2,1,0:T(8,128)S(1)} %get-tuple-element.134), channel_id=1, source_target_pairs={{0,1},{1,2},{2,3},{3,4},{4,5},{5,6},{6,7},{7,8},{8,9},{9,10},{10,1... | collective-permute-start | bytes 491528 | tf_op jit(solution)/shard_map/ppermute | solution.py:32
  183.6 7.1 %collective-permute-start.9 = (f32[1,10,4096]{2,1,0:T(8,128)S(1)}, f32[1,10,4096]{2,1,0:T(8,128)S(1)}, u32[]{:S(2)}, u32[]{:S(2)}) collective-permute-start(f32[1,10,4096]{2,1,0:T(8,128)S(1)} %get-tuple-element.135), channel_id=1, source_target_pairs={{1,0},{2,1},{3,2},{4,3},{5,4},{6,5},{7,6},{8,7},{9,8},{10,9},{11,1... | collective-permute-start | bytes 491528 | tf_op jit(solution)/shard_map/ppermute | solution.py:34

commit v3 on v2

--- a/solution.py
+++ b/solution.py
@@ -12,6 +12,7 @@
 P_SIZE = 16
 NANG = 3600
 BLOCK = 64
+LANES = 128
 ITERS = 2
 
 
@@ -174,6 +175,84 @@
     return current + step_length * (smooth_weight * divergence - (current - fidelity))
 
 
+def footprint_mats(angle_value, shift, row_global, rows_total):
+    radians, stretch, spread = geometry(angle_value)
+    shifted = shift_reach * jnp.sin(radians + 2.0 * math.pi * row_global / rows_total)
+    inside = jnp.arange(BLOCK).astype(jnp.float32) - 0.5 * (BLOCK - 1)
+    centre = BLOCK + inside[None, :] * stretch + shifted[:, None]
+    centre = jnp.concatenate([centre, centre], axis=1)
+    parity = shift - 2 * ((shift + 2) // 2 - 1)
+    half = (jnp.arange(LANES) >= BLOCK).astype(jnp.int32)
+    place = jnp.arange(LANES)[:, None]
+    taps = jnp.stack(
+        [
+            place - BLOCK * (half[None, None, :] + parity[:, None, None]),
+            place + LANES - BLOCK * (half[None, None, :] + parity[:, None, None]),
+            jnp.broadcast_to(place, (LANES, LANES))[None].repeat(shift.shape[0], 0),
+        ],
+        axis=1,
+    )
+    places = taps.astype(jnp.float32) + 0.5
+    weights = (
+        jnp.maximum(0.0, 1.0 - jnp.abs(places - centre[:, None, None, :]) / spread) / spread
+    )
+    valid = (taps >= 0) & (taps < 2 * BLOCK)
+    return jnp.where(valid, weights, 0.0).astype(jnp.bfloat16)
+
+
+def backproject_kernel(shift_ref, tiles_ref, mats_ref, out_ref):
+    p = pl.program_id(0)
+    tile_count = out_ref.shape[2] // LANES
+    depth_count = out_ref.shape[1]
+
+    @pl.when(p == 0)
+    def _():
+        out_ref[...] = jnp.zeros_like(out_ref)
+
+    ends = jnp.concatenate([tiles_ref[0, 1], tiles_ref[0, tile_count]], axis=0).astype(jnp.bfloat16)
+    for row in range(out_ref.shape[0]):
+        shift = shift_ref[p, row]
+        start = (shift + 2) // 2
+        low = tiles_ref[0, pl.ds(start, tile_count)].reshape(tile_count * depth_count, LANES)
+        high = tiles_ref[0, pl.ds(start + 1, tile_count)].reshape(tile_count * depth_count, LANES)
+        result = jnp.dot(
+            low.astype(jnp.bfloat16), mats_ref[0, row, 0], preferred_element_type=jnp.float32
+        ) + jnp.dot(
+            high.astype(jnp.bfloat16), mats_ref[0, row, 1], preferred_element_type=jnp.float32
+        )
+        edge = jnp.dot(ends, mats_ref[0, row, 2], preferred_element_type=jnp.float32)
+        shift_vec = jnp.full((depth_count, LANES), shift, jnp.int32)
+        for tile in range(tile_count):
+            part = result[tile * depth_count:(tile + 1) * depth_count]
+            if tile == 0:
+                part = jnp.where(shift_vec < 0, edge[:depth_count], part)
+            elif tile == tile_count - 2:
+                part = jnp.where(shift_vec >= 2, edge[depth_count:], part)
+            elif tile == tile_count - 1:
+                part = jnp.where(shift_vec >= 0, edge[depth_count:], part)
+            lanes = pl.ds(tile * LANES, LANES)
+            out_ref[row, :, lanes] = out_ref[row, :, lanes] + part
+
+
+def backproject(shifts, tiles, mats, column_count):
+    count, rows = shifts.shape
+    depth_count = tiles.shape[2]
+    return pl.pallas_call(
+        backproject_kernel,
+        out_shape=jax.ShapeDtypeStruct((rows, depth_count, column_count), jnp.float32),
+        grid_spec=pltpu.PrefetchScalarGridSpec(
+            num_scalar_prefetch=1,
+            grid=(count,),
+            in_specs=[
+                pl.BlockSpec((1,) + tiles.shape[1:], lambda p, s: (p, 0, 0, 0)),
+                pl.BlockSpec((1,) + mats.shape[1:], lambda p, s: (p, 0, 0, 0, 0)),
+            ],
+            out_specs=pl.BlockSpec((rows, depth_count, column_count), lambda p, s: (0, 0, 0)),
+        ),
+        compiler_params=pltpu.CompilerParams(dimension_semantics=("arbitrary",)),
+    )(shifts, tiles, mats)
+
+
 def per_device(filtered, angle_index, band_offset, band_length, foot_block):
     depth_count = filtered.shape[1]
     row_count = foot_block.shape[1]
@@ -192,18 +271,14 @@
     rows_total = lax.axis_size("gy") * row_count
     depth_total = lax.axis_size("gz") * depth_count
     row_global = (row_base + jnp.arange(row_count)).astype(jnp.float32)
-
-    def one_projection(running, inputs):
-        projected, angle_value, blocks = inputs
-        radians, stretch, spread = geometry(angle_value)
-        weights = footprint(radians, stretch, spread, row_global, rows_total, BLOCK)
-        column_tiles = projected.reshape(depth_count, column_count // BLOCK, BLOCK)
-        window = jnp.concatenate([column_tiles[:, blocks], column_tiles[:, blocks + 1]], axis=-1)
-        product = jnp.einsum("yiu,zybu->yzbi", weights, window, preferred_element_type=jnp.float32)
-        return (running + product.reshape(running.shape), None)
-
-    initial = jnp.zeros((row_count, depth_count, X), jnp.float32)
-    summed, _unused = lax.scan(one_projection, initial, (columns, angle_index, foot_block))
+    shifts = foot_block[:, :, 2] - 2
+    mats = jax.vmap(footprint_mats, in_axes=(0, 0, None, None))(
+        angle_index, shifts, row_global, rows_total
+    )
+    tile_count = column_count // LANES
+    tiles = columns.astype(jnp.float32).reshape(P_SIZE, depth_count, tile_count, LANES)
+    tiles = jnp.pad(tiles.transpose(0, 2, 1, 3), ((0, 0), (1, 2), (0, 0), (0, 0)))
+    summed = backproject(shifts, tiles, mats, column_count)
     backprojection = math.pi / P_SIZE * summed
     current = backprojection
     padded_fidelity = jnp.pad(backprojection, ((1, 1), (1, 1), (0, 0)))

time: 196 us -> 131 us (0.67)
  local copies, waits for them, and re-layouts: 54.1 us -> 2.89 us
  Pallas kernels: 25.4 us -> 42.8 us
  loops' own time: 14.3 us -> 0 us
  matrix products: 9.15 us -> 0.85 us
  waiting for transfers between devices: 32.1 us -> 27.2 us
  other arithmetic: 25.4 us -> 22.4 us
    gather x48 -> x0, local copies, waits for them, and re-layouts: 30.5 us -> none  [the longest x32 17.4 us: one_projection(): column_tiles[:, blocks + 1]]
    another operation x1 -> x0, loops' own time: 14.3 us -> none  [per_device(): lax.scan(one_projection, initial, (columns, angle_index, foot_block))]
    pallas_call x0 -> x1, Pallas kernels: none -> 13.2 us  [backproject(): pl.pallas_call(backproject_kernel, out_shape=jax.ShapeDtypeStruct((rows,...]
    select_n x16 -> x0, other arithmetic: 11 us -> none  [one_projection(): column_tiles[:, blocks]]
    reshape x48 -> x0, local copies, waits for them, and re-layouts: 10 us -> none  [the longest x16 5.75 us: one_projection(): return (running + product.reshape(running.shape), None)]
    dynamic_slice x32 -> x0, local copies, waits for them, and re-layouts: 9.64 us -> none  [per_device(): lax.scan(one_projection, initial, (columns, angle_index, foot_block))]
    dot_general x16 -> x0, matrix products: 7.47 us -> none  [one_projection(): jnp.einsum('yiu,zybu->yzbi', weights, window, preferred_element_type=jnp....]
    convert_element_type x0 -> x2, other arithmetic: none -> 6.67 us  [the longest x1 6.66 us: footprint_mats(): return jnp.where(valid, weights, 0.0).astype(jnp.bfloat16)]
  transfers between devices with their start and end apart: 10 -> 10, of which waited for: 7 -> 6; matrix products, arithmetic and copies ran while one was open for 1% -> 10% of each run, Pallas kernels for 0% -> 0%
where the time goes in v3:
time: 131 us; the launch traced here: 130 us
  Pallas kernels  42.8 us (33%)
  starting transfers between devices  33.8 us (26%)
  waiting for transfers between devices  27.2 us (21%)
  other arithmetic  22.4 us (17%)
  local copies, waits for them, and re-layouts  2.89 us (2%)
    pallas_call x1, Pallas kernels, gather_columns(): pl.pallas_call(functools.partial(gather_kernel, count), out_shape=jax.Sha...  29.5 us
    ppermute x5, waiting for transfers between devices, with_halo(): lax.ppermute(head, axis, [((i + 1) % count, i) for i in range(ends)])  24 us
    ppermute x5, starting transfers between devices, with_halo(): lax.ppermute(tail, axis, [(i, (i + 1) % count) for i in range(ends)])  22.7 us
    pallas_call x1, Pallas kernels, backproject(): pl.pallas_call(backproject_kernel, out_shape=jax.ShapeDtypeStruct((rows,...  13.2 us
    ppermute x5, starting transfers between devices, with_halo(): lax.ppermute(head, axis, [((i + 1) % count, i) for i in range(ends)])  11 us
    convert_element_type x1, other arithmetic, footprint_mats(): return jnp.where(valid, weights, 0.0).astype(jnp.bfloat16)  6.66 us
    ppermute x5, waiting for transfers between devices, with_halo(): lax.ppermute(tail, axis, [(i, (i + 1) % count) for i in range(ends)])  3.16 us
    pad x1, other arithmetic, per_device(): jnp.pad(tiles.transpose(0, 2, 1, 3), ((0, 0), (1, 2), (0, 0), (0, 0)))  2.83 us
  transfers between devices with their start and end apart: 10, of which 6 were waited for; matrix products, arithmetic and copies ran while one was open for 10% of the time, Pallas kernels for 0%

profile of v3, /device:TPU:151, one launch (start us, length us, event | category | flops | bytes accessed | tf_op | source)
XLA Modules:
  0.0 130.2 jit_solution(4691709989946269041)
XLA Ops:
  0.9 7.5 %collective-permute-start = (bf16[16,4,256]{2,1,0:T(4,128)(2,1)S(1)}, bf16[16,4,256]{2,1,0:T(4,128)(2,1)S(1)}, u32[]{:S(2)}, u32[]{:S(2)}) collective-permute-start(bf16[16,4,256]{2,1,0:T(4,128)(2,1)S(1)} %get-tuple-element.19), channel_id=1, source_target_pairs={{0,16},{16,32},{32,48},{48,64},{64,80},{80,96},{96,112},{112,128},... | collective-permute-start | bytes 98312 | tf_op jit(solution)/shard_map/ppermute | solution.py:33
  8.4 1.9 %collective-permute-start.1 = (bf16[16,4,256]{2,1,0:T(4,128)(2,1)S(1)}, bf16[16,4,256]{2,1,0:T(4,128)(2,1)S(1)}, u32[]{:S(2)}, u32[]{:S(2)}) collective-permute-start(bf16[16,4,256]{2,1,0:T(4,128)(2,1)S(1)} %get-tuple-element.20), channel_id=1, source_target_pairs={{16,0},{32,16},{48,32},{64,48},{80,64},{96,80},{112,96},{128,112},... | collective-permute-start | bytes 98312 | tf_op jit(solution)/shard_map/ppermute | solution.py:35
  16.4 6.7 %select_convert_fusion.mats_ref = bf16[16,4,3,128,128]{4,3,2,1,0:T(8,128)(2,1)} fusion(s32[16,4,1,128,128]{4,3,2,1,0:T(8,128)S(1)} %broadcast_in_dim.10, s32[16,4,1,128,128]{4,3,2,1,0:T(8,128)S(1)} %get-tuple-element.22, s32[16,4,1,128,128]{4,3,2,1,0:T(8,128)S(1)} %get-tuple-element.21, f32[16]{0:T(128)S(1)} %get-tuple-element.26, ...), kind=kLoop, calls=%fused_computation.1 | loop fusion | flops 47185920 | bytes 18907200 | tf_op jit(solution)/shard_map/vmap()/convert_element_type | solution.py:200
  23.9 29.5 %shard_map.55 = bf16[16,8,4096]{2,1,0:T(8,128)(2,1)} custom-call(bf16[16,8,256]{2,1,0:T(8,128)(2,1)} %convolution_convert_fusion.local_ref), custom_call_target="tpu_custom_call" | custom-call | tf_op jit(solution)/shard_map/pallas_call | solution.py:89
  53.4 2.8 %pad_convert_fusion.tiles_ref = f32[16,35,8,128]{3,2,1,0:T(8,128)} fusion(bf16[16,32,8,128]{3,2,1,0:T(8,128)(2,1)} %bitcast.20), kind=kLoop, calls=%fused_computation.26 | loop fusion | flops 573440 | bytes 3342336 | tf_op jit(solution)/shard_map/jit(_pad)/pad | solution.py:280
  56.3 13.2 %shard_map.56 = f32[4,8,4096]{2,1,0:T(8,128)} custom-call(s32[16,4]{1,0:T(8,128)} %get-tuple-element.24.shift_ref, f32[16,35,8,128]{3,2,1,0:T(8,128)} %pad_convert_fusion.tiles_ref, bf16[16,4,3,128,128]{4,3,2,1,0:T(8,128)(2,1)} %select_convert_fusion.mats_ref), custom_call_target="tpu_custom_call" | custom-call | tf_op jit(solution)/shard_map/pallas_call | solution.py:240
  70.7 5.5 %collective-permute-start.2 = (f32[4,1,4096]{2,1,0:T(1,128)S(1)}, f32[4,1,4096]{2,1,0:T(1,128)S(1)}, u32[]{:S(2)}, u32[]{:S(2)}) collective-permute-start(f32[4,1,4096]{2,1,0:T(1,128)S(1)} %get-tuple-element.17), channel_id=1, source_target_pairs={{0,16},{16,32},{32,48},{48,64},{64,80},{80,96},{96,112},{112,128},... | collective-permute-start | bytes 196616 | tf_op jit(solution)/shard_map/ppermute | solution.py:33
  76.2 1.9 %collective-permute-start.3 = (f32[4,1,4096]{2,1,0:T(1,128)S(1)}, f32[4,1,4096]{2,1,0:T(1,128)S(1)}, u32[]{:S(2)}, u32[]{:S(2)}) collective-permute-start(f32[4,1,4096]{2,1,0:T(1,128)S(1)} %get-tuple-element.18), channel_id=1, source_target_pairs={{16,0},{32,16},{48,32},{64,48},{80,64},{96,80},{112,96},{128,112},... | collective-permute-start | bytes 196616 | tf_op jit(solution)/shard_map/ppermute | solution.py:35
  78.1 8.6 %collective-permute-done.3 = f32[4,1,4096]{2,1,0:T(1,128)S(1)} collective-permute-done((f32[4,1,4096]{2,1,0:T(1,128)S(1)}, f32[4,1,4096]{2,1,0:T(1,128)S(1)}, u32[]{:S(2)}, u32[]{:S(2)}) %collective-permute-start.3) | collective-permute-done | bytes 65568 | tf_op jit(solution)/shard_map/ppermute | solution.py:35
  86.8 1.9 %collective-permute-start.4 = (f32[1,10,4096]{2,1,0:T(8,128)S(1)}, f32[1,10,4096]{2,1,0:T(8,128)S(1)}, u32[]{:S(2)}, u32[]{:S(2)}) collective-permute-start(f32[1,10,4096]{2,1,0:T(8,128)S(1)} %get-tuple-element.15), channel_id=1, source_target_pairs={{0,1},{1,2},{2,3},{3,4},{4,5},{5,6},{6,7},{7,8},{8,9},{9,10},{10,1... | collective-permute-start | bytes 491528 | tf_op jit(solution)/shard_map/ppermute | solution.py:33
  88.7 3.4 %collective-permute-start.5 = (f32[1,10,4096]{2,1,0:T(8,128)S(1)}, f32[1,10,4096]{2,1,0:T(8,128)S(1)}, u32[]{:S(2)}, u32[]{:S(2)}) collective-permute-start(f32[1,10,4096]{2,1,0:T(8,128)S(1)} %get-tuple-element.16), channel_id=1, source_target_pairs={{1,0},{2,1},{3,2},{4,3},{5,4},{6,5},{7,6},{8,7},{9,8},{10,9},{11,1... | collective-permute-start | bytes 491528 | tf_op jit(solution)/shard_map/ppermute | solution.py:35
  92.1 1.8 %collective-permute-done.4 = f32[1,10,4096]{2,1,0:T(8,128)S(1)} collective-permute-done((f32[1,10,4096]{2,1,0:T(8,128)S(1)}, f32[1,10,4096]{2,1,0:T(8,128)S(1)}, u32[]{:S(2)}, u32[]{:S(2)}) %collective-permute-start.4) | collective-permute-done | bytes 163872 | tf_op jit(solution)/shard_map/ppermute | solution.py:33
  93.9 3.8 %collective-permute-done.5 = f32[1,10,4096]{2,1,0:T(8,128)S(1)} collective-permute-done((f32[1,10,4096]{2,1,0:T(8,128)S(1)}, f32[1,10,4096]{2,1,0:T(8,128)S(1)}, u32[]{:S(2)}, u32[]{:S(2)}) %collective-permute-start.5) | collective-permute-done | bytes 163872 | tf_op jit(solution)/shard_map/ppermute | solution.py:35
  98.8 1.1 fusion
  100.0 1.2 multiply_add_fusion
  101.3 2.9 %collective-permute-start.6 = (f32[4,1,4096]{2,1,0:T(1,128)S(1)}, f32[4,1,4096]{2,1,0:T(1,128)S(1)}, u32[]{:S(2)}, u32[]{:S(2)}) collective-permute-start(f32[4,1,4096]{2,1,0:T(1,128)S(1)} %get-tuple-element.11), channel_id=1, source_target_pairs={{0,16},{16,32},{32,48},{48,64},{64,80},{80,96},{96,112},{112,128},... | collective-permute-start | bytes 196616 | tf_op jit(solution)/shard_map/ppermute | solution.py:33
  104.2 1.9 %collective-permute-start.7 = (f32[4,1,4096]{2,1,0:T(1,128)S(1)}, f32[4,1,4096]{2,1,0:T(1,128)S(1)}, u32[]{:S(2)}, u32[]{:S(2)}) collective-permute-start(f32[4,1,4096]{2,1,0:T(1,128)S(1)} %get-tuple-element.12), channel_id=1, source_target_pairs={{16,0},{32,16},{48,32},{64,48},{80,64},{96,80},{112,96},{128,112},... | collective-permute-start | bytes 196616 | tf_op jit(solution)/shard_map/ppermute | solution.py:35
  106.2 7.9 %collective-permute-done.7 = f32[4,1,4096]{2,1,0:T(1,128)S(1)} collective-permute-done((f32[4,1,4096]{2,1,0:T(1,128)S(1)}, f32[4,1,4096]{2,1,0:T(1,128)S(1)}, u32[]{:S(2)}, u32[]{:S(2)}) %collective-permute-start.7) | collective-permute-done | bytes 65568 | tf_op jit(solution)/shard_map/ppermute | solution.py:35
  114.2 4.9 %collective-permute-start.8 = (f32[1,10,4096]{2,1,0:T(8,128)S(1)}, f32[1,10,4096]{2,1,0:T(8,128)S(1)}, u32[]{:S(2)}, u32[]{:S(2)}) collective-permute-start(f32[1,10,4096]{2,1,0:T(8,128)S(1)} %get-tuple-element.13), channel_id=1, source_target_pairs={{0,1},{1,2},{2,3},{3,4},{4,5},{5,6},{6,7},{7,8},{8,9},{9,10},{10,1... | collective-permute-start | bytes 491528 | tf_op jit(solution)/shard_map/ppermute | solution.py:33
  119.1 1.9 %collective-permute-start.9 = (f32[1,10,4096]{2,1,0:T(8,128)S(1)}, f32[1,10,4096]{2,1,0:T(8,128)S(1)}, u32[]{:S(2)}, u32[]{:S(2)}) collective-permute-start(f32[1,10,4096]{2,1,0:T(8,128)S(1)} %get-tuple-element.14), channel_id=1, source_target_pairs={{1,0},{2,1},{3,2},{4,3},{5,4},{6,5},{7,6},{8,7},{9,8},{10,9},{11,1... | collective-permute-start | bytes 491528 | tf_op jit(solution)/shard_map/ppermute | solution.py:35
  121.0 1.4 %collective-permute-done.8 = f32[1,10,4096]{2,1,0:T(8,128)S(1)} collective-permute-done((f32[1,10,4096]{2,1,0:T(8,128)S(1)}, f32[1,10,4096]{2,1,0:T(8,128)S(1)}, u32[]{:S(2)}, u32[]{:S(2)}) %collective-permute-start.8) | collective-permute-done | bytes 163872 | tf_op jit(solution)/shard_map/ppermute | solution.py:33
  122.4 3.8 %collective-permute-done.9 = f32[1,10,4096]{2,1,0:T(8,128)S(1)} collective-permute-done((f32[1,10,4096]{2,1,0:T(8,128)S(1)}, f32[1,10,4096]{2,1,0:T(8,128)S(1)}, u32[]{:S(2)}, u32[]{:S(2)}) %collective-permute-start.9) | collective-permute-done | bytes 163872 | tf_op jit(solution)/shard_map/ppermute | solution.py:35
  127.4 1.1 fusion.1
  129.0 1.2 fusion.6
  (51 shorter events, 12.0 us)
Async XLA Ops:
  0.9 22.1 %collective-permute-start = (bf16[16,4,256]{2,1,0:T(4,128)(2,1)S(1)}, bf16[16,4,256]{2,1,0:T(4,128)(2,1)S(1)}, u32[]{:S(2)}, u32[]{:S(2)}) collective-permute-start(bf16[16,4,256]{2,1,0:T(4,128)(2,1)S(1)} %get-tuple-element.19), channel_id=1, source_target_pairs={{0,16},{16,32},{32,48},{48,64},{64,80},{80,96},{96,112},{112,128},... | collective-permute-start | bytes 98312 | tf_op jit(solution)/shard_map/ppermute | solution.py:33
  8.4 14.6 %collective-permute-start.1 = (bf16[16,4,256]{2,1,0:T(4,128)(2,1)S(1)}, bf16[16,4,256]{2,1,0:T(4,128)(2,1)S(1)}, u32[]{:S(2)}, u32[]{:S(2)}) collective-permute-start(bf16[16,4,256]{2,1,0:T(4,128)(2,1)S(1)} %get-tuple-element.20), channel_id=1, source_target_pairs={{16,0},{32,16},{48,32},{64,48},{80,64},{96,80},{112,96},{128,112},... | collective-permute-start | bytes 98312 | tf_op jit(solution)/shard_map/ppermute | solution.py:35
  14.6 1.1 copy-start.1
  16.3 6.7 %copy-start = (bf16[16,8,256]{2,1,0:T(8,128)(2,1)S(1)}, bf16[16,8,256]{2,1,0:T(8,128)(2,1)}, u32[]{:S(2)}) copy-start(bf16[16,8,256]{2,1,0:T(8,128)(2,1)} %param.5) | copy-start | bytes 196612
  70.7 7.5 %collective-permute-start.2 = (f32[4,1,4096]{2,1,0:T(1,128)S(1)}, f32[4,1,4096]{2,1,0:T(1,128)S(1)}, u32[]{:S(2)}, u32[]{:S(2)}) collective-permute-start(f32[4,1,4096]{2,1,0:T(1,128)S(1)} %get-tuple-element.17), channel_id=1, source_target_pairs={{0,16},{16,32},{32,48},{48,64},{64,80},{80,96},{96,112},{112,128},... | collective-permute-start | bytes 196616 | tf_op jit(solution)/shard_map/ppermute | solution.py:33
  76.2 10.5 %collective-permute-start.3 = (f32[4,1,4096]{2,1,0:T(1,128)S(1)}, f32[4,1,4096]{2,1,0:T(1,128)S(1)}, u32[]{:S(2)}, u32[]{:S(2)}) collective-permute-start(f32[4,1,4096]{2,1,0:T(1,128)S(1)} %get-tuple-element.18), channel_id=1, source_target_pairs={{16,0},{32,16},{48,32},{64,48},{80,64},{96,80},{112,96},{128,112},... | collective-permute-start | bytes 196616 | tf_op jit(solution)/shard_map/ppermute | solution.py:35
  86.8 7.1 %collective-permute-start.4 = (f32[1,10,4096]{2,1,0:T(8,128)S(1)}, f32[1,10,4096]{2,1,0:T(8,128)S(1)}, u32[]{:S(2)}, u32[]{:S(2)}) collective-permute-start(f32[1,10,4096]{2,1,0:T(8,128)S(1)} %get-tuple-element.15), channel_id=1, source_target_pairs={{0,1},{1,2},{2,3},{3,4},{4,5},{5,6},{6,7},{7,8},{8,9},{9,10},{10,1... | collective-permute-start | bytes 491528 | tf_op jit(solution)/shard_map/ppermute | solution.py:33
  88.7 8.9 %collective-permute-start.5 = (f32[1,10,4096]{2,1,0:T(8,128)S(1)}, f32[1,10,4096]{2,1,0:T(8,128)S(1)}, u32[]{:S(2)}, u32[]{:S(2)}) collective-permute-start(f32[1,10,4096]{2,1,0:T(8,128)S(1)} %get-tuple-element.16), channel_id=1, source_target_pairs={{1,0},{2,1},{3,2},{4,3},{5,4},{6,5},{7,6},{8,7},{9,8},{10,9},{11,1... | collective-permute-start | bytes 491528 | tf_op jit(solution)/shard_map/ppermute | solution.py:35
  101.3 4.9 %collective-permute-start.6 = (f32[4,1,4096]{2,1,0:T(1,128)S(1)}, f32[4,1,4096]{2,1,0:T(1,128)S(1)}, u32[]{:S(2)}, u32[]{:S(2)}) collective-permute-start(f32[4,1,4096]{2,1,0:T(1,128)S(1)} %get-tuple-element.11), channel_id=1, source_target_pairs={{0,16},{16,32},{32,48},{48,64},{64,80},{80,96},{96,112},{112,128},... | collective-permute-start | bytes 196616 | tf_op jit(solution)/shard_map/ppermute | solution.py:33
  104.2 9.9 %collective-permute-start.7 = (f32[4,1,4096]{2,1,0:T(1,128)S(1)}, f32[4,1,4096]{2,1,0:T(1,128)S(1)}, u32[]{:S(2)}, u32[]{:S(2)}) collective-permute-start(f32[4,1,4096]{2,1,0:T(1,128)S(1)} %get-tuple-element.12), channel_id=1, source_target_pairs={{16,0},{32,16},{48,32},{64,48},{80,64},{96,80},{112,96},{128,112},... | collective-permute-start | bytes 196616 | tf_op jit(solution)/shard_map/ppermute | solution.py:35
  114.2 8.2 %collective-permute-start.8 = (f32[1,10,4096]{2,1,0:T(8,128)S(1)}, f32[1,10,4096]{2,1,0:T(8,128)S(1)}, u32[]{:S(2)}, u32[]{:S(2)}) collective-permute-start(f32[1,10,4096]{2,1,0:T(8,128)S(1)} %get-tuple-element.13), channel_id=1, source_target_pairs={{0,1},{1,2},{2,3},{3,4},{4,5},{5,6},{6,7},{7,8},{8,9},{9,10},{10,1... | collective-permute-start | bytes 491528 | tf_op jit(solution)/shard_map/ppermute | solution.py:33
  119.1 7.1 %collective-permute-start.9 = (f32[1,10,4096]{2,1,0:T(8,128)S(1)}, f32[1,10,4096]{2,1,0:T(8,128)S(1)}, u32[]{:S(2)}, u32[]{:S(2)}) collective-permute-start(f32[1,10,4096]{2,1,0:T(8,128)S(1)} %get-tuple-element.14), channel_id=1, source_target_pairs={{1,0},{2,1},{3,2},{4,3},{5,4},{6,5},{7,6},{8,7},{9,8},{10,9},{11,1... | collective-permute-start | bytes 491528 | tf_op jit(solution)/shard_map/ppermute | solution.py:35

commit v4 on v3

--- a/solution.py
+++ b/solution.py
@@ -98,6 +98,38 @@
         ],
         compiler_params=pltpu.CompilerParams(collective_id=0, has_side_effects=True),
     )(local)
+
+
+def with_wide_halo(cells, width):
+    rows, depth = cells.shape[0], cells.shape[1]
+    row_count = lax.axis_size("gy")
+    depth_count = lax.axis_size("gz")
+
+    def moved(piece, row_step, depth_step):
+        pairs = []
+        for a in range(depth_count):
+            for b in range(row_count):
+                ta, tb = a + depth_step, b + row_step
+                if 0 <= ta < depth_count and 0 <= tb < row_count:
+                    pairs.append((a * row_count + b, ta * row_count + tb))
+        return lax.ppermute(piece, ("gz", "gy"), pairs)
+
+    head_rows, tail_rows = slice(0, width), slice(rows - width, rows)
+    head_depth, tail_depth = slice(0, width), slice(depth - width, depth)
+    whole = slice(None)
+    parts = {}
+    for row_step, row_part in ((1, tail_rows), (0, whole), (-1, head_rows)):
+        for depth_step, depth_part in ((1, tail_depth), (0, whole), (-1, head_depth)):
+            if row_step == 0 and depth_step == 0:
+                parts[(0, 0)] = cells
+            else:
+                parts[(row_step, depth_step)] = moved(
+                    cells[row_part, depth_part], row_step, depth_step
+                )
+    bands = [
+        jnp.concatenate([parts[(r, 1)], parts[(r, 0)], parts[(r, -1)]], axis=1) for r in (1, 0, -1)
+    ]
+    return jnp.concatenate(bands, axis=0)
 
 
 def geometry(angle_value):
@@ -281,13 +313,15 @@
     summed = backproject(shifts, tiles, mats, column_count)
     backprojection = math.pi / P_SIZE * summed
     current = backprojection
-    padded_fidelity = jnp.pad(backprojection, ((1, 1), (1, 1), (0, 0)))
+    extended = with_wide_halo(backprojection, ITERS)
+    fidelity = extended
+    current = extended
     for turn_index in range(ITERS):
-        extended = with_halo(current, (("gz", 1), ("gy", 0)), 1)
-        updated = smooth_update(
-            extended, padded_fidelity, row_base - 1, depth_base - 1, rows_total, depth_total
-        )
-        current = updated[1:-1, 1:-1]
+        reach = ITERS - turn_index
+        current = smooth_update(
+            current, fidelity, row_base - reach, depth_base - reach, rows_total, depth_total
+        )[1:-1, 1:-1]
+        fidelity = fidelity[1:-1, 1:-1]
     return current
 
 

time: 131 us -> 122 us (0.931)
  the two profiles are of different devices: /device:TPU:151 before, /device:TPU:159 now
where the time goes in v4:
time: 122 us; the launch traced here: 121 us
  starting transfers between devices  41.7 us (34%)
  Pallas kernels  40.9 us (34%)
  other arithmetic  23.4 us (19%)
  waiting for transfers between devices  10.3 us (8%)
  local copies, waits for them, and re-layouts  3.23 us (3%)
    ppermute x8, starting transfers between devices, moved(): return lax.ppermute(piece, ('gz', 'gy'), pairs)  32.3 us
    pallas_call x1, Pallas kernels, gather_columns(): pl.pallas_call(functools.partial(gather_kernel, count), out_shape=jax.Sha...  27.7 us
    pallas_call x1, Pallas kernels, backproject(): pl.pallas_call(backproject_kernel, out_shape=jax.ShapeDtypeStruct((rows,...  13.2 us
    ppermute x8, waiting for transfers between devices, moved(): return lax.ppermute(piece, ('gz', 'gy'), pairs)  10.3 us
    ppermute x1, starting transfers between devices, with_halo(): lax.ppermute(tail, axis, [(i, (i + 1) % count) for i in range(ends)])  7.49 us
    convert_element_type x1, other arithmetic, footprint_mats(): return jnp.where(valid, weights, 0.0).astype(jnp.bfloat16)  6.66 us
    add x2, other arithmetic, smooth_update(): current + step_length * (smooth_weight * divergence - (current - fidelity))  3.15 us
    pad x1, other arithmetic, per_device(): jnp.pad(tiles.transpose(0, 2, 1, 3), ((0, 0), (1, 2), (0, 0), (0, 0)))  2.84 us
  transfers between devices with their start and end apart: 10, of which 1 were waited for; matrix products, arithmetic and copies ran while one was open for 10% of the time, Pallas kernels for 0%

profile of v4, /device:TPU:159, one launch (start us, length us, event | category | flops | bytes accessed | tf_op | source)
XLA Modules:
  0.0 120.9 jit_solution(9531166658271087)
XLA Ops:
  0.0 0.9 fusion.30
  0.9 7.5 %collective-permute-start = (bf16[16,4,256]{2,1,0:T(4,128)(2,1)S(1)}, bf16[16,4,256]{2,1,0:T(4,128)(2,1)S(1)}, u32[]{:S(2)}, u32[]{:S(2)}) collective-permute-start(bf16[16,4,256]{2,1,0:T(4,128)(2,1)S(1)} %get-tuple-element.19), channel_id=1, source_target_pairs={{0,16},{16,32},{32,48},{48,64},{64,80},{80,96},{96,112},{112,128},... | collective-permute-start | bytes 98312 | tf_op jit(solution)/shard_map/ppermute | solution.py:33
  8.4 1.9 %collective-permute-start.1 = (bf16[16,4,256]{2,1,0:T(4,128)(2,1)S(1)}, bf16[16,4,256]{2,1,0:T(4,128)(2,1)S(1)}, u32[]{:S(2)}, u32[]{:S(2)}) collective-permute-start(bf16[16,4,256]{2,1,0:T(4,128)(2,1)S(1)} %get-tuple-element.20), channel_id=1, source_target_pairs={{16,0},{32,16},{48,32},{64,48},{80,64},{96,80},{112,96},{128,112},... | collective-permute-start | bytes 98312 | tf_op jit(solution)/shard_map/ppermute | solution.py:35
  12.9 0.8 slice.102
  14.6 1.1 iota_subtract_fusion
  16.4 6.7 %select_convert_fusion.mats_ref = bf16[16,4,3,128,128]{4,3,2,1,0:T(8,128)(2,1)} fusion(s32[16,4,1,128,128]{4,3,2,1,0:T(8,128)S(1)} %broadcast_in_dim.10, s32[16,4,1,128,128]{4,3,2,1,0:T(8,128)S(1)} %get-tuple-element.22, s32[16,4,1,128,128]{4,3,2,1,0:T(8,128)S(1)} %get-tuple-element.21, f32[16]{0:T(128)S(1)} %get-tuple-element.26, ...), kind=kLoop, calls=%fused_computation.1 | loop fusion | flops 47185920 | bytes 18907200 | tf_op jit(solution)/shard_map/vmap()/convert_element_type | solution.py:232
  23.1 0.8 convolution_convert_fusion.local_ref
  23.9 27.7 %shard_map.55 = bf16[16,8,4096]{2,1,0:T(8,128)(2,1)} custom-call(bf16[16,8,256]{2,1,0:T(8,128)(2,1)} %convolution_convert_fusion.local_ref), custom_call_target="tpu_custom_call" | custom-call | tf_op jit(solution)/shard_map/pallas_call | solution.py:89
  51.6 2.8 %pad_convert_fusion.tiles_ref = f32[16,35,8,128]{3,2,1,0:T(8,128)} fusion(bf16[16,32,8,128]{3,2,1,0:T(8,128)(2,1)} %bitcast.20), kind=kLoop, calls=%fused_computation.25 | loop fusion | flops 573440 | bytes 3342336 | tf_op jit(solution)/shard_map/jit(_pad)/pad | solution.py:312
  54.4 13.2 %shard_map.56 = f32[4,8,4096]{2,1,0:T(8,128)} custom-call(s32[16,4]{1,0:T(8,128)} %get-tuple-element.24.shift_ref, f32[16,35,8,128]{3,2,1,0:T(8,128)} %pad_convert_fusion.tiles_ref, bf16[16,4,3,128,128]{4,3,2,1,0:T(8,128)(2,1)} %select_convert_fusion.mats_ref), custom_call_target="tpu_custom_call" | custom-call | tf_op jit(solution)/shard_map/pallas_call | solution.py:272
  67.7 1.1 broadcast_multiply_fusion
  68.9 9.4 %collective-permute-start.2 = (f32[2,2,4096]{2,1,0:T(2,128)S(1)}, f32[2,2,4096]{2,1,0:T(2,128)S(1)}, u32[]{:S(2)}, u32[]{:S(2)}) collective-permute-start(f32[2,2,4096]{2,1,0:T(2,128)S(1)} %get-tuple-element.11), channel_id=1, source_target_pairs={{0,17},{1,18},{2,19},{3,20},{4,21},{5,22},{6,23},{7,24},{8,25},{9,... | collective-permute-start | bytes 196616 | tf_op jit(solution)/shard_map/ppermute | solution.py:115
  78.3 1.9 %collective-permute-start.4 = (f32[2,2,4096]{2,1,0:T(2,128)S(1)}, f32[2,2,4096]{2,1,0:T(2,128)S(1)}, u32[]{:S(2)}, u32[]{:S(2)}) collective-permute-start(f32[2,2,4096]{2,1,0:T(2,128)S(1)} %get-tuple-element.14), channel_id=1, source_target_pairs={{16,1},{17,2},{18,3},{19,4},{20,5},{21,6},{22,7},{23,8},{24,9},{25... | collective-permute-start | bytes 196616 | tf_op jit(solution)/shard_map/ppermute | solution.py:115
  80.2 1.9 %collective-permute-start.3 = (f32[2,8,4096]{2,1,0:T(8,128)S(1)}, f32[2,8,4096]{2,1,0:T(8,128)S(1)}, u32[]{:S(2)}, u32[]{:S(2)}) collective-permute-start(f32[2,8,4096]{2,1,0:T(8,128)S(1)} %get-tuple-element.15), channel_id=1, source_target_pairs={{0,1},{1,2},{2,3},{3,4},{4,5},{5,6},{6,7},{7,8},{8,9},{9,10},{10,1... | collective-permute-start | bytes 786440 | tf_op jit(solution)/shard_map/ppermute | solution.py:115
  82.2 3.4 %collective-permute-start.8 = (f32[2,8,4096]{2,1,0:T(8,128)S(1)}, f32[2,8,4096]{2,1,0:T(8,128)S(1)}, u32[]{:S(2)}, u32[]{:S(2)}) collective-permute-start(f32[2,8,4096]{2,1,0:T(8,128)S(1)} %get-tuple-element.16), channel_id=1, source_target_pairs={{1,0},{2,1},{3,2},{4,3},{5,4},{6,5},{7,6},{8,7},{9,8},{10,9},{11,1... | collective-permute-start | bytes 786440 | tf_op jit(solution)/shard_map/ppermute | solution.py:115
  85.6 9.3 %collective-permute-start.7 = (f32[2,2,4096]{2,1,0:T(2,128)S(1)}, f32[2,2,4096]{2,1,0:T(2,128)S(1)}, u32[]{:S(2)}, u32[]{:S(2)}) collective-permute-start(f32[2,2,4096]{2,1,0:T(2,128)S(1)} %get-tuple-element.13), channel_id=1, source_target_pairs={{1,16},{2,17},{3,18},{4,19},{5,20},{6,21},{7,22},{8,23},{9,24},{10... | collective-permute-start | bytes 196616 | tf_op jit(solution)/shard_map/ppermute | solution.py:115
  94.9 1.9 %collective-permute-start.5 = (f32[4,2,4096]{2,1,0:T(2,128)S(1)}, f32[4,2,4096]{2,1,0:T(2,128)S(1)}, u32[]{:S(2)}, u32[]{:S(2)}) collective-permute-start(f32[4,2,4096]{2,1,0:T(2,128)S(1)} %get-tuple-element.17), channel_id=1, source_target_pairs={{0,16},{1,17},{2,18},{3,19},{4,20},{5,21},{6,22},{7,23},{8,24},{9,... | collective-permute-start | bytes 393224 | tf_op jit(solution)/shard_map/ppermute | solution.py:115
  96.9 2.4 %collective-permute-start.6 = (f32[4,2,4096]{2,1,0:T(2,128)S(1)}, f32[4,2,4096]{2,1,0:T(2,128)S(1)}, u32[]{:S(2)}, u32[]{:S(2)}) collective-permute-start(f32[4,2,4096]{2,1,0:T(2,128)S(1)} %get-tuple-element.18), channel_id=1, source_target_pairs={{16,0},{17,1},{18,2},{19,3},{20,4},{21,5},{22,6},{23,7},{24,8},{25... | collective-permute-start | bytes 393224 | tf_op jit(solution)/shard_map/ppermute | solution.py:115
  99.3 2.1 %collective-permute-start.9 = (f32[2,2,4096]{2,1,0:T(2,128)S(1)}, f32[2,2,4096]{2,1,0:T(2,128)S(1)}, u32[]{:S(2)}, u32[]{:S(2)}) collective-permute-start(f32[2,2,4096]{2,1,0:T(2,128)S(1)} %get-tuple-element.12), channel_id=1, source_target_pairs={{17,0},{18,1},{19,2},{20,3},{21,4},{22,5},{23,6},{24,7},{25,8},{26... | collective-permute-start | bytes 196616 | tf_op jit(solution)/shard_map/ppermute | solution.py:115
  101.5 10.3 %collective-permute-done.9 = f32[2,2,4096]{2,1,0:T(2,128)S(1)} collective-permute-done((f32[2,2,4096]{2,1,0:T(2,128)S(1)}, f32[2,2,4096]{2,1,0:T(2,128)S(1)}, u32[]{:S(2)}, u32[]{:S(2)}) %collective-permute-start.9) | collective-permute-done | bytes 65568 | tf_op jit(solution)/shard_map/ppermute | solution.py:115
  113.2 1.5 %fusion = (f32[8,12,4096]{2,1,0:T(8,128)S(1)}, f32[8,12,4096]{2,1,0:T(8,128)S(1)}, f32[8,12,4096]{2,1,0:T(8,128)S(1)}) fusion(f32[7,12,4096]{2,1,0:T(8,128)S(1)} %slice_subtract_fusion.2, f32[8]{0:T(128)S(1)} %and_convert_fusion.3, f32[8,12,4095]{2,1,0:T(8,128)S(1)} %slice_subtract_fusion, f32[12]{0:T(128)S(1)} %and_convert_fusion.2, ...), kind=kLoop, calls=%fused_computation.11 | loop fusion | flops 4325376 | bytes 9109200 | tf_op jit(solution)/shard_map/div | solution.py:191
  114.9 1.9 %multiply_add_fusion = f32[8,12,4096]{2,1,0:T(8,128)S(1)} fusion(f32[8,12,4095]{2,1,0:T(8,128)S(1)} %bitcast.16, f32[8,12,4096]{2,1,0:T(8,128)S(1)} %get-tuple-element.6, f32[8,11,4096]{2,1,0:T(8,128)S(1)} %bitcast.17, f32[8,12,4096]{2,1,0:T(8,128)S(1)} %get-tuple-element.7, f32[8,12,4096]{2,1,0:T(8,128)S(1)} %get-tuple-element.5, ...), kind=kLoop, calls=%fused_computation.6 | loop fusion | flops 7077888 | bytes 12254848 | tf_op jit(solution)/shard_map/add | solution.py:207
  118.0 1.1 fusion.2
  119.7 1.2 %fusion.6 = f32[4,8,4096]{2,1,0:T(8,128)} fusion(f32[6,10,4096]{2,1,0:T(8,128)S(1)} %slice.161, f32[6,10,4096]{2,1,0:T(8,128)S(1)} %slice.151, f32[6,10,4095]{2,1,0:T(8,128)S(1)} %bitcast.19, f32[6,10,4096]{2,1,0:T(8,128)S(1)} %get-tuple-element.9, f32[6,10,4096]{2,1,0:T(8,128)S(1)} %pad_subtract_fusion), kind=kLoop, calls=%fused_computation.30 | loop fusion | flops 917504 | bytes 3604240 | tf_op jit(solution)/shard_map/add | solution.py:207
  (52 shorter events, 7.4 us)
Async XLA Ops:
  0.9 22.1 %collective-permute-start = (bf16[16,4,256]{2,1,0:T(4,128)(2,1)S(1)}, bf16[16,4,256]{2,1,0:T(4,128)(2,1)S(1)}, u32[]{:S(2)}, u32[]{:S(2)}) collective-permute-start(bf16[16,4,256]{2,1,0:T(4,128)(2,1)S(1)} %get-tuple-element.19), channel_id=1, source_target_pairs={{0,16},{16,32},{32,48},{48,64},{64,80},{80,96},{96,112},{112,128},... | collective-permute-start | bytes 98312 | tf_op jit(solution)/shard_map/ppermute | solution.py:33
  8.4 14.6 %collective-permute-start.1 = (bf16[16,4,256]{2,1,0:T(4,128)(2,1)S(1)}, bf16[16,4,256]{2,1,0:T(4,128)(2,1)S(1)}, u32[]{:S(2)}, u32[]{:S(2)}) collective-permute-start(bf16[16,4,256]{2,1,0:T(4,128)(2,1)S(1)} %get-tuple-element.20), channel_id=1, source_target_pairs={{16,0},{32,16},{48,32},{64,48},{80,64},{96,80},{112,96},{128,112},... | collective-permute-start | bytes 98312 | tf_op jit(solution)/shard_map/ppermute | solution.py:35
  14.6 1.1 copy-start.1
  16.4 6.7 %copy-start = (bf16[16,8,256]{2,1,0:T(8,128)(2,1)S(1)}, bf16[16,8,256]{2,1,0:T(8,128)(2,1)}, u32[]{:S(2)}) copy-start(bf16[16,8,256]{2,1,0:T(8,128)(2,1)} %param.5) | copy-start | bytes 196612
  68.9 26.0 %collective-permute-start.2 = (f32[2,2,4096]{2,1,0:T(2,128)S(1)}, f32[2,2,4096]{2,1,0:T(2,128)S(1)}, u32[]{:S(2)}, u32[]{:S(2)}) collective-permute-start(f32[2,2,4096]{2,1,0:T(2,128)S(1)} %get-tuple-element.11), channel_id=1, source_target_pairs={{0,17},{1,18},{2,19},{3,20},{4,21},{5,22},{6,23},{7,24},{8,25},{9,... | collective-permute-start | bytes 196616 | tf_op jit(solution)/shard_map/ppermute | solution.py:115
  78.3 18.6 %collective-permute-start.4 = (f32[2,2,4096]{2,1,0:T(2,128)S(1)}, f32[2,2,4096]{2,1,0:T(2,128)S(1)}, u32[]{:S(2)}, u32[]{:S(2)}) collective-permute-start(f32[2,2,4096]{2,1,0:T(2,128)S(1)} %get-tuple-element.14), channel_id=1, source_target_pairs={{16,1},{17,2},{18,3},{19,4},{20,5},{21,6},{22,7},{23,8},{24,9},{25... | collective-permute-start | bytes 196616 | tf_op jit(solution)/shard_map/ppermute | solution.py:115
  80.2 31.6 %collective-permute-start.3 = (f32[2,8,4096]{2,1,0:T(8,128)S(1)}, f32[2,8,4096]{2,1,0:T(8,128)S(1)}, u32[]{:S(2)}, u32[]{:S(2)}) collective-permute-start(f32[2,8,4096]{2,1,0:T(8,128)S(1)} %get-tuple-element.15), channel_id=1, source_target_pairs={{0,1},{1,2},{2,3},{3,4},{4,5},{5,6},{6,7},{7,8},{8,9},{9,10},{10,1... | collective-permute-start | bytes 786440 | tf_op jit(solution)/shard_map/ppermute | solution.py:115
  82.2 29.6 %collective-permute-start.8 = (f32[2,8,4096]{2,1,0:T(8,128)S(1)}, f32[2,8,4096]{2,1,0:T(8,128)S(1)}, u32[]{:S(2)}, u32[]{:S(2)}) collective-permute-start(f32[2,8,4096]{2,1,0:T(8,128)S(1)} %get-tuple-element.16), channel_id=1, source_target_pairs={{1,0},{2,1},{3,2},{4,3},{5,4},{6,5},{7,6},{8,7},{9,8},{10,9},{11,1... | collective-permute-start | bytes 786440 | tf_op jit(solution)/shard_map/ppermute | solution.py:115
  85.6 13.7 %collective-permute-start.7 = (f32[2,2,4096]{2,1,0:T(2,128)S(1)}, f32[2,2,4096]{2,1,0:T(2,128)S(1)}, u32[]{:S(2)}, u32[]{:S(2)}) collective-permute-start(f32[2,2,4096]{2,1,0:T(2,128)S(1)} %get-tuple-element.13), channel_id=1, source_target_pairs={{1,16},{2,17},{3,18},{4,19},{5,20},{6,21},{7,22},{8,23},{9,24},{10... | collective-permute-start | bytes 196616 | tf_op jit(solution)/shard_map/ppermute | solution.py:115
  94.9 16.8 %collective-permute-start.5 = (f32[4,2,4096]{2,1,0:T(2,128)S(1)}, f32[4,2,4096]{2,1,0:T(2,128)S(1)}, u32[]{:S(2)}, u32[]{:S(2)}) collective-permute-start(f32[4,2,4096]{2,1,0:T(2,128)S(1)} %get-tuple-element.17), channel_id=1, source_target_pairs={{0,16},{1,17},{2,18},{3,19},{4,20},{5,21},{6,22},{7,23},{8,24},{9,... | collective-permute-start | bytes 393224 | tf_op jit(solution)/shard_map/ppermute | solution.py:115
  96.9 14.9 %collective-permute-start.6 = (f32[4,2,4096]{2,1,0:T(2,128)S(1)}, f32[4,2,4096]{2,1,0:T(2,128)S(1)}, u32[]{:S(2)}, u32[]{:S(2)}) collective-permute-start(f32[4,2,4096]{2,1,0:T(2,128)S(1)} %get-tuple-element.18), channel_id=1, source_target_pairs={{16,0},{17,1},{18,2},{19,3},{20,4},{21,5},{22,6},{23,7},{24,8},{25... | collective-permute-start | bytes 393224 | tf_op jit(solution)/shard_map/ppermute | solution.py:115
  99.3 12.4 %collective-permute-start.9 = (f32[2,2,4096]{2,1,0:T(2,128)S(1)}, f32[2,2,4096]{2,1,0:T(2,128)S(1)}, u32[]{:S(2)}, u32[]{:S(2)}) collective-permute-start(f32[2,2,4096]{2,1,0:T(2,128)S(1)} %get-tuple-element.12), channel_id=1, source_target_pairs={{17,0},{18,1},{19,2},{20,3},{21,4},{22,5},{23,6},{24,7},{25,8},{26... | collective-permute-start | bytes 196616 | tf_op jit(solution)/shard_map/ppermute | solution.py:115

commit v5 on v3

--- a/solution.py
+++ b/solution.py
@@ -98,6 +98,66 @@
         ],
         compiler_params=pltpu.CompilerParams(collective_id=0, has_side_effects=True),
     )(local)
+
+
+STEPS = ((1, 1), (1, 0), (1, -1), (0, 1), (0, -1), (-1, 1), (-1, 0), (-1, -1))
+
+
+def halo_kernel(count, *refs):
+    pieces = len(STEPS)
+    sources, targets = refs[:pieces], refs[pieces:2 * pieces]
+    send_sem, recv_sem = refs[2 * pieces], refs[2 * pieces + 1]
+    row_count, depth_count = count
+    row_me = lax.axis_index("gy")
+    depth_me = lax.axis_index("gz")
+    peers = [
+        (lax.rem(depth_me + depth_step + depth_count, depth_count),
+         lax.rem(row_me + row_step + row_count, row_count))
+        for row_step, depth_step in STEPS
+    ]
+    barrier = pltpu.get_barrier_semaphore()
+    for peer in peers:
+        pl.semaphore_signal(barrier, inc=1, device_id=peer, device_id_type=pl.DeviceIdType.MESH)
+    pl.semaphore_wait(barrier, pieces)
+    copies = []
+    for k, peer in enumerate(peers):
+        copy = pltpu.make_async_remote_copy(
+            src_ref=sources[k],
+            dst_ref=targets[k],
+            send_sem=send_sem.at[k],
+            recv_sem=recv_sem.at[k],
+            device_id=peer,
+            device_id_type=pl.DeviceIdType.MESH,
+        )
+        copy.start()
+        copies.append(copy)
+    for copy in copies:
+        copy.wait()
+
+
+def with_wide_halo(cells, width):
+    rows, depth = cells.shape[0], cells.shape[1]
+    count = (lax.axis_size("gy"), lax.axis_size("gz"))
+    row_parts = {1: slice(rows - width, rows), 0: slice(None), -1: slice(0, width)}
+    depth_parts = {1: slice(depth - width, depth), 0: slice(None), -1: slice(0, width)}
+    sent = [cells[row_parts[r], depth_parts[d]] for r, d in STEPS]
+    received = pl.pallas_call(
+        functools.partial(halo_kernel, count),
+        out_shape=[jax.ShapeDtypeStruct(piece.shape, piece.dtype) for piece in sent],
+        in_specs=[pl.BlockSpec(memory_space=pl.ANY)] * len(STEPS),
+        out_specs=[pl.BlockSpec(memory_space=pl.ANY)] * len(STEPS),
+        scratch_shapes=[
+            pltpu.SemaphoreType.DMA((len(STEPS),)),
+            pltpu.SemaphoreType.DMA((len(STEPS),)),
+        ],
+        compiler_params=pltpu.CompilerParams(collective_id=1, has_side_effects=True),
+    )(*sent)
+    parts = dict(zip(STEPS, received))
+    parts[(0, 0)] = cells
+    bands = [
+        jnp.concatenate([parts[(r, 1)], parts[(r, 0)], parts[(r, -1)]], axis=1) for r in (1, 0, -1)
+    ]
+    return jnp.concatenate(bands, axis=0)
 
 
 def geometry(angle_value):
@@ -281,13 +341,15 @@
     summed = backproject(shifts, tiles, mats, column_count)
     backprojection = math.pi / P_SIZE * summed
     current = backprojection
-    padded_fidelity = jnp.pad(backprojection, ((1, 1), (1, 1), (0, 0)))
+    extended = with_wide_halo(backprojection, ITERS)
+    fidelity = extended
+    current = extended
     for turn_index in range(ITERS):
-        extended = with_halo(current, (("gz", 1), ("gy", 0)), 1)
-        updated = smooth_update(
-            extended, padded_fidelity, row_base - 1, depth_base - 1, rows_total, depth_total
-        )
-        current = updated[1:-1, 1:-1]
+        reach = ITERS - turn_index
+        current = smooth_update(
+            current, fidelity, row_base - reach, depth_base - reach, rows_total, depth_total
+        )[1:-1, 1:-1]
+        fidelity = fidelity[1:-1, 1:-1]
     return current
 
 

time: 131 us -> 107 us (0.82)
  the two profiles are of different devices: /device:TPU:151 before, /device:TPU:135 now
where the time goes in v5:
time: 107 us; the launch traced here: 106 us
  Pallas kernels  64.9 us (61%)
  other arithmetic  24.6 us (23%)
  starting transfers between devices  9.42 us (9%)
  local copies, waits for them, and re-layouts  6.32 us (6%)
    pallas_call x1, Pallas kernels, gather_columns(): pl.pallas_call(functools.partial(gather_kernel, count), out_shape=jax.Sha...  29.9 us
    pallas_call x1, Pallas kernels, with_wide_halo(): pl.pallas_call(functools.partial(halo_kernel, count), out_shape=[jax.Shap...  21.7 us
    pallas_call x1, Pallas kernels, backproject(): pl.pallas_call(backproject_kernel, out_shape=jax.ShapeDtypeStruct((rows,...  13.2 us
    ppermute x1, starting transfers between devices, with_halo(): lax.ppermute(tail, axis, [(i, (i + 1) % count) for i in range(ends)])  7.49 us
    convert_element_type x1, other arithmetic, footprint_mats(): return jnp.where(valid, weights, 0.0).astype(jnp.bfloat16)  6.66 us
    add x2, other arithmetic, smooth_update(): current + step_length * (smooth_weight * divergence - (current - fidelity))  3.13 us
    pad x1, other arithmetic, per_device(): jnp.pad(tiles.transpose(0, 2, 1, 3), ((0, 0), (1, 2), (0, 0), (0, 0)))  2.83 us
    div x2, other arithmetic, smooth_update(): normal_rows = forward_rows / magnitude  2.65 us
  transfers between devices with their start and end apart: 2, of which 0 were waited for; matrix products, arithmetic and copies ran while one was open for 12% of the time, Pallas kernels for 0%

profile of v5, /device:TPU:135, one launch (start us, length us, event | category | flops | bytes accessed | tf_op | source)
XLA Modules:
  0.0 106.4 jit_solution(6744986657937459154)
XLA Ops:
  0.0 0.9 fusion.30
  0.9 7.5 %collective-permute-start = (bf16[16,4,256]{2,1,0:T(4,128)(2,1)S(1)}, bf16[16,4,256]{2,1,0:T(4,128)(2,1)S(1)}, u32[]{:S(2)}, u32[]{:S(2)}) collective-permute-start(bf16[16,4,256]{2,1,0:T(4,128)(2,1)S(1)} %get-tuple-element.35), channel_id=1, source_target_pairs={{0,16},{16,32},{32,48},{48,64},{64,80},{80,96},{96,112},{112,128},... | collective-permute-start | bytes 98312 | tf_op jit(solution)/shard_map/ppermute | solution.py:33
  8.4 1.9 %collective-permute-start.1 = (bf16[16,4,256]{2,1,0:T(4,128)(2,1)S(1)}, bf16[16,4,256]{2,1,0:T(4,128)(2,1)S(1)}, u32[]{:S(2)}, u32[]{:S(2)}) collective-permute-start(bf16[16,4,256]{2,1,0:T(4,128)(2,1)S(1)} %get-tuple-element.36), channel_id=1, source_target_pairs={{16,0},{32,16},{48,32},{64,48},{80,64},{96,80},{112,96},{128,112},... | collective-permute-start | bytes 98312 | tf_op jit(solution)/shard_map/ppermute | solution.py:35
  10.4 0.7 convert_bitcast_fusion
  11.1 0.7 bitcast_add_fusion
  11.8 0.7 multiply_add_fusion.3
  12.9 0.8 slice.102
  14.6 1.1 %iota_subtract_fusion = (s32[16,4,1,128,128]{4,3,2,1,0:T(8,128)S(1)}, s32[16,4,1,128,128]{4,3,2,1,0:T(8,128)S(1)}) fusion(s32[16,4,128]{2,1,0:T(4,128)S(1)} %add_multiply_fusion, s32[128]{0:T(128)S(1)} %iota_add_fusion), kind=kLoop, calls=%fused_computation.2 | loop fusion | flops 2097152 | bytes 8421888 | tf_op jit(solution)/shard_map/vmap()/sub | solution.py:249
  16.4 6.7 %select_convert_fusion.mats_ref = bf16[16,4,3,128,128]{4,3,2,1,0:T(8,128)(2,1)} fusion(s32[16,4,1,128,128]{4,3,2,1,0:T(8,128)S(1)} %broadcast_in_dim.10, s32[16,4,1,128,128]{4,3,2,1,0:T(8,128)S(1)} %get-tuple-element.38, s32[16,4,1,128,128]{4,3,2,1,0:T(8,128)S(1)} %get-tuple-element.37, f32[16]{0:T(128)S(1)} %get-tuple-element.42, ...), kind=kLoop, calls=%fused_computation.1 | loop fusion | flops 47185920 | bytes 18907200 | tf_op jit(solution)/shard_map/vmap()/convert_element_type | solution.py:260
  23.1 0.8 convolution_convert_fusion.local_ref
  23.9 29.9 %shard_map.55 = bf16[16,8,4096]{2,1,0:T(8,128)(2,1)} custom-call(bf16[16,8,256]{2,1,0:T(8,128)(2,1)} %convolution_convert_fusion.local_ref), custom_call_target="tpu_custom_call" | custom-call | tf_op jit(solution)/shard_map/pallas_call | solution.py:89
  53.9 2.8 %pad_convert_fusion.tiles_ref = f32[16,35,8,128]{3,2,1,0:T(8,128)} fusion(bf16[16,32,8,128]{3,2,1,0:T(8,128)(2,1)} %bitcast.20), kind=kLoop, calls=%fused_computation.25 | loop fusion | flops 573440 | bytes 3342336 | tf_op jit(solution)/shard_map/jit(_pad)/pad | solution.py:340
  56.7 13.2 %shard_map.56 = f32[4,8,4096]{2,1,0:T(8,128)} custom-call(s32[16,4]{1,0:T(8,128)} %get-tuple-element.40.shift_ref, f32[16,35,8,128]{3,2,1,0:T(8,128)} %pad_convert_fusion.tiles_ref, bf16[16,4,3,128,128]{4,3,2,1,0:T(8,128)(2,1)} %select_convert_fusion.mats_ref), custom_call_target="tpu_custom_call" | custom-call | tf_op jit(solution)/shard_map/pallas_call | solution.py:300
  70.0 1.1 %broadcast_multiply_fusion = f32[4,8,4096]{2,1,0:T(8,128)S(1)} fusion(f32[4,8,4096]{2,1,0:T(8,128)} %shard_map.56), kind=kLoop, calls=%fused_computation.34 | loop fusion | flops 131072 | bytes 1048576 | tf_op jit(solution)/shard_map/mul | solution.py:342
  71.1 0.7 fusion.27
  71.8 0.8 fusion.28
  72.6 0.8 fusion.29
  73.4 21.7 %shard_map.57 = (f32[2,2,4096]{2,1,0:T(2,128)}, f32[2,8,4096]{2,1,0:T(8,128)}, f32[2,2,4096]{2,1,0:T(2,128)}, f32[4,2,4096]{2,1,0:T(2,128)}, f32[4,2,4096]{2,1,0...) custom-call(f32[2,2,4096]{2,1,0:T(2,128)} %get-tuple-element.30.refs_0_, ...), custom_call_target="tpu_custom_call" | custom-call | tf_op jit(solution)/shard_map/pallas_call | solution.py:144
  95.1 1.6 %maximum_maximum_fusion = f32[8,12,4096]{2,1,0:T(8,128)S(1)} fusion(f32[2,2,4096]{2,1,0:T(2,128)} %get-tuple-element.20, f32[2,8,4096]{2,1,0:T(8,128)} %get-tuple-element.19, f32[2,2,4096]{2,1,0:T(2,128)} %get-tuple-element.18, f32[4,2,4096]{2,1,0:T(2,128)} %get-tuple-element.17, f32[4,8,4096]{2,1,0:T(8,128)S(1)} %broadcast_multiply_fusion, ...), kind=kLoop, calls=%fused_computation.5 | loop fusion | flops 3145728 | bytes 3145728 | tf_op jit(solution)/shard_map/concatenate | solution.py:160
  97.7 1.5 %fusion = (f32[8,12,4096]{2,1,0:T(8,128)S(1)}, f32[8,12,4096]{2,1,0:T(8,128)S(1)}, f32[8,12,4096]{2,1,0:T(8,128)S(1)}) fusion(f32[7,12,4096]{2,1,0:T(8,128)S(1)} %slice_subtract_fusion.2, f32[8]{0:T(128)S(1)} %and_convert_fusion.3, f32[8,12,4095]{2,1,0:T(8,128)S(1)} %slice_subtract_fusion, f32[12]{0:T(128)S(1)} %and_convert_fusion.2, ...), kind=kLoop, calls=%fused_computation.11 | loop fusion | flops 4325376 | bytes 9109200 | tf_op jit(solution)/shard_map/div | solution.py:219
  99.5 0.7 copy-done
  100.4 1.9 %multiply_add_fusion = f32[8,12,4096]{2,1,0:T(8,128)S(1)} fusion(f32[8,12,4095]{2,1,0:T(8,128)S(1)} %bitcast.16, f32[8,12,4096]{2,1,0:T(8,128)S(1)} %get-tuple-element.22, f32[8,11,4096]{2,1,0:T(8,128)S(1)} %bitcast.17, f32[8,12,4096]{2,1,0:T(8,128)S(1)} %get-tuple-element.23, f32[8,12,4096]{2,1,0:T(8,128)S(1)} %get-tuple-element.21, ...), kind=kLoop, calls=%fused_computation.6 | loop fusion | flops 7077888 | bytes 12254848 | tf_op jit(solution)/shard_map/add | solution.py:235
  103.5 1.1 %fusion.2 = (f32[6,10,4096]{2,1,0:T(8,128)S(1)}, f32[6,10,4096]{2,1,0:T(8,128)S(1)}, f32[6,10,4096]{2,1,0:T(8,128)S(1)}) fusion(f32[5,10,4096]{2,1,0:T(8,128)S(1)} %slice_subtract_fusion.5, f32[6]{0:T(128)S(1)} %and_convert_fusion.1, f32[6,10,4095]{2,1,0:T(8,128)S(1)} %slice_subtract_fusion.3, f32[10]{0:T(128)S(1)} %and_convert_fusion, ...), kind=kLoop, calls=%fused_computation.21 | loop fusion | flops 2703360 | bytes 5635920 | tf_op jit(solution)/shard_map/div | solution.py:219
  105.2 1.2 %fusion.6 = f32[4,8,4096]{2,1,0:T(8,128)} fusion(f32[6,10,4096]{2,1,0:T(8,128)S(1)} %slice.161, f32[6,10,4096]{2,1,0:T(8,128)S(1)} %slice.151, f32[6,10,4095]{2,1,0:T(8,128)S(1)} %bitcast.19, f32[6,10,4096]{2,1,0:T(8,128)S(1)} %get-tuple-element.25, f32[6,10,4096]{2,1,0:T(8,128)S(1)} %pad_subtract_fusion), kind=kLoop, calls=%fused_computation.30 | loop fusion | flops 917504 | bytes 3604240 | tf_op jit(solution)/shard_map/add | solution.py:235
  (53 shorter events, 5.0 us)
Async XLA Ops:
  0.9 22.1 %collective-permute-start = (bf16[16,4,256]{2,1,0:T(4,128)(2,1)S(1)}, bf16[16,4,256]{2,1,0:T(4,128)(2,1)S(1)}, u32[]{:S(2)}, u32[]{:S(2)}) collective-permute-start(bf16[16,4,256]{2,1,0:T(4,128)(2,1)S(1)} %get-tuple-element.35), channel_id=1, source_target_pairs={{0,16},{16,32},{32,48},{48,64},{64,80},{80,96},{96,112},{112,128},... | collective-permute-start | bytes 98312 | tf_op jit(solution)/shard_map/ppermute | solution.py:33
  8.4 14.6 %collective-permute-start.1 = (bf16[16,4,256]{2,1,0:T(4,128)(2,1)S(1)}, bf16[16,4,256]{2,1,0:T(4,128)(2,1)S(1)}, u32[]{:S(2)}, u32[]{:S(2)}) collective-permute-start(bf16[16,4,256]{2,1,0:T(4,128)(2,1)S(1)} %get-tuple-element.36), channel_id=1, source_target_pairs={{16,0},{32,16},{48,32},{64,48},{80,64},{96,80},{112,96},{128,112},... | collective-permute-start | bytes 98312 | tf_op jit(solution)/shard_map/ppermute | solution.py:35
  14.6 1.1 %copy-start.9 = (s32[16,1]{0,1:T(1,128)S(1)}, s32[16,1]{0,1:T(1,128)}, u32[]{:S(2)}) copy-start(s32[16,1]{0,1:T(1,128)} %param.7) | copy-start | bytes 196
  16.4 6.7 %copy-start.8 = (bf16[16,8,256]{2,1,0:T(8,128)(2,1)S(1)}, bf16[16,8,256]{2,1,0:T(8,128)(2,1)}, u32[]{:S(2)}) copy-start(bf16[16,8,256]{2,1,0:T(8,128)(2,1)} %param.5) | copy-start | bytes 196612
  99.2 1.0 copy-start
  99.3 1.0 copy-start.1
  99.3 1.0 copy-start.2
  99.3 1.1 %copy-start.3 = (f32[4,2,4096]{2,1,0:T(2,128)S(1)}, f32[4,2,4096]{2,1,0:T(2,128)}, u32[]{:S(2)}) copy-start(f32[4,2,4096]{2,1,0:T(2,128)} %get-tuple-element.17) | copy-start | bytes 393220
  99.3 1.1 %copy-start.4 = (f32[2,2,4096]{2,1,0:T(2,128)S(1)}, f32[2,2,4096]{2,1,0:T(2,128)}, u32[]{:S(2)}) copy-start(f32[2,2,4096]{2,1,0:T(2,128)} %get-tuple-element.13) | copy-start | bytes 196612
  99.3 1.1 copy-start.5
  99.3 1.1 copy-start.6
  99.3 1.1 %copy-start.7 = (f32[2,2,4096]{2,1,0:T(2,128)S(1)}, f32[2,2,4096]{2,1,0:T(2,128)}, u32[]{:S(2)}) copy-start(f32[2,2,4096]{2,1,0:T(2,128)} %get-tuple-element.20) | copy-start | bytes 196612

commit v6 on v5

--- a/solution.py
+++ b/solution.py
@@ -40,47 +40,77 @@
 
 
 def gather_kernel(count, local_ref, out_ref, send_sem, recv_sem, own_sem):
+    ring = count // 2
+    forward_steps = ring // 2
+    backward_steps = ring - 1 - forward_steps
     me = lax.axis_index("gy")
     depth_index = lax.axis_index("gz")
+    half = me // ring
+    place = me % ring
     width = local_ref.shape[2]
+    mesh_kind = pl.DeviceIdType.MESH
+
+    def device(half_of, place_of):
+        return half_of * ring + lax.rem(place_of + 2 * ring, ring)
+
+    partner = device(1 - half, place)
+    right = device(half, place + 1)
+    left = device(half, place - 1)
+
+    def slot(index):
+        return out_ref.at[:, :, pl.ds(pl.multiple_of(index * width, width), width)]
+
     barrier = pltpu.get_barrier_semaphore()
-    for step in range(1, count):
-        peer = lax.rem(me + step, count)
-        pl.semaphore_signal(
-            barrier, inc=1, device_id=(depth_index, peer), device_id_type=pl.DeviceIdType.MESH
-        )
-    pl.semaphore_wait(barrier, count - 1)
-    own_slot = pl.ds(pl.multiple_of(me * width, width), width)
-    own = pltpu.make_async_copy(local_ref, out_ref.at[:, :, own_slot], own_sem)
+    for peer in (partner, right, left):
+        pl.semaphore_signal(barrier, inc=1, device_id=(depth_index, peer), device_id_type=mesh_kind)
+    pl.semaphore_wait(barrier, 3)
+
+    own = pltpu.make_async_copy(local_ref, slot(me), own_sem)
     own.start()
     sends = []
-    for step in range(1, count):
-        peer = lax.rem(me + step, count)
+
+    def send(source, index, peer):
         copy = pltpu.make_async_remote_copy(
-            src_ref=local_ref,
-            dst_ref=out_ref.at[:, :, own_slot],
-            send_sem=send_sem.at[step],
-            recv_sem=recv_sem.at[step],
+            src_ref=source,
+            dst_ref=slot(index),
+            send_sem=send_sem.at[len(sends)],
+            recv_sem=recv_sem.at[index],
             device_id=(depth_index, peer),
-            device_id_type=pl.DeviceIdType.MESH,
+            device_id_type=mesh_kind,
         )
         copy.start()
         sends.append(copy)
+
+    def arrived(index):
+        pltpu.make_async_remote_copy(
+            src_ref=local_ref,
+            dst_ref=slot(index),
+            send_sem=send_sem.at[0],
+            recv_sem=recv_sem.at[index],
+            device_id=(depth_index, partner),
+            device_id_type=mesh_kind,
+        ).wait_recv()
+
+    send(local_ref, me, partner)
+    arrived(partner)
+    for step in range(1, forward_steps + 1):
+        for direction, peer, limit in ((-1, right, forward_steps), (1, left, backward_steps)):
+            if step > limit:
+                continue
+            if step == 1:
+                send(local_ref, me, peer)
+                send(slot(partner), partner, peer)
+                continue
+            for half_of in (0, 1):
+                index = device(half_of, place + direction * (step - 1))
+                arrived(index)
+                send(slot(index), index, peer)
+    for direction, steps in ((-1, forward_steps), (1, backward_steps)):
+        for half_of in (0, 1):
+            arrived(device(half_of, place + direction * steps))
     own.wait()
     for copy in sends:
         copy.wait_send()
-    for step in range(1, count):
-        sender = lax.rem(me + count - step, count)
-        slot = pl.ds(pl.multiple_of(sender * width, width), width)
-        arriving = pltpu.make_async_remote_copy(
-            src_ref=local_ref,
-            dst_ref=out_ref.at[:, :, slot],
-            send_sem=send_sem.at[step],
-            recv_sem=recv_sem.at[step],
-            device_id=(depth_index, sender),
-            device_id_type=pl.DeviceIdType.MESH,
-        )
-        arriving.wait_recv()
 
 
 def gather_columns(local):

time: 107 us -> 106 us (level)
  the two profiles are of different devices: /device:TPU:135 before, /device:TPU:56 now
where the time goes in v6:
time: 106 us; the launch traced here: 105 us
  Pallas kernels  69.8 us (66%)
  other arithmetic  24.6 us (23%)
  local copies, waits for them, and re-layouts  6.32 us (6%)
  starting transfers between devices  3.03 us (3%)
    pallas_call x1, Pallas kernels, with_wide_halo(): pl.pallas_call(functools.partial(halo_kernel, count), out_shape=[jax.Shap...  30.6 us
    pallas_call x1, Pallas kernels, gather_columns(): pl.pallas_call(functools.partial(gather_kernel, count), out_shape=jax.Sha...  25.9 us
    pallas_call x1, Pallas kernels, backproject(): pl.pallas_call(backproject_kernel, out_shape=jax.ShapeDtypeStruct((rows,...  13.2 us
    convert_element_type x1, other arithmetic, footprint_mats(): return jnp.where(valid, weights, 0.0).astype(jnp.bfloat16)  6.66 us
    add x2, other arithmetic, smooth_update(): current + step_length * (smooth_weight * divergence - (current - fidelity))  3.13 us
    pad x1, other arithmetic, per_device(): jnp.pad(tiles.transpose(0, 2, 1, 3), ((0, 0), (1, 2), (0, 0), (0, 0)))  2.83 us
    div x2, other arithmetic, smooth_update(): normal_rows = forward_rows / magnitude  2.65 us
    slice x3, local copies, waits for them, and re-layouts, with_wide_halo(): sent = [cells[row_parts[r], depth_parts[d]] for r, d in STEPS]  2.36 us
  transfers between devices with their start and end apart: 2, of which 0 were waited for; matrix products, arithmetic and copies ran while one was open for 12% of the time, Pallas kernels for 0%

profile of v6, /device:TPU:56, one launch (start us, length us, event | category | flops | bytes accessed | tf_op | source)
XLA Modules:
  0.0 104.9 jit_solution(10881493423035271107)
XLA Ops:
  0.0 0.9 fusion.30
  0.9 1.7 %collective-permute-start = (bf16[16,4,256]{2,1,0:T(4,128)(2,1)S(1)}, bf16[16,4,256]{2,1,0:T(4,128)(2,1)S(1)}, u32[]{:S(2)}, u32[]{:S(2)}) collective-permute-start(bf16[16,4,256]{2,1,0:T(4,128)(2,1)S(1)} %get-tuple-element.35), channel_id=1, source_target_pairs={{0,16},{16,32},{32,48},{48,64},{64,80},{80,96},{96,112},{112,128},... | collective-permute-start | bytes 98312 | tf_op jit(solution)/shard_map/ppermute | solution.py:33
  2.7 1.3 %collective-permute-start.1 = (bf16[16,4,256]{2,1,0:T(4,128)(2,1)S(1)}, bf16[16,4,256]{2,1,0:T(4,128)(2,1)S(1)}, u32[]{:S(2)}, u32[]{:S(2)}) collective-permute-start(bf16[16,4,256]{2,1,0:T(4,128)(2,1)S(1)} %get-tuple-element.36), channel_id=1, source_target_pairs={{16,0},{32,16},{48,32},{64,48},{80,64},{96,80},{112,96},{128,112},... | collective-permute-start | bytes 98312 | tf_op jit(solution)/shard_map/ppermute | solution.py:35
  4.0 0.7 convert_bitcast_fusion
  4.7 0.7 bitcast_add_fusion
  5.4 0.7 multiply_add_fusion.3
  6.5 0.8 slice.102
  8.2 1.1 %iota_subtract_fusion = (s32[16,4,1,128,128]{4,3,2,1,0:T(8,128)S(1)}, s32[16,4,1,128,128]{4,3,2,1,0:T(8,128)S(1)}) fusion(s32[16,4,128]{2,1,0:T(4,128)S(1)} %add_multiply_fusion, s32[128]{0:T(128)S(1)} %iota_add_fusion), kind=kLoop, calls=%fused_computation.2 | loop fusion | flops 2097152 | bytes 8421888 | tf_op jit(solution)/shard_map/vmap()/sub | solution.py:279
  10.0 6.7 %select_convert_fusion.mats_ref = bf16[16,4,3,128,128]{4,3,2,1,0:T(8,128)(2,1)} fusion(s32[16,4,1,128,128]{4,3,2,1,0:T(8,128)S(1)} %broadcast_in_dim.10, s32[16,4,1,128,128]{4,3,2,1,0:T(8,128)S(1)} %get-tuple-element.38, s32[16,4,1,128,128]{4,3,2,1,0:T(8,128)S(1)} %get-tuple-element.37, f32[16]{0:T(128)S(1)} %get-tuple-element.42, ...), kind=kLoop, calls=%fused_computation.1 | loop fusion | flops 47185920 | bytes 18907200 | tf_op jit(solution)/shard_map/vmap()/convert_element_type | solution.py:290
  16.7 0.8 convolution_convert_fusion.local_ref
  17.6 25.9 %shard_map.55 = bf16[16,8,4096]{2,1,0:T(8,128)(2,1)} custom-call(bf16[16,8,256]{2,1,0:T(8,128)(2,1)} %convolution_convert_fusion.local_ref), custom_call_target="tpu_custom_call" | custom-call | tf_op jit(solution)/shard_map/pallas_call | solution.py:119
  43.5 2.8 %pad_convert_fusion.tiles_ref = f32[16,35,8,128]{3,2,1,0:T(8,128)} fusion(bf16[16,32,8,128]{3,2,1,0:T(8,128)(2,1)} %bitcast.20), kind=kLoop, calls=%fused_computation.25 | loop fusion | flops 573440 | bytes 3342336 | tf_op jit(solution)/shard_map/jit(_pad)/pad | solution.py:370
  46.3 13.2 %shard_map.56 = f32[4,8,4096]{2,1,0:T(8,128)} custom-call(s32[16,4]{1,0:T(8,128)} %get-tuple-element.40.shift_ref, f32[16,35,8,128]{3,2,1,0:T(8,128)} %pad_convert_fusion.tiles_ref, bf16[16,4,3,128,128]{4,3,2,1,0:T(8,128)(2,1)} %select_convert_fusion.mats_ref), custom_call_target="tpu_custom_call" | custom-call | tf_op jit(solution)/shard_map/pallas_call | solution.py:330
  59.6 1.1 %broadcast_multiply_fusion = f32[4,8,4096]{2,1,0:T(8,128)S(1)} fusion(f32[4,8,4096]{2,1,0:T(8,128)} %shard_map.56), kind=kLoop, calls=%fused_computation.34 | loop fusion | flops 131072 | bytes 1048576 | tf_op jit(solution)/shard_map/mul | solution.py:372
  60.7 0.7 fusion.27
  61.4 0.8 fusion.28
  62.2 0.8 fusion.29
  63.0 30.6 %shard_map.57 = (f32[2,2,4096]{2,1,0:T(2,128)}, f32[2,8,4096]{2,1,0:T(8,128)}, f32[2,2,4096]{2,1,0:T(2,128)}, f32[4,2,4096]{2,1,0:T(2,128)}, f32[4,2,4096]{2,1,0...) custom-call(f32[2,2,4096]{2,1,0:T(2,128)} %get-tuple-element.30.refs_0_, ...), custom_call_target="tpu_custom_call" | custom-call | tf_op jit(solution)/shard_map/pallas_call | solution.py:174
  93.6 1.6 %maximum_maximum_fusion = f32[8,12,4096]{2,1,0:T(8,128)S(1)} fusion(f32[2,2,4096]{2,1,0:T(2,128)} %get-tuple-element.20, f32[2,8,4096]{2,1,0:T(8,128)} %get-tuple-element.19, f32[2,2,4096]{2,1,0:T(2,128)} %get-tuple-element.18, f32[4,2,4096]{2,1,0:T(2,128)} %get-tuple-element.17, f32[4,8,4096]{2,1,0:T(8,128)S(1)} %broadcast_multiply_fusion, ...), kind=kLoop, calls=%fused_computation.5 | loop fusion | flops 3145728 | bytes 3145728 | tf_op jit(solution)/shard_map/concatenate | solution.py:190
  96.2 1.5 %fusion = (f32[8,12,4096]{2,1,0:T(8,128)S(1)}, f32[8,12,4096]{2,1,0:T(8,128)S(1)}, f32[8,12,4096]{2,1,0:T(8,128)S(1)}) fusion(f32[7,12,4096]{2,1,0:T(8,128)S(1)} %slice_subtract_fusion.2, f32[8]{0:T(128)S(1)} %and_convert_fusion.3, f32[8,12,4095]{2,1,0:T(8,128)S(1)} %slice_subtract_fusion, f32[12]{0:T(128)S(1)} %and_convert_fusion.2, ...), kind=kLoop, calls=%fused_computation.11 | loop fusion | flops 4325376 | bytes 9109200 | tf_op jit(solution)/shard_map/div | solution.py:249
  98.0 0.7 copy-done
  98.9 1.9 %multiply_add_fusion = f32[8,12,4096]{2,1,0:T(8,128)S(1)} fusion(f32[8,12,4095]{2,1,0:T(8,128)S(1)} %bitcast.16, f32[8,12,4096]{2,1,0:T(8,128)S(1)} %get-tuple-element.22, f32[8,11,4096]{2,1,0:T(8,128)S(1)} %bitcast.17, f32[8,12,4096]{2,1,0:T(8,128)S(1)} %get-tuple-element.23, f32[8,12,4096]{2,1,0:T(8,128)S(1)} %get-tuple-element.21, ...), kind=kLoop, calls=%fused_computation.6 | loop fusion | flops 7077888 | bytes 12254848 | tf_op jit(solution)/shard_map/add | solution.py:265
  102.1 1.1 %fusion.2 = (f32[6,10,4096]{2,1,0:T(8,128)S(1)}, f32[6,10,4096]{2,1,0:T(8,128)S(1)}, f32[6,10,4096]{2,1,0:T(8,128)S(1)}) fusion(f32[5,10,4096]{2,1,0:T(8,128)S(1)} %slice_subtract_fusion.5, f32[6]{0:T(128)S(1)} %and_convert_fusion.1, f32[6,10,4095]{2,1,0:T(8,128)S(1)} %slice_subtract_fusion.3, f32[10]{0:T(128)S(1)} %and_convert_fusion, ...), kind=kLoop, calls=%fused_computation.21 | loop fusion | flops 2703360 | bytes 5635920 | tf_op jit(solution)/shard_map/div | solution.py:249
  103.7 1.2 %fusion.6 = f32[4,8,4096]{2,1,0:T(8,128)} fusion(f32[6,10,4096]{2,1,0:T(8,128)S(1)} %slice.161, f32[6,10,4096]{2,1,0:T(8,128)S(1)} %slice.151, f32[6,10,4095]{2,1,0:T(8,128)S(1)} %bitcast.19, f32[6,10,4096]{2,1,0:T(8,128)S(1)} %get-tuple-element.25, f32[6,10,4096]{2,1,0:T(8,128)S(1)} %pad_subtract_fusion), kind=kLoop, calls=%fused_computation.30 | loop fusion | flops 917504 | bytes 3604240 | tf_op jit(solution)/shard_map/add | solution.py:265
  (53 shorter events, 5.0 us)
Async XLA Ops:
  0.9 15.7 %collective-permute-start = (bf16[16,4,256]{2,1,0:T(4,128)(2,1)S(1)}, bf16[16,4,256]{2,1,0:T(4,128)(2,1)S(1)}, u32[]{:S(2)}, u32[]{:S(2)}) collective-permute-start(bf16[16,4,256]{2,1,0:T(4,128)(2,1)S(1)} %get-tuple-element.35), channel_id=1, source_target_pairs={{0,16},{16,32},{32,48},{48,64},{64,80},{80,96},{96,112},{112,128},... | collective-permute-start | bytes 98312 | tf_op jit(solution)/shard_map/ppermute | solution.py:33
  2.7 14.0 %collective-permute-start.1 = (bf16[16,4,256]{2,1,0:T(4,128)(2,1)S(1)}, bf16[16,4,256]{2,1,0:T(4,128)(2,1)S(1)}, u32[]{:S(2)}, u32[]{:S(2)}) collective-permute-start(bf16[16,4,256]{2,1,0:T(4,128)(2,1)S(1)} %get-tuple-element.36), channel_id=1, source_target_pairs={{16,0},{32,16},{48,32},{64,48},{80,64},{96,80},{112,96},{128,112},... | collective-permute-start | bytes 98312 | tf_op jit(solution)/shard_map/ppermute | solution.py:35
  8.2 1.1 %copy-start.9 = (s32[16,1]{0,1:T(1,128)S(1)}, s32[16,1]{0,1:T(1,128)}, u32[]{:S(2)}) copy-start(s32[16,1]{0,1:T(1,128)} %param.7) | copy-start | bytes 196
  10.0 6.7 %copy-start.8 = (bf16[16,8,256]{2,1,0:T(8,128)(2,1)S(1)}, bf16[16,8,256]{2,1,0:T(8,128)(2,1)}, u32[]{:S(2)}) copy-start(bf16[16,8,256]{2,1,0:T(8,128)(2,1)} %param.5) | copy-start | bytes 196612
  97.8 1.0 copy-start
  97.8 1.0 copy-start.1
  97.8 1.0 copy-start.2
  97.8 1.1 %copy-start.3 = (f32[4,2,4096]{2,1,0:T(2,128)S(1)}, f32[4,2,4096]{2,1,0:T(2,128)}, u32[]{:S(2)}) copy-start(f32[4,2,4096]{2,1,0:T(2,128)} %get-tuple-element.17) | copy-start | bytes 393220
  97.8 1.1 %copy-start.4 = (f32[2,2,4096]{2,1,0:T(2,128)S(1)}, f32[2,2,4096]{2,1,0:T(2,128)}, u32[]{:S(2)}) copy-start(f32[2,2,4096]{2,1,0:T(2,128)} %get-tuple-element.13) | copy-start | bytes 196612
  97.8 1.1 %copy-start.5 = (f32[2,2,4096]{2,1,0:T(2,128)S(1)}, f32[2,2,4096]{2,1,0:T(2,128)}, u32[]{:S(2)}) copy-start(f32[2,2,4096]{2,1,0:T(2,128)} %get-tuple-element.15) | copy-start | bytes 196612
  97.8 1.1 %copy-start.6 = (f32[2,2,4096]{2,1,0:T(2,128)S(1)}, f32[2,2,4096]{2,1,0:T(2,128)}, u32[]{:S(2)}) copy-start(f32[2,2,4096]{2,1,0:T(2,128)} %get-tuple-element.18) | copy-start | bytes 196612
  97.8 1.1 %copy-start.7 = (f32[2,2,4096]{2,1,0:T(2,128)S(1)}, f32[2,2,4096]{2,1,0:T(2,128)}, u32[]{:S(2)}) copy-start(f32[2,2,4096]{2,1,0:T(2,128)} %get-tuple-element.20) | copy-start | bytes 196612

commit v7 on v6

--- a/solution.py
+++ b/solution.py
@@ -265,29 +265,17 @@
     return current + step_length * (smooth_weight * divergence - (current - fidelity))
 
 
-def footprint_mats(angle_value, shift, row_global, rows_total):
+def footprint_mats(angle_value, row_global, rows_total):
     radians, stretch, spread = geometry(angle_value)
     shifted = shift_reach * jnp.sin(radians + 2.0 * math.pi * row_global / rows_total)
     inside = jnp.arange(BLOCK).astype(jnp.float32) - 0.5 * (BLOCK - 1)
     centre = BLOCK + inside[None, :] * stretch + shifted[:, None]
     centre = jnp.concatenate([centre, centre], axis=1)
-    parity = shift - 2 * ((shift + 2) // 2 - 1)
-    half = (jnp.arange(LANES) >= BLOCK).astype(jnp.int32)
-    place = jnp.arange(LANES)[:, None]
-    taps = jnp.stack(
-        [
-            place - BLOCK * (half[None, None, :] + parity[:, None, None]),
-            place + LANES - BLOCK * (half[None, None, :] + parity[:, None, None]),
-            jnp.broadcast_to(place, (LANES, LANES))[None].repeat(shift.shape[0], 0),
-        ],
-        axis=1,
-    )
-    places = taps.astype(jnp.float32) + 0.5
+    places = jnp.arange(LANES).astype(jnp.float32)[:, None] + 0.5
     weights = (
-        jnp.maximum(0.0, 1.0 - jnp.abs(places - centre[:, None, None, :]) / spread) / spread
-    )
-    valid = (taps >= 0) & (taps < 2 * BLOCK)
-    return jnp.where(valid, weights, 0.0).astype(jnp.bfloat16)
+        jnp.maximum(0.0, 1.0 - jnp.abs(places[None] - centre[:, None, :]) / spread) / spread
+    )
+    return weights.astype(jnp.bfloat16)
 
 
 def backproject_kernel(shift_ref, tiles_ref, mats_ref, out_ref):
@@ -300,17 +288,29 @@
         out_ref[...] = jnp.zeros_like(out_ref)
 
     ends = jnp.concatenate([tiles_ref[0, 1], tiles_ref[0, tile_count]], axis=0).astype(jnp.bfloat16)
+    second_half = lax.broadcasted_iota(jnp.int32, (LANES, LANES), 1) >= BLOCK
+    empty = jnp.zeros((BLOCK, LANES), jnp.bfloat16)
     for row in range(out_ref.shape[0]):
         shift = shift_ref[p, row]
         start = (shift + 2) // 2
+        odd = jnp.full((LANES, LANES), shift - 2 * (start - 1), jnp.int32) == 1
+        whole = mats_ref[0, row]
+        down = jnp.concatenate([empty, whole[:BLOCK]], axis=0)
+        up = jnp.concatenate([whole[BLOCK:], empty], axis=0)
+        nothing = jnp.zeros_like(whole)
+        first = jnp.where(
+            second_half, jnp.where(odd, nothing, down), jnp.where(odd, down, whole)
+        )
+        second = jnp.where(
+            second_half, jnp.where(odd, whole, up), jnp.where(odd, up, nothing)
+        )
         low = tiles_ref[0, pl.ds(start, tile_count)].reshape(tile_count * depth_count, LANES)
         high = tiles_ref[0, pl.ds(start + 1, tile_count)].reshape(tile_count * depth_count, LANES)
+        taps = jnp.concatenate([low, high], axis=1).astype(jnp.bfloat16)
         result = jnp.dot(
-            low.astype(jnp.bfloat16), mats_ref[0, row, 0], preferred_element_type=jnp.float32
-        ) + jnp.dot(
-            high.astype(jnp.bfloat16), mats_ref[0, row, 1], preferred_element_type=jnp.float32
-        )
-        edge = jnp.dot(ends, mats_ref[0, row, 2], preferred_element_type=jnp.float32)
+            taps, jnp.concatenate([first, second], axis=0), preferred_element_type=jnp.float32
+        )
+        edge = jnp.dot(ends, whole, preferred_element_type=jnp.float32)
         shift_vec = jnp.full((depth_count, LANES), shift, jnp.int32)
         for tile in range(tile_count):
             part = result[tile * depth_count:(tile + 1) * depth_count]
@@ -335,7 +335,7 @@
             grid=(count,),
             in_specs=[
                 pl.BlockSpec((1,) + tiles.shape[1:], lambda p, s: (p, 0, 0, 0)),
-                pl.BlockSpec((1,) + mats.shape[1:], lambda p, s: (p, 0, 0, 0, 0)),
+                pl.BlockSpec((1,) + mats.shape[1:], lambda p, s: (p, 0, 0, 0)),
             ],
             out_specs=pl.BlockSpec((rows, depth_count, column_count), lambda p, s: (0, 0, 0)),
         ),
@@ -362,9 +362,7 @@
     depth_total = lax.axis_size("gz") * depth_count
     row_global = (row_base + jnp.arange(row_count)).astype(jnp.float32)
     shifts = foot_block[:, :, 2] - 2
-    mats = jax.vmap(footprint_mats, in_axes=(0, 0, None, None))(
-        angle_index, shifts, row_global, rows_total
-    )
+    mats = jax.vmap(footprint_mats, in_axes=(0, None, None))(angle_index, row_global, rows_total)
     tile_count = column_count // LANES
     tiles = columns.astype(jnp.float32).reshape(P_SIZE, depth_count, tile_count, LANES)
     tiles = jnp.pad(tiles.transpose(0, 2, 1, 3), ((0, 0), (1, 2), (0, 0), (0, 0)))

time: 106 us -> 99.8 us (0.942)
  other arithmetic: 24.6 us -> 19.2 us
    convert_element_type x2 -> x1, other arithmetic: 6.67 us -> 2.34 us  [footprint_mats(): return weights.astype(jnp.bfloat16)]
    sub x2 -> x1, other arithmetic: 1.69 us -> 0.01 us  [per_device(): shifts = foot_block[:, :, 2] - 2]
  transfers between devices with their start and end apart: 2 -> 2, of which waited for: 0 -> 0; matrix products, arithmetic and copies ran while one was open for 12% -> 7% of each run, Pallas kernels for 0% -> 0%
where the time goes in v7:
time: 99.8 us; the launch traced here: 99.1 us
  Pallas kernels  69.3 us (69%)
  other arithmetic  19.2 us (19%)
  local copies, waits for them, and re-layouts  6.39 us (6%)
  starting transfers between devices  3.03 us (3%)
    pallas_call x1, Pallas kernels, with_wide_halo(): pl.pallas_call(functools.partial(halo_kernel, count), out_shape=[jax.Shap...  30.6 us
    pallas_call x1, Pallas kernels, gather_columns(): pl.pallas_call(functools.partial(gather_kernel, count), out_shape=jax.Sha...  25.9 us
    pallas_call x1, Pallas kernels, backproject(): pl.pallas_call(backproject_kernel, out_shape=jax.ShapeDtypeStruct((rows,...  12.8 us
    add x2, other arithmetic, smooth_update(): current + step_length * (smooth_weight * divergence - (current - fidelity))  3.13 us
    pad x1, other arithmetic, per_device(): jnp.pad(tiles.transpose(0, 2, 1, 3), ((0, 0), (1, 2), (0, 0), (0, 0)))  2.78 us
    div x2, other arithmetic, smooth_update(): normal_rows = forward_rows / magnitude  2.65 us
    slice x3, local copies, waits for them, and re-layouts, with_wide_halo(): sent = [cells[row_parts[r], depth_parts[d]] for r, d in STEPS]  2.35 us
    convert_element_type x1, other arithmetic, footprint_mats(): return weights.astype(jnp.bfloat16)  2.34 us
  transfers between devices with their start and end apart: 2, of which 0 were waited for; matrix products, arithmetic and copies ran while one was open for 7% of the time, Pallas kernels for 0%

profile of v7, /device:TPU:56, one launch (start us, length us, event | category | flops | bytes accessed | tf_op | source)
XLA Modules:
  0.0 99.1 jit_solution(7376651211004979673)
XLA Ops:
  0.0 1.0 fusion.25
  1.0 1.7 %collective-permute-start = (bf16[16,4,256]{2,1,0:T(4,128)(2,1)S(1)}, bf16[16,4,256]{2,1,0:T(4,128)(2,1)S(1)}, u32[]{:S(2)}, u32[]{:S(2)}) collective-permute-start(bf16[16,4,256]{2,1,0:T(4,128)(2,1)S(1)} %get-tuple-element.35), channel_id=1, source_target_pairs={{0,16},{16,32},{32,48},{48,64},{64,80},{80,96},{96,112},{112,128},... | collective-permute-start | bytes 98312 | tf_op jit(solution)/shard_map/ppermute | solution.py:33
  2.7 1.3 %collective-permute-start.1 = (bf16[16,4,256]{2,1,0:T(4,128)(2,1)S(1)}, bf16[16,4,256]{2,1,0:T(4,128)(2,1)S(1)}, u32[]{:S(2)}, u32[]{:S(2)}) collective-permute-start(bf16[16,4,256]{2,1,0:T(4,128)(2,1)S(1)} %get-tuple-element.36), channel_id=1, source_target_pairs={{16,0},{32,16},{48,32},{64,48},{80,64},{96,80},{112,96},{128,112},... | collective-permute-start | bytes 98312 | tf_op jit(solution)/shard_map/ppermute | solution.py:35
  4.1 0.7 bitcast_add_fusion
  4.8 0.7 convert_bitcast_fusion
  5.5 0.7 multiply_add_fusion.3
  6.6 0.8 slice.102
  7.5 0.7 fusion.18
  8.3 2.3 %divide_convert_fusion.mats_ref = bf16[16,4,128,128]{3,2,1,0:T(8,128)(2,1)} fusion(f32[16]{0:T(128)S(1)} %get-tuple-element.38, f32[16,4,128]{2,1,0:T(4,128)S(1)} %pad_maximum_fusion, f32[128]{0:T(128)S(1)} %convert_add_fusion.1), kind=kLoop, calls=%fused_computation | loop fusion | flops 7340032 | bytes 2130496 | tf_op jit(solution)/shard_map/vmap()/convert_element_type | solution.py:278
  11.3 0.8 convolution_convert_fusion.local_ref
  12.2 25.9 %shard_map.55 = bf16[16,8,4096]{2,1,0:T(8,128)(2,1)} custom-call(bf16[16,8,256]{2,1,0:T(8,128)(2,1)} %convolution_convert_fusion.local_ref), custom_call_target="tpu_custom_call" | custom-call | tf_op jit(solution)/shard_map/pallas_call | solution.py:119
  38.1 2.8 %pad_convert_fusion.tiles_ref = f32[16,35,8,128]{3,2,1,0:T(8,128)} fusion(bf16[16,32,8,128]{3,2,1,0:T(8,128)(2,1)} %bitcast.21), kind=kLoop, calls=%fused_computation.22 | loop fusion | flops 573440 | bytes 3342336 | tf_op jit(solution)/shard_map/jit(_pad)/pad | solution.py:368
  40.9 12.8 %shard_map.56 = f32[4,8,4096]{2,1,0:T(8,128)} custom-call(s32[16,4]{1,0:T(8,128)} %copy.9.shift_ref, f32[16,35,8,128]{3,2,1,0:T(8,128)} %pad_convert_fusion.tiles_ref, bf16[16,4,128,128]{3,2,1,0:T(8,128)(2,1)} %divide_convert_fusion.mats_ref), custom_call_target="tpu_custom_call" | custom-call | tf_op jit(solution)/shard_map/pallas_call | solution.py:330
  53.7 1.1 %broadcast_multiply_fusion = f32[4,8,4096]{2,1,0:T(8,128)S(1)} fusion(f32[4,8,4096]{2,1,0:T(8,128)} %shard_map.56), kind=kLoop, calls=%fused_computation.31 | loop fusion | flops 131072 | bytes 1048576 | tf_op jit(solution)/shard_map/mul | solution.py:370
  54.8 0.8 fusion.22
  55.6 0.8 fusion.24
  56.4 0.8 fusion.23
  57.2 30.6 %shard_map.57 = (f32[2,2,4096]{2,1,0:T(2,128)}, f32[2,8,4096]{2,1,0:T(8,128)}, f32[2,2,4096]{2,1,0:T(2,128)}, f32[4,2,4096]{2,1,0:T(2,128)}, f32[4,2,4096]{2,1,0...) custom-call(f32[2,2,4096]{2,1,0:T(2,128)} %get-tuple-element.30.refs_0_, ...), custom_call_target="tpu_custom_call" | custom-call | tf_op jit(solution)/shard_map/pallas_call | solution.py:174
  87.8 1.6 %maximum_maximum_fusion = f32[8,12,4096]{2,1,0:T(8,128)S(1)} fusion(f32[2,2,4096]{2,1,0:T(2,128)} %get-tuple-element.20, f32[2,8,4096]{2,1,0:T(8,128)} %get-tuple-element.19, f32[2,2,4096]{2,1,0:T(2,128)} %get-tuple-element.18, f32[4,2,4096]{2,1,0:T(2,128)} %get-tuple-element.17, f32[4,8,4096]{2,1,0:T(8,128)S(1)} %broadcast_multiply_fusion, ...), kind=kLoop, calls=%fused_computation.3 | loop fusion | flops 3145728 | bytes 3145728 | tf_op jit(solution)/shard_map/concatenate | solution.py:190
  90.5 1.5 %fusion = (f32[8,12,4096]{2,1,0:T(8,128)S(1)}, f32[8,12,4096]{2,1,0:T(8,128)S(1)}, f32[8,12,4096]{2,1,0:T(8,128)S(1)}) fusion(f32[7,12,4096]{2,1,0:T(8,128)S(1)} %slice_subtract_fusion.2, f32[8]{0:T(128)S(1)} %and_convert_fusion.3, f32[8,12,4095]{2,1,0:T(8,128)S(1)} %slice_subtract_fusion, f32[12]{0:T(128)S(1)} %and_convert_fusion.2, ...), kind=kLoop, calls=%fused_computation.8 | loop fusion | flops 4325376 | bytes 9109200 | tf_op jit(solution)/shard_map/div | solution.py:249
  92.3 0.7 copy-done
  93.2 1.9 %multiply_add_fusion = f32[8,12,4096]{2,1,0:T(8,128)S(1)} fusion(f32[8,12,4095]{2,1,0:T(8,128)S(1)} %bitcast.17, f32[8,12,4096]{2,1,0:T(8,128)S(1)} %get-tuple-element.22, f32[8,11,4096]{2,1,0:T(8,128)S(1)} %bitcast.18, f32[8,12,4096]{2,1,0:T(8,128)S(1)} %get-tuple-element.23, f32[8,12,4096]{2,1,0:T(8,128)S(1)} %get-tuple-element.21, ...), kind=kLoop, calls=%fused_computation.4 | loop fusion | flops 7077888 | bytes 12254848 | tf_op jit(solution)/shard_map/add | solution.py:265
  96.2 1.1 %fusion.2 = (f32[6,10,4096]{2,1,0:T(8,128)S(1)}, f32[6,10,4096]{2,1,0:T(8,128)S(1)}, f32[6,10,4096]{2,1,0:T(8,128)S(1)}) fusion(f32[5,10,4096]{2,1,0:T(8,128)S(1)} %slice_subtract_fusion.5, f32[6]{0:T(128)S(1)} %and_convert_fusion.1, f32[6,10,4095]{2,1,0:T(8,128)S(1)} %slice_subtract_fusion.3, f32[10]{0:T(128)S(1)} %and_convert_fusion, ...), kind=kLoop, calls=%fused_computation.18 | loop fusion | flops 2703360 | bytes 5635920 | tf_op jit(solution)/shard_map/div | solution.py:249
  97.8 1.2 %fusion.6 = f32[4,8,4096]{2,1,0:T(8,128)} fusion(f32[6,10,4096]{2,1,0:T(8,128)S(1)} %slice.161, f32[6,10,4096]{2,1,0:T(8,128)S(1)} %slice.151, f32[6,10,4095]{2,1,0:T(8,128)S(1)} %bitcast.20, f32[6,10,4096]{2,1,0:T(8,128)S(1)} %get-tuple-element.25, f32[6,10,4096]{2,1,0:T(8,128)S(1)} %pad_subtract_fusion), kind=kLoop, calls=%fused_computation.27 | loop fusion | flops 917504 | bytes 3604240 | tf_op jit(solution)/shard_map/add | solution.py:265
  (47 shorter events, 4.3 us)
Async XLA Ops:
  0.0 11.3 %copy-start.8 = (bf16[16,8,256]{2,1,0:T(8,128)(2,1)S(1)}, bf16[16,8,256]{2,1,0:T(8,128)(2,1)}, u32[]{:S(2)}) copy-start(bf16[16,8,256]{2,1,0:T(8,128)(2,1)} %param.5) | copy-start | bytes 196612
  1.0 10.4 %collective-permute-start = (bf16[16,4,256]{2,1,0:T(4,128)(2,1)S(1)}, bf16[16,4,256]{2,1,0:T(4,128)(2,1)S(1)}, u32[]{:S(2)}, u32[]{:S(2)}) collective-permute-start(bf16[16,4,256]{2,1,0:T(4,128)(2,1)S(1)} %get-tuple-element.35), channel_id=1, source_target_pairs={{0,16},{16,32},{32,48},{48,64},{64,80},{80,96},{96,112},{112,128},... | collective-permute-start | bytes 98312 | tf_op jit(solution)/shard_map/ppermute | solution.py:33
  2.7 8.6 %collective-permute-start.1 = (bf16[16,4,256]{2,1,0:T(4,128)(2,1)S(1)}, bf16[16,4,256]{2,1,0:T(4,128)(2,1)S(1)}, u32[]{:S(2)}, u32[]{:S(2)}) collective-permute-start(bf16[16,4,256]{2,1,0:T(4,128)(2,1)S(1)} %get-tuple-element.36), channel_id=1, source_target_pairs={{16,0},{32,16},{48,32},{64,48},{80,64},{96,80},{112,96},{128,112},... | collective-permute-start | bytes 98312 | tf_op jit(solution)/shard_map/ppermute | solution.py:35
  92.1 1.0 copy-start
  92.1 1.0 %copy-start.1 = (f32[2,8,4096]{2,1,0:T(8,128)S(1)}, f32[2,8,4096]{2,1,0:T(8,128)}, u32[]{:S(2)}) copy-start(f32[2,8,4096]{2,1,0:T(8,128)} %get-tuple-element.19) | copy-start | bytes 786436
  92.1 1.0 %copy-start.2 = (f32[4,2,4096]{2,1,0:T(2,128)S(1)}, f32[4,2,4096]{2,1,0:T(2,128)}, u32[]{:S(2)}) copy-start(f32[4,2,4096]{2,1,0:T(2,128)} %get-tuple-element.16) | copy-start | bytes 393220
  92.1 1.1 %copy-start.3 = (f32[4,2,4096]{2,1,0:T(2,128)S(1)}, f32[4,2,4096]{2,1,0:T(2,128)}, u32[]{:S(2)}) copy-start(f32[4,2,4096]{2,1,0:T(2,128)} %get-tuple-element.17) | copy-start | bytes 393220
  92.1 1.1 %copy-start.4 = (f32[2,2,4096]{2,1,0:T(2,128)S(1)}, f32[2,2,4096]{2,1,0:T(2,128)}, u32[]{:S(2)}) copy-start(f32[2,2,4096]{2,1,0:T(2,128)} %get-tuple-element.13) | copy-start | bytes 196612
  92.1 1.1 %copy-start.5 = (f32[2,2,4096]{2,1,0:T(2,128)S(1)}, f32[2,2,4096]{2,1,0:T(2,128)}, u32[]{:S(2)}) copy-start(f32[2,2,4096]{2,1,0:T(2,128)} %get-tuple-element.15) | copy-start | bytes 196612
  92.1 1.1 %copy-start.6 = (f32[2,2,4096]{2,1,0:T(2,128)S(1)}, f32[2,2,4096]{2,1,0:T(2,128)}, u32[]{:S(2)}) copy-start(f32[2,2,4096]{2,1,0:T(2,128)} %get-tuple-element.18) | copy-start | bytes 196612
  92.1 1.1 %copy-start.7 = (f32[2,2,4096]{2,1,0:T(2,128)S(1)}, f32[2,2,4096]{2,1,0:T(2,128)}, u32[]{:S(2)}) copy-start(f32[2,2,4096]{2,1,0:T(2,128)} %get-tuple-element.20) | copy-start | bytes 196612

commit v8 on v7

--- a/solution.py
+++ b/solution.py
@@ -240,15 +240,15 @@
     forward_width = jnp.concatenate(
         [current[:, :, 1:] - current[:, :, :-1], jnp.zeros_like(current[:, :, :1])], 2
     )
-    magnitude = jnp.sqrt(
+    inverse = lax.rsqrt(
         forward_rows * forward_rows
         + forward_depth * forward_depth
         + forward_width * forward_width
         + gradient_floor
     )
-    normal_rows = forward_rows / magnitude
-    normal_depth = forward_depth / magnitude
-    normal_width = forward_width / magnitude
+    normal_rows = forward_rows * inverse
+    normal_depth = forward_depth * inverse
+    normal_width = forward_width * inverse
     divergence = normal_rows - jnp.concatenate(
         [jnp.zeros_like(normal_rows[:1]), normal_rows[:-1]], 0
     )

time: 99.8 us -> 99.2 us (level)
    div x2 -> x0, other arithmetic: 2.65 us -> none  [smooth_update(): normal_rows = forward_rows / magnitude]
    mul x0 -> x2, other arithmetic: none -> 2.02 us  [smooth_update(): normal_rows = forward_rows * inverse]
where the time goes in v8:
time: 99.2 us; the launch traced here: 98.5 us
  Pallas kernels  69.3 us (70%)
  other arithmetic  18.5 us (19%)
  local copies, waits for them, and re-layouts  6.39 us (6%)
  starting transfers between devices  3.03 us (3%)
    pallas_call x1, Pallas kernels, with_wide_halo(): pl.pallas_call(functools.partial(halo_kernel, count), out_shape=[jax.Shap...  30.6 us
    pallas_call x1, Pallas kernels, gather_columns(): pl.pallas_call(functools.partial(gather_kernel, count), out_shape=jax.Sha...  25.9 us
    pallas_call x1, Pallas kernels, backproject(): pl.pallas_call(backproject_kernel, out_shape=jax.ShapeDtypeStruct((rows,...  12.8 us
    add x2, other arithmetic, smooth_update(): current + step_length * (smooth_weight * divergence - (current - fidelity))  3.13 us
    pad x1, other arithmetic, per_device(): jnp.pad(tiles.transpose(0, 2, 1, 3), ((0, 0), (1, 2), (0, 0), (0, 0)))  2.78 us
    slice x3, local copies, waits for them, and re-layouts, with_wide_halo(): sent = [cells[row_parts[r], depth_parts[d]] for r, d in STEPS]  2.35 us
    convert_element_type x1, other arithmetic, footprint_mats(): return weights.astype(jnp.bfloat16)  2.34 us
    mul x2, other arithmetic, smooth_update(): normal_rows = forward_rows * inverse  2.02 us
  transfers between devices with their start and end apart: 2, of which 0 were waited for; matrix products, arithmetic and copies ran while one was open for 7% of the time, Pallas kernels for 0%

profile of v8, /device:TPU:56, one launch (start us, length us, event | category | flops | bytes accessed | tf_op | source)
XLA Modules:
  0.0 98.5 jit_solution(8732813349923886677)
XLA Ops:
  0.0 1.0 fusion.25
  1.0 1.7 %collective-permute-start = (bf16[16,4,256]{2,1,0:T(4,128)(2,1)S(1)}, bf16[16,4,256]{2,1,0:T(4,128)(2,1)S(1)}, u32[]{:S(2)}, u32[]{:S(2)}) collective-permute-start(bf16[16,4,256]{2,1,0:T(4,128)(2,1)S(1)} %get-tuple-element.35), channel_id=1, source_target_pairs={{0,16},{16,32},{32,48},{48,64},{64,80},{80,96},{96,112},{112,128},... | collective-permute-start | bytes 98312 | tf_op jit(solution)/shard_map/ppermute | solution.py:33
  2.7 1.3 %collective-permute-start.1 = (bf16[16,4,256]{2,1,0:T(4,128)(2,1)S(1)}, bf16[16,4,256]{2,1,0:T(4,128)(2,1)S(1)}, u32[]{:S(2)}, u32[]{:S(2)}) collective-permute-start(bf16[16,4,256]{2,1,0:T(4,128)(2,1)S(1)} %get-tuple-element.36), channel_id=1, source_target_pairs={{16,0},{32,16},{48,32},{64,48},{80,64},{96,80},{112,96},{128,112},... | collective-permute-start | bytes 98312 | tf_op jit(solution)/shard_map/ppermute | solution.py:35
  4.1 0.7 bitcast_add_fusion
  4.8 0.7 convert_bitcast_fusion
  5.5 0.7 multiply_add_fusion.3
  6.6 0.8 slice.102
  7.5 0.7 fusion.18
  8.3 2.3 %divide_convert_fusion.mats_ref = bf16[16,4,128,128]{3,2,1,0:T(8,128)(2,1)} fusion(f32[16]{0:T(128)S(1)} %get-tuple-element.38, f32[16,4,128]{2,1,0:T(4,128)S(1)} %pad_maximum_fusion, f32[128]{0:T(128)S(1)} %convert_add_fusion.1), kind=kLoop, calls=%fused_computation | loop fusion | flops 7340032 | bytes 2130496 | tf_op jit(solution)/shard_map/vmap()/convert_element_type | solution.py:278
  11.3 0.8 convolution_convert_fusion.local_ref
  12.2 25.9 %shard_map.55 = bf16[16,8,4096]{2,1,0:T(8,128)(2,1)} custom-call(bf16[16,8,256]{2,1,0:T(8,128)(2,1)} %convolution_convert_fusion.local_ref), custom_call_target="tpu_custom_call" | custom-call | tf_op jit(solution)/shard_map/pallas_call | solution.py:119
  38.1 2.8 %pad_convert_fusion.tiles_ref = f32[16,35,8,128]{3,2,1,0:T(8,128)} fusion(bf16[16,32,8,128]{3,2,1,0:T(8,128)(2,1)} %bitcast.21), kind=kLoop, calls=%fused_computation.22 | loop fusion | flops 573440 | bytes 3342336 | tf_op jit(solution)/shard_map/jit(_pad)/pad | solution.py:368
  40.9 12.8 %shard_map.56 = f32[4,8,4096]{2,1,0:T(8,128)} custom-call(s32[16,4]{1,0:T(8,128)} %copy.9.shift_ref, f32[16,35,8,128]{3,2,1,0:T(8,128)} %pad_convert_fusion.tiles_ref, bf16[16,4,128,128]{3,2,1,0:T(8,128)(2,1)} %divide_convert_fusion.mats_ref), custom_call_target="tpu_custom_call" | custom-call | tf_op jit(solution)/shard_map/pallas_call | solution.py:330
  53.8 1.1 %broadcast_multiply_fusion = f32[4,8,4096]{2,1,0:T(8,128)S(1)} fusion(f32[4,8,4096]{2,1,0:T(8,128)} %shard_map.56), kind=kLoop, calls=%fused_computation.31 | loop fusion | flops 131072 | bytes 1048576 | tf_op jit(solution)/shard_map/mul | solution.py:370
  54.8 0.8 fusion.22
  55.6 0.8 fusion.24
  56.4 0.8 fusion.23
  57.2 30.6 %shard_map.57 = (f32[2,2,4096]{2,1,0:T(2,128)}, f32[2,8,4096]{2,1,0:T(8,128)}, f32[2,2,4096]{2,1,0:T(2,128)}, f32[4,2,4096]{2,1,0:T(2,128)}, f32[4,2,4096]{2,1,0...) custom-call(f32[2,2,4096]{2,1,0:T(2,128)} %get-tuple-element.30.refs_0_, ...), custom_call_target="tpu_custom_call" | custom-call | tf_op jit(solution)/shard_map/pallas_call | solution.py:174
  87.8 1.6 %maximum_maximum_fusion = f32[8,12,4096]{2,1,0:T(8,128)S(1)} fusion(f32[2,2,4096]{2,1,0:T(2,128)} %get-tuple-element.20, f32[2,8,4096]{2,1,0:T(8,128)} %get-tuple-element.19, f32[2,2,4096]{2,1,0:T(2,128)} %get-tuple-element.18, f32[4,2,4096]{2,1,0:T(2,128)} %get-tuple-element.17, f32[4,8,4096]{2,1,0:T(8,128)S(1)} %broadcast_multiply_fusion, ...), kind=kLoop, calls=%fused_computation.3 | loop fusion | flops 3145728 | bytes 3145728 | tf_op jit(solution)/shard_map/concatenate | solution.py:190
  90.6 1.2 %fusion = (f32[8,12,4096]{2,1,0:T(8,128)S(1)}, f32[8,12,4096]{2,1,0:T(8,128)S(1)}, f32[8,12,4096]{2,1,0:T(8,128)S(1)}) fusion(f32[7,12,4096]{2,1,0:T(8,128)S(1)} %slice_subtract_fusion.2, f32[8]{0:T(128)S(1)} %and_convert_fusion.3, f32[8,12,4095]{2,1,0:T(8,128)S(1)} %slice_subtract_fusion, f32[12]{0:T(128)S(1)} %and_convert_fusion.2, ...), kind=kLoop, calls=%fused_computation.8 | loop fusion | flops 4325376 | bytes 9109200 | tf_op jit(solution)/shard_map/mul | solution.py:249
  92.0 0.7 copy-done
  92.9 1.9 %multiply_add_fusion = f32[8,12,4096]{2,1,0:T(8,128)S(1)} fusion(f32[8,12,4095]{2,1,0:T(8,128)S(1)} %bitcast.17, f32[8,12,4096]{2,1,0:T(8,128)S(1)} %get-tuple-element.22, f32[8,11,4096]{2,1,0:T(8,128)S(1)} %bitcast.18, f32[8,12,4096]{2,1,0:T(8,128)S(1)} %get-tuple-element.23, f32[8,12,4096]{2,1,0:T(8,128)S(1)} %get-tuple-element.21, ...), kind=kLoop, calls=%fused_computation.4 | loop fusion | flops 7077888 | bytes 12254848 | tf_op jit(solution)/shard_map/add | solution.py:265
  95.9 0.8 fusion.2
  97.2 1.2 %fusion.6 = f32[4,8,4096]{2,1,0:T(8,128)} fusion(f32[6,10,4096]{2,1,0:T(8,128)S(1)} %slice.161, f32[6,10,4096]{2,1,0:T(8,128)S(1)} %slice.151, f32[6,10,4095]{2,1,0:T(8,128)S(1)} %bitcast.20, f32[6,10,4096]{2,1,0:T(8,128)S(1)} %get-tuple-element.25, f32[6,10,4096]{2,1,0:T(8,128)S(1)} %pad_subtract_fusion), kind=kLoop, calls=%fused_computation.27 | loop fusion | flops 917504 | bytes 3604240 | tf_op jit(solution)/shard_map/add | solution.py:265
  (47 shorter events, 4.3 us)
Async XLA Ops:
  0.0 11.3 %copy-start.8 = (bf16[16,8,256]{2,1,0:T(8,128)(2,1)S(1)}, bf16[16,8,256]{2,1,0:T(8,128)(2,1)}, u32[]{:S(2)}) copy-start(bf16[16,8,256]{2,1,0:T(8,128)(2,1)} %param.5) | copy-start | bytes 196612
  1.0 10.4 %collective-permute-start = (bf16[16,4,256]{2,1,0:T(4,128)(2,1)S(1)}, bf16[16,4,256]{2,1,0:T(4,128)(2,1)S(1)}, u32[]{:S(2)}, u32[]{:S(2)}) collective-permute-start(bf16[16,4,256]{2,1,0:T(4,128)(2,1)S(1)} %get-tuple-element.35), channel_id=1, source_target_pairs={{0,16},{16,32},{32,48},{48,64},{64,80},{80,96},{96,112},{112,128},... | collective-permute-start | bytes 98312 | tf_op jit(solution)/shard_map/ppermute | solution.py:33
  2.7 8.6 %collective-permute-start.1 = (bf16[16,4,256]{2,1,0:T(4,128)(2,1)S(1)}, bf16[16,4,256]{2,1,0:T(4,128)(2,1)S(1)}, u32[]{:S(2)}, u32[]{:S(2)}) collective-permute-start(bf16[16,4,256]{2,1,0:T(4,128)(2,1)S(1)} %get-tuple-element.36), channel_id=1, source_target_pairs={{16,0},{32,16},{48,32},{64,48},{80,64},{96,80},{112,96},{128,112},... | collective-permute-start | bytes 98312 | tf_op jit(solution)/shard_map/ppermute | solution.py:35
  91.8 1.0 copy-start
  91.8 1.0 %copy-start.1 = (f32[2,8,4096]{2,1,0:T(8,128)S(1)}, f32[2,8,4096]{2,1,0:T(8,128)}, u32[]{:S(2)}) copy-start(f32[2,8,4096]{2,1,0:T(8,128)} %get-tuple-element.19) | copy-start | bytes 786436
  91.8 1.0 %copy-start.2 = (f32[4,2,4096]{2,1,0:T(2,128)S(1)}, f32[4,2,4096]{2,1,0:T(2,128)}, u32[]{:S(2)}) copy-start(f32[4,2,4096]{2,1,0:T(2,128)} %get-tuple-element.16) | copy-start | bytes 393220
  91.8 1.1 %copy-start.3 = (f32[4,2,4096]{2,1,0:T(2,128)S(1)}, f32[4,2,4096]{2,1,0:T(2,128)}, u32[]{:S(2)}) copy-start(f32[4,2,4096]{2,1,0:T(2,128)} %get-tuple-element.17) | copy-start | bytes 393220
  91.8 1.1 %copy-start.4 = (f32[2,2,4096]{2,1,0:T(2,128)S(1)}, f32[2,2,4096]{2,1,0:T(2,128)}, u32[]{:S(2)}) copy-start(f32[2,2,4096]{2,1,0:T(2,128)} %get-tuple-element.13) | copy-start | bytes 196612
  91.8 1.1 %copy-start.5 = (f32[2,2,4096]{2,1,0:T(2,128)S(1)}, f32[2,2,4096]{2,1,0:T(2,128)}, u32[]{:S(2)}) copy-start(f32[2,2,4096]{2,1,0:T(2,128)} %get-tuple-element.15) | copy-start | bytes 196612
  91.8 1.1 %copy-start.6 = (f32[2,2,4096]{2,1,0:T(2,128)S(1)}, f32[2,2,4096]{2,1,0:T(2,128)}, u32[]{:S(2)}) copy-start(f32[2,2,4096]{2,1,0:T(2,128)} %get-tuple-element.18) | copy-start | bytes 196612
  91.8 1.1 %copy-start.7 = (f32[2,2,4096]{2,1,0:T(2,128)S(1)}, f32[2,2,4096]{2,1,0:T(2,128)}, u32[]{:S(2)}) copy-start(f32[2,2,4096]{2,1,0:T(2,128)} %get-tuple-element.20) | copy-start | bytes 196612

commit v9 on v8

--- a/solution.py
+++ b/solution.py
@@ -278,7 +278,7 @@
     return weights.astype(jnp.bfloat16)
 
 
-def backproject_kernel(shift_ref, tiles_ref, mats_ref, out_ref):
+def backproject_kernel(shift_ref, columns_ref, mats_ref, out_ref, tiles_ref):
     p = pl.program_id(0)
     tile_count = out_ref.shape[2] // LANES
     depth_count = out_ref.shape[1]
@@ -286,6 +286,12 @@
     @pl.when(p == 0)
     def _():
         out_ref[...] = jnp.zeros_like(out_ref)
+        tiles_ref[...] = jnp.zeros_like(tiles_ref)
+
+    for tile in range(tile_count):
+        tiles_ref[0, tile + 1] = columns_ref[0, :, tile * LANES:(tile + 1) * LANES].astype(
+            jnp.float32
+        )
 
     ends = jnp.concatenate([tiles_ref[0, 1], tiles_ref[0, tile_count]], axis=0).astype(jnp.bfloat16)
     second_half = lax.broadcasted_iota(jnp.int32, (LANES, LANES), 1) >= BLOCK
@@ -323,10 +329,15 @@
             lanes = pl.ds(tile * LANES, LANES)
             out_ref[row, :, lanes] = out_ref[row, :, lanes] + part
 
-
-def backproject(shifts, tiles, mats, column_count):
+    @pl.when(p == pl.num_programs(0) - 1)
+    def _():
+        out_ref[...] = math.pi / P_SIZE * out_ref[...]
+
+
+def backproject(shifts, columns, mats):
     count, rows = shifts.shape
-    depth_count = tiles.shape[2]
+    depth_count, column_count = columns.shape[1], columns.shape[2]
+    tile_count = column_count // LANES
     return pl.pallas_call(
         backproject_kernel,
         out_shape=jax.ShapeDtypeStruct((rows, depth_count, column_count), jnp.float32),
@@ -334,13 +345,14 @@
             num_scalar_prefetch=1,
             grid=(count,),
             in_specs=[
-                pl.BlockSpec((1,) + tiles.shape[1:], lambda p, s: (p, 0, 0, 0)),
+                pl.BlockSpec((1,) + columns.shape[1:], lambda p, s: (p, 0, 0)),
                 pl.BlockSpec((1,) + mats.shape[1:], lambda p, s: (p, 0, 0, 0)),
             ],
             out_specs=pl.BlockSpec((rows, depth_count, column_count), lambda p, s: (0, 0, 0)),
+            scratch_shapes=[pltpu.VMEM((1, tile_count + 3, depth_count, LANES), jnp.float32)],
         ),
         compiler_params=pltpu.CompilerParams(dimension_semantics=("arbitrary",)),
-    )(shifts, tiles, mats)
+    )(shifts, columns, mats)
 
 
 def per_device(filtered, angle_index, band_offset, band_length, foot_block):
@@ -363,11 +375,7 @@
     row_global = (row_base + jnp.arange(row_count)).astype(jnp.float32)
     shifts = foot_block[:, :, 2] - 2
     mats = jax.vmap(footprint_mats, in_axes=(0, None, None))(angle_index, row_global, rows_total)
-    tile_count = column_count // LANES
-    tiles = columns.astype(jnp.float32).reshape(P_SIZE, depth_count, tile_count, LANES)
-    tiles = jnp.pad(tiles.transpose(0, 2, 1, 3), ((0, 0), (1, 2), (0, 0), (0, 0)))
-    summed = backproject(shifts, tiles, mats, column_count)
-    backprojection = math.pi / P_SIZE * summed
+    backprojection = backproject(shifts, columns, mats)
     current = backprojection
     extended = with_wide_halo(backprojection, ITERS)
     fidelity = extended

time: 99.2 us -> 98.5 us (level)
  other arithmetic: 18.5 us -> 14.7 us
  local copies, waits for them, and re-layouts: 6.39 us -> 9.94 us
    slice x3, local copies, waits for them, and re-layouts: 2.35 us -> 5.89 us  [with_wide_halo(): sent = [cells[row_parts[r], depth_parts[d]] for r, d in STEPS]]
    pad x1 -> x0, other arithmetic: 2.78 us -> none  [per_device(): jnp.pad(tiles.transpose(0, 2, 1, 3), ((0, 0), (1, 2), (0, 0), (0, 0)))]
    mul x1 -> x0, other arithmetic: 1.09 us -> none  [per_device(): backprojection = math.pi / P_SIZE * summed]
where the time goes in v9:
time: 98.5 us; the launch traced here: 97.8 us
  Pallas kernels  69 us (70%)
  other arithmetic  14.7 us (15%)
  local copies, waits for them, and re-layouts  9.94 us (10%)
  starting transfers between devices  3.03 us (3%)
    pallas_call x1, Pallas kernels, with_wide_halo(): pl.pallas_call(functools.partial(halo_kernel, count), out_shape=[jax.Shap...  30.6 us
    pallas_call x1, Pallas kernels, gather_columns(): pl.pallas_call(functools.partial(gather_kernel, count), out_shape=jax.Sha...  25.9 us
    pallas_call x1, Pallas kernels, backproject(): pl.pallas_call(backproject_kernel, out_shape=jax.ShapeDtypeStruct((rows,...  12.5 us
    slice x3, local copies, waits for them, and re-layouts, with_wide_halo(): sent = [cells[row_parts[r], depth_parts[d]] for r, d in STEPS]  5.89 us
    add x2, other arithmetic, smooth_update(): current + step_length * (smooth_weight * divergence - (current - fidelity))  3.13 us
    convert_element_type x1, other arithmetic, footprint_mats(): return weights.astype(jnp.bfloat16)  2.37 us
    mul x2, other arithmetic, smooth_update(): normal_rows = forward_rows * inverse  2.02 us
  transfers between devices with their start and end apart: 2, of which 0 were waited for; matrix products, arithmetic and copies ran while one was open for 7% of the time, Pallas kernels for 0%

profile of v9, /device:TPU:56, one launch (start us, length us, event | category | flops | bytes accessed | tf_op | source)
XLA Modules:
  0.0 97.8 jit_solution(2740817466553951855)
XLA Ops:
  0.0 1.0 fusion.25
  1.0 1.7 %collective-permute-start = (bf16[16,4,256]{2,1,0:T(4,128)(2,1)S(1)}, bf16[16,4,256]{2,1,0:T(4,128)(2,1)S(1)}, u32[]{:S(2)}, u32[]{:S(2)}) collective-permute-start(bf16[16,4,256]{2,1,0:T(4,128)(2,1)S(1)} %get-tuple-element.35), channel_id=1, source_target_pairs={{0,16},{16,32},{32,48},{48,64},{64,80},{80,96},{96,112},{112,128},... | collective-permute-start | bytes 98312 | tf_op jit(solution)/shard_map/ppermute | solution.py:33
  2.7 1.3 %collective-permute-start.1 = (bf16[16,4,256]{2,1,0:T(4,128)(2,1)S(1)}, bf16[16,4,256]{2,1,0:T(4,128)(2,1)S(1)}, u32[]{:S(2)}, u32[]{:S(2)}) collective-permute-start(bf16[16,4,256]{2,1,0:T(4,128)(2,1)S(1)} %get-tuple-element.36), channel_id=1, source_target_pairs={{16,0},{32,16},{48,32},{64,48},{80,64},{96,80},{112,96},{128,112},... | collective-permute-start | bytes 98312 | tf_op jit(solution)/shard_map/ppermute | solution.py:35
  4.1 0.7 bitcast_add_fusion
  4.8 0.7 convert_bitcast_fusion
  5.5 0.7 multiply_add_fusion.3
  6.6 0.8 slice.102
  7.5 0.7 fusion.18
  8.3 2.4 %divide_convert_fusion.mats_ref = bf16[16,4,128,128]{3,2,1,0:T(8,128)(2,1)} fusion(f32[16]{0:T(128)S(1)} %get-tuple-element.38, f32[16,4,128]{2,1,0:T(4,128)S(1)} %pad_maximum_fusion, f32[128]{0:T(128)S(1)} %convert_add_fusion.1), kind=kLoop, calls=%fused_computation | loop fusion | flops 7340032 | bytes 2130496 | tf_op jit(solution)/shard_map/vmap()/convert_element_type | solution.py:278
  10.7 0.7 copy.9.shift_ref
  11.4 0.8 convolution_convert_fusion.local_ref
  12.2 25.9 %shard_map.55.columns_ref = bf16[16,8,4096]{2,1,0:T(8,128)(2,1)} custom-call(bf16[16,8,256]{2,1,0:T(8,128)(2,1)} %convolution_convert_fusion.local_ref), custom_call_target="tpu_custom_call" | custom-call | tf_op jit(solution)/shard_map/pallas_call | solution.py:119
  38.2 12.5 %shard_map.56 = f32[4,8,4096]{2,1,0:T(8,128)} custom-call(s32[16,4]{1,0:T(8,128)} %copy.9.shift_ref, bf16[16,8,4096]{2,1,0:T(8,128)(2,1)} %shard_map.55.columns_ref, bf16[16,4,128,128]{3,2,1,0:T(8,128)(2,1)} %divide_convert_fusion.mats_ref), custom_call_target="tpu_custom_call" | custom-call | tf_op jit(solution)/shard_map/pallas_call | solution.py:341
  50.7 2.0 %fusion.22 = (f32[2,2,4096]{2,1,0:T(2,128)}, f32[2,2,4096]{2,1,0:T(2,128)}, f32[2,2,4096]{2,1,0:T(2,128)}, f32[2,2,4096]{2,1,0:T(2,128)}) fusion(f32[4,8,4096]{2,1,0:T(8,128)} %shard_map.56), kind=kLoop, calls=%fused_computation.68 | loop fusion | bytes 524288 | tf_op jit(solution)/shard_map/slice | solution.py:173
  52.7 2.0 %fusion.24 = (f32[4,2,4096]{2,1,0:T(2,128)}, f32[4,2,4096]{2,1,0:T(2,128)}) fusion(f32[4,8,4096]{2,1,0:T(8,128)} %shard_map.56), kind=kLoop, calls=%fused_computation.70 | loop fusion | bytes 524288 | tf_op jit(solution)/shard_map/slice | solution.py:173
  54.7 1.9 %fusion.23 = (f32[2,8,4096]{2,1,0:T(8,128)}, f32[2,8,4096]{2,1,0:T(8,128)}) fusion(f32[4,8,4096]{2,1,0:T(8,128)} %shard_map.56), kind=kLoop, calls=%fused_computation.69 | loop fusion | bytes 1048576 | tf_op jit(solution)/shard_map/slice | solution.py:173
  56.6 30.6 %shard_map.57 = (f32[2,2,4096]{2,1,0:T(2,128)}, f32[2,8,4096]{2,1,0:T(8,128)}, f32[2,2,4096]{2,1,0:T(2,128)}, f32[4,2,4096]{2,1,0:T(2,128)}, f32[4,2,4096]{2,1,0...) custom-call(f32[2,2,4096]{2,1,0:T(2,128)} %get-tuple-element.30.refs_0_, ...), custom_call_target="tpu_custom_call" | custom-call | tf_op jit(solution)/shard_map/pallas_call | solution.py:174
  87.2 1.6 %maximum_maximum_fusion = f32[8,12,4096]{2,1,0:T(8,128)S(1)} fusion(f32[2,2,4096]{2,1,0:T(2,128)} %get-tuple-element.20, f32[2,8,4096]{2,1,0:T(8,128)} %get-tuple-element.19, f32[2,2,4096]{2,1,0:T(2,128)} %get-tuple-element.18, f32[4,2,4096]{2,1,0:T(2,128)} %get-tuple-element.17, f32[4,8,4096]{2,1,0:T(8,128)S(1)} %copy-done, ...), kind=kLoop, calls=%fused_computation.3 | loop fusion | flops 3145728 | bytes 3145728 | tf_op jit(solution)/shard_map/concatenate | solution.py:190
  89.3 0.6 slice_subtract_fusion
  89.9 1.2 %fusion = (f32[8,12,4096]{2,1,0:T(8,128)S(1)}, f32[8,12,4096]{2,1,0:T(8,128)S(1)}, f32[8,12,4096]{2,1,0:T(8,128)S(1)}) fusion(f32[7,12,4096]{2,1,0:T(8,128)S(1)} %slice_subtract_fusion.2, f32[8]{0:T(128)S(1)} %and_convert_fusion.3, f32[8,12,4095]{2,1,0:T(8,128)S(1)} %slice_subtract_fusion, f32[12]{0:T(128)S(1)} %and_convert_fusion.2, ...), kind=kLoop, calls=%fused_computation.8 | loop fusion | flops 4325376 | bytes 9109200 | tf_op jit(solution)/shard_map/mul | solution.py:249
  91.4 0.7 copy-done.1
  92.3 1.9 %multiply_add_fusion = f32[8,12,4096]{2,1,0:T(8,128)S(1)} fusion(f32[8,12,4095]{2,1,0:T(8,128)S(1)} %bitcast.14, f32[8,12,4096]{2,1,0:T(8,128)S(1)} %get-tuple-element.22, f32[8,11,4096]{2,1,0:T(8,128)S(1)} %bitcast.15, f32[8,12,4096]{2,1,0:T(8,128)S(1)} %get-tuple-element.23, f32[8,12,4096]{2,1,0:T(8,128)S(1)} %get-tuple-element.21, ...), kind=kLoop, calls=%fused_computation.4 | loop fusion | flops 7077888 | bytes 12254848 | tf_op jit(solution)/shard_map/add | solution.py:265
  95.2 0.8 fusion.2
  96.6 1.2 %fusion.6 = f32[4,8,4096]{2,1,0:T(8,128)} fusion(f32[6,10,4096]{2,1,0:T(8,128)S(1)} %slice.161, f32[6,10,4096]{2,1,0:T(8,128)S(1)} %slice.151, f32[6,10,4095]{2,1,0:T(8,128)S(1)} %bitcast.17, f32[6,10,4096]{2,1,0:T(8,128)S(1)} %get-tuple-element.25, f32[6,10,4096]{2,1,0:T(8,128)S(1)} %pad_subtract_fusion), kind=kLoop, calls=%fused_computation.26 | loop fusion | flops 917504 | bytes 3604240 | tf_op jit(solution)/shard_map/add | solution.py:265
  (47 shorter events, 3.0 us)
Async XLA Ops:
  0.0 11.4 %copy-start.9 = (bf16[16,8,256]{2,1,0:T(8,128)(2,1)S(1)}, bf16[16,8,256]{2,1,0:T(8,128)(2,1)}, u32[]{:S(2)}) copy-start(bf16[16,8,256]{2,1,0:T(8,128)(2,1)} %param.5) | copy-start | bytes 196612
  1.0 10.4 %collective-permute-start = (bf16[16,4,256]{2,1,0:T(4,128)(2,1)S(1)}, bf16[16,4,256]{2,1,0:T(4,128)(2,1)S(1)}, u32[]{:S(2)}, u32[]{:S(2)}) collective-permute-start(bf16[16,4,256]{2,1,0:T(4,128)(2,1)S(1)} %get-tuple-element.35), channel_id=1, source_target_pairs={{0,16},{16,32},{32,48},{48,64},{64,80},{80,96},{96,112},{112,128},... | collective-permute-start | bytes 98312 | tf_op jit(solution)/shard_map/ppermute | solution.py:33
  2.7 8.6 %collective-permute-start.1 = (bf16[16,4,256]{2,1,0:T(4,128)(2,1)S(1)}, bf16[16,4,256]{2,1,0:T(4,128)(2,1)S(1)}, u32[]{:S(2)}, u32[]{:S(2)}) collective-permute-start(bf16[16,4,256]{2,1,0:T(4,128)(2,1)S(1)} %get-tuple-element.36), channel_id=1, source_target_pairs={{16,0},{32,16},{48,32},{64,48},{80,64},{96,80},{112,96},{128,112},... | collective-permute-start | bytes 98312 | tf_op jit(solution)/shard_map/ppermute | solution.py:35
  50.7 36.5 %copy-start = (f32[4,8,4096]{2,1,0:T(8,128)S(1)}, f32[4,8,4096]{2,1,0:T(8,128)}, u32[]{:S(2)}) copy-start(f32[4,8,4096]{2,1,0:T(8,128)} %shard_map.56) | copy-start | bytes 1572868
  91.1 1.0 copy-start.1
  91.1 1.0 %copy-start.2 = (f32[2,8,4096]{2,1,0:T(8,128)S(1)}, f32[2,8,4096]{2,1,0:T(8,128)}, u32[]{:S(2)}) copy-start(f32[2,8,4096]{2,1,0:T(8,128)} %get-tuple-element.19) | copy-start | bytes 786436
  91.2 1.0 %copy-start.3 = (f32[4,2,4096]{2,1,0:T(2,128)S(1)}, f32[4,2,4096]{2,1,0:T(2,128)}, u32[]{:S(2)}) copy-start(f32[4,2,4096]{2,1,0:T(2,128)} %get-tuple-element.16) | copy-start | bytes 393220
  91.2 1.1 %copy-start.4 = (f32[4,2,4096]{2,1,0:T(2,128)S(1)}, f32[4,2,4096]{2,1,0:T(2,128)}, u32[]{:S(2)}) copy-start(f32[4,2,4096]{2,1,0:T(2,128)} %get-tuple-element.17) | copy-start | bytes 393220
  91.2 1.1 %copy-start.5 = (f32[2,2,4096]{2,1,0:T(2,128)S(1)}, f32[2,2,4096]{2,1,0:T(2,128)}, u32[]{:S(2)}) copy-start(f32[2,2,4096]{2,1,0:T(2,128)} %get-tuple-element.13) | copy-start | bytes 196612
  91.2 1.1 %copy-start.6 = (f32[2,2,4096]{2,1,0:T(2,128)S(1)}, f32[2,2,4096]{2,1,0:T(2,128)}, u32[]{:S(2)}) copy-start(f32[2,2,4096]{2,1,0:T(2,128)} %get-tuple-element.15) | copy-start | bytes 196612
  91.2 1.1 %copy-start.7 = (f32[2,2,4096]{2,1,0:T(2,128)S(1)}, f32[2,2,4096]{2,1,0:T(2,128)}, u32[]{:S(2)}) copy-start(f32[2,2,4096]{2,1,0:T(2,128)} %get-tuple-element.18) | copy-start | bytes 196612
  91.2 1.1 %copy-start.8 = (f32[2,2,4096]{2,1,0:T(2,128)S(1)}, f32[2,2,4096]{2,1,0:T(2,128)}, u32[]{:S(2)}) copy-start(f32[2,2,4096]{2,1,0:T(2,128)} %get-tuple-element.20) | copy-start | bytes 196612

commit v10 on v9

--- a/solution.py
+++ b/solution.py
@@ -133,11 +133,14 @@
 STEPS = ((1, 1), (1, 0), (1, -1), (0, 1), (0, -1), (-1, 1), (-1, 0), (-1, -1))
 
 
-def halo_kernel(count, *refs):
+def halo_kernel(count, width, cells_ref, *refs):
     pieces = len(STEPS)
-    sources, targets = refs[:pieces], refs[pieces:2 * pieces]
-    send_sem, recv_sem = refs[2 * pieces], refs[2 * pieces + 1]
+    targets = refs[:pieces]
+    send_sem, recv_sem = refs[pieces], refs[pieces + 1]
     row_count, depth_count = count
+    rows, depth = cells_ref.shape[0], cells_ref.shape[1]
+    row_parts = {1: pl.ds(rows - width, width), 0: pl.ds(0, rows), -1: pl.ds(0, width)}
+    depth_parts = {1: pl.ds(depth - width, width), 0: pl.ds(0, depth), -1: pl.ds(0, width)}
     row_me = lax.axis_index("gy")
     depth_me = lax.axis_index("gz")
     peers = [
@@ -151,8 +154,9 @@
     pl.semaphore_wait(barrier, pieces)
     copies = []
     for k, peer in enumerate(peers):
+        row_step, depth_step = STEPS[k]
         copy = pltpu.make_async_remote_copy(
-            src_ref=sources[k],
+            src_ref=cells_ref.at[row_parts[row_step], depth_parts[depth_step]],
             dst_ref=targets[k],
             send_sem=send_sem.at[k],
             recv_sem=recv_sem.at[k],
@@ -172,16 +176,16 @@
     depth_parts = {1: slice(depth - width, depth), 0: slice(None), -1: slice(0, width)}
     sent = [cells[row_parts[r], depth_parts[d]] for r, d in STEPS]
     received = pl.pallas_call(
-        functools.partial(halo_kernel, count),
+        functools.partial(halo_kernel, count, width),
         out_shape=[jax.ShapeDtypeStruct(piece.shape, piece.dtype) for piece in sent],
-        in_specs=[pl.BlockSpec(memory_space=pl.ANY)] * len(STEPS),
+        in_specs=[pl.BlockSpec(memory_space=pl.ANY)],
         out_specs=[pl.BlockSpec(memory_space=pl.ANY)] * len(STEPS),
         scratch_shapes=[
             pltpu.SemaphoreType.DMA((len(STEPS),)),
             pltpu.SemaphoreType.DMA((len(STEPS),)),
         ],
         compiler_params=pltpu.CompilerParams(collective_id=1, has_side_effects=True),
-    )(*sent)
+    )(cells)
     parts = dict(zip(STEPS, received))
     parts[(0, 0)] = cells
     bands = [

time: 98.5 us -> 92.8 us (0.942)
  local copies, waits for them, and re-layouts: 9.94 us -> 4.19 us
    slice x3 -> x0, local copies, waits for them, and re-layouts: 5.89 us -> none  [with_wide_halo(): sent = [cells[row_parts[r], depth_parts[d]] for r, d in STEPS]]
  transfers between devices with their start and end apart: 2 -> 2, of which waited for: 0 -> 0; matrix products, arithmetic and copies ran while one was open for 7% -> 8% of each run, Pallas kernels for 0% -> 0%
where the time goes in v10:
time: 92.8 us; the launch traced here: 92.2 us
  Pallas kernels  69 us (74%)
  other arithmetic  14.8 us (16%)
  local copies, waits for them, and re-layouts  4.19 us (5%)
  starting transfers between devices  3.03 us (3%)
    pallas_call x1, Pallas kernels, with_wide_halo(): pl.pallas_call(functools.partial(halo_kernel, count, width), out_shape=[j...  30.6 us
    pallas_call x1, Pallas kernels, gather_columns(): pl.pallas_call(functools.partial(gather_kernel, count), out_shape=jax.Sha...  25.9 us
    pallas_call x1, Pallas kernels, backproject(): pl.pallas_call(backproject_kernel, out_shape=jax.ShapeDtypeStruct((rows,...  12.5 us
    add x2, other arithmetic, smooth_update(): current + step_length * (smooth_weight * divergence - (current - fidelity))  3.13 us
    convert_element_type x1, other arithmetic, footprint_mats(): return weights.astype(jnp.bfloat16)  2.38 us
    mul x2, other arithmetic, smooth_update(): normal_rows = forward_rows * inverse  2.02 us
  transfers between devices with their start and end apart: 2, of which 0 were waited for; matrix products, arithmetic and copies ran while one was open for 8% of the time, Pallas kernels for 0%

profile of v10, /device:TPU:56, one launch (start us, length us, event | category | flops | bytes accessed | tf_op | source)
XLA Modules:
  0.0 92.2 jit_solution(15046246853493127548)
XLA Ops:
  0.0 1.0 %fusion.22 = (bf16[16,4,256]{2,1,0:T(4,128)(2,1)S(1)}, bf16[16,4,256]{2,1,0:T(4,128)(2,1)S(1)}) fusion(bf16[16,8,256]{2,1,0:T(8,128)(2,1)} %param.5), kind=kLoop, calls=%fused_computation.68 | loop fusion | bytes 131072 | tf_op jit(solution)/shard_map/slice | solution.py:30
  1.0 1.7 %collective-permute-start = (bf16[16,4,256]{2,1,0:T(4,128)(2,1)S(1)}, bf16[16,4,256]{2,1,0:T(4,128)(2,1)S(1)}, u32[]{:S(2)}, u32[]{:S(2)}) collective-permute-start(bf16[16,4,256]{2,1,0:T(4,128)(2,1)S(1)} %get-tuple-element.27), channel_id=1, source_target_pairs={{0,16},{16,32},{32,48},{48,64},{64,80},{80,96},{96,112},{112,128},... | collective-permute-start | bytes 98312 | tf_op jit(solution)/shard_map/ppermute | solution.py:33
  2.7 1.3 %collective-permute-start.1 = (bf16[16,4,256]{2,1,0:T(4,128)(2,1)S(1)}, bf16[16,4,256]{2,1,0:T(4,128)(2,1)S(1)}, u32[]{:S(2)}, u32[]{:S(2)}) collective-permute-start(bf16[16,4,256]{2,1,0:T(4,128)(2,1)S(1)} %get-tuple-element.28), channel_id=1, source_target_pairs={{16,0},{32,16},{48,32},{64,48},{80,64},{96,80},{112,96},{128,112},... | collective-permute-start | bytes 98312 | tf_op jit(solution)/shard_map/ppermute | solution.py:35
  4.1 0.7 bitcast_add_fusion
  4.8 0.7 convert_bitcast_fusion
  5.5 0.7 multiply_add_fusion.3
  6.6 0.8 slice.78
  7.5 0.7 fusion.18
  8.3 2.4 %divide_convert_fusion.mats_ref = bf16[16,4,128,128]{3,2,1,0:T(8,128)(2,1)} fusion(f32[16]{0:T(128)S(1)} %get-tuple-element.30, f32[16,4,128]{2,1,0:T(4,128)S(1)} %pad_maximum_fusion, f32[128]{0:T(128)S(1)} %convert_add_fusion.1), kind=kLoop, calls=%fused_computation | loop fusion | flops 7340032 | bytes 2130496 | tf_op jit(solution)/shard_map/vmap()/convert_element_type | solution.py:282
  10.7 0.7 copy.9.shift_ref
  11.4 0.8 convolution_convert_fusion.local_ref
  12.2 25.9 %shard_map.55.columns_ref = bf16[16,8,4096]{2,1,0:T(8,128)(2,1)} custom-call(bf16[16,8,256]{2,1,0:T(8,128)(2,1)} %convolution_convert_fusion.local_ref), custom_call_target="tpu_custom_call" | custom-call | tf_op jit(solution)/shard_map/pallas_call | solution.py:119
  38.2 12.5 %shard_map.56.cells_ref = f32[4,8,4096]{2,1,0:T(8,128)} custom-call(s32[16,4]{1,0:T(8,128)} %copy.9.shift_ref, bf16[16,8,4096]{2,1,0:T(8,128)(2,1)} %shard_map.55.columns_ref, bf16[16,4,128,128]{3,2,1,0:T(8,128)(2,1)} %divide_convert_fusion.mats_ref), custom_call_target="tpu_custom_call" | custom-call | tf_op jit(solution)/shard_map/pallas_call | solution.py:345
  50.7 30.6 %shard_map.57 = (f32[2,2,4096]{2,1,0:T(2,128)}, f32[2,8,4096]{2,1,0:T(8,128)}, f32[2,2,4096]{2,1,0:T(2,128)}, f32[4,2,4096]{2,1,0:T(2,128)}, f32[4,2,4096]{2,1,0...) custom-call(f32[4,8,4096]{2,1,0:T(8,128)} %shard_map.56.cells_ref), custom_call_target="tpu_custom_call" | custom-call | tf_op jit(solution)/shard_map/pallas_call | solution.py:178
  81.3 1.7 %maximum_maximum_fusion = f32[8,12,4096]{2,1,0:T(8,128)S(1)} fusion(f32[2,2,4096]{2,1,0:T(2,128)} %get-tuple-element.20, f32[2,8,4096]{2,1,0:T(8,128)} %get-tuple-element.19, f32[2,2,4096]{2,1,0:T(2,128)} %get-tuple-element.18, f32[4,2,4096]{2,1,0:T(2,128)} %get-tuple-element.17, f32[4,8,4096]{2,1,0:T(8,128)} %shard_map.56.cells_ref, ...), kind=kLoop, calls=%fused_computation.3 | loop fusion | flops 3145728 | bytes 3145728 | tf_op jit(solution)/shard_map/concatenate | solution.py:194
  83.3 0.3 slice_subtract_fusion.1
  83.6 0.6 slice_subtract_fusion
  84.2 1.2 %fusion = (f32[8,12,4096]{2,1,0:T(8,128)S(1)}, f32[8,12,4096]{2,1,0:T(8,128)S(1)}, f32[8,12,4096]{2,1,0:T(8,128)S(1)}) fusion(f32[7,12,4096]{2,1,0:T(8,128)S(1)} %slice_subtract_fusion.2, f32[8]{0:T(128)S(1)} %and_convert_fusion.3, f32[8,12,4095]{2,1,0:T(8,128)S(1)} %slice_subtract_fusion, f32[12]{0:T(128)S(1)} %and_convert_fusion.2, ...), kind=kLoop, calls=%fused_computation.8 | loop fusion | flops 4325376 | bytes 9109200 | tf_op jit(solution)/shard_map/mul | solution.py:253
  85.6 0.8 copy-done
  86.7 1.9 %multiply_add_fusion = f32[8,12,4096]{2,1,0:T(8,128)S(1)} fusion(f32[8,12,4095]{2,1,0:T(8,128)S(1)} %bitcast.14, f32[8,12,4096]{2,1,0:T(8,128)S(1)} %get-tuple-element.22, f32[8,11,4096]{2,1,0:T(8,128)S(1)} %bitcast.15, f32[8,12,4096]{2,1,0:T(8,128)S(1)} %get-tuple-element.23, f32[8,12,4096]{2,1,0:T(8,128)S(1)} %get-tuple-element.21, ...), kind=kLoop, calls=%fused_computation.4 | loop fusion | flops 7077888 | bytes 12254848 | tf_op jit(solution)/shard_map/add | solution.py:269
  88.7 0.5 slice_subtract_fusion.3
  89.6 0.8 fusion.2
  90.6 0.4 pad_subtract_fusion
  91.0 1.2 %fusion.6 = f32[4,8,4096]{2,1,0:T(8,128)} fusion(f32[6,10,4096]{2,1,0:T(8,128)S(1)} %slice.121, f32[6,10,4096]{2,1,0:T(8,128)S(1)} %slice.111, f32[6,10,4095]{2,1,0:T(8,128)S(1)} %bitcast.17, f32[6,10,4096]{2,1,0:T(8,128)S(1)} %get-tuple-element.25, f32[6,10,4096]{2,1,0:T(8,128)S(1)} %pad_subtract_fusion), kind=kLoop, calls=%fused_computation.26 | loop fusion | flops 917504 | bytes 3604240 | tf_op jit(solution)/shard_map/add | solution.py:269
  (44 shorter events, 1.9 us)
Async XLA Ops:
  0.0 11.4 %copy-start.9 = (bf16[16,8,256]{2,1,0:T(8,128)(2,1)S(1)}, bf16[16,8,256]{2,1,0:T(8,128)(2,1)}, u32[]{:S(2)}) copy-start(bf16[16,8,256]{2,1,0:T(8,128)(2,1)} %param.5) | copy-start | bytes 196612
  1.0 10.4 %collective-permute-start = (bf16[16,4,256]{2,1,0:T(4,128)(2,1)S(1)}, bf16[16,4,256]{2,1,0:T(4,128)(2,1)S(1)}, u32[]{:S(2)}, u32[]{:S(2)}) collective-permute-start(bf16[16,4,256]{2,1,0:T(4,128)(2,1)S(1)} %get-tuple-element.27), channel_id=1, source_target_pairs={{0,16},{16,32},{32,48},{48,64},{64,80},{80,96},{96,112},{112,128},... | collective-permute-start | bytes 98312 | tf_op jit(solution)/shard_map/ppermute | solution.py:33
  2.7 8.6 %collective-permute-start.1 = (bf16[16,4,256]{2,1,0:T(4,128)(2,1)S(1)}, bf16[16,4,256]{2,1,0:T(4,128)(2,1)S(1)}, u32[]{:S(2)}, u32[]{:S(2)}) collective-permute-start(bf16[16,4,256]{2,1,0:T(4,128)(2,1)S(1)} %get-tuple-element.28), channel_id=1, source_target_pairs={{16,0},{32,16},{48,32},{64,48},{80,64},{96,80},{112,96},{128,112},... | collective-permute-start | bytes 98312 | tf_op jit(solution)/shard_map/ppermute | solution.py:35
  85.4 1.0 %copy-start = (f32[4,8,4096]{2,1,0:T(8,128)S(1)}, f32[4,8,4096]{2,1,0:T(8,128)}, u32[]{:S(2)}) copy-start(f32[4,8,4096]{2,1,0:T(8,128)} %shard_map.56.cells_ref) | copy-start | bytes 1572868
  85.4 1.1 %copy-start.1 = (f32[2,8,4096]{2,1,0:T(8,128)S(1)}, f32[2,8,4096]{2,1,0:T(8,128)}, u32[]{:S(2)}) copy-start(f32[2,8,4096]{2,1,0:T(8,128)} %get-tuple-element.14) | copy-start | bytes 786436
  85.4 1.2 %copy-start.2 = (f32[2,8,4096]{2,1,0:T(8,128)S(1)}, f32[2,8,4096]{2,1,0:T(8,128)}, u32[]{:S(2)}) copy-start(f32[2,8,4096]{2,1,0:T(8,128)} %get-tuple-element.19) | copy-start | bytes 786436
  85.4 1.2 %copy-start.3 = (f32[4,2,4096]{2,1,0:T(2,128)S(1)}, f32[4,2,4096]{2,1,0:T(2,128)}, u32[]{:S(2)}) copy-start(f32[4,2,4096]{2,1,0:T(2,128)} %get-tuple-element.16) | copy-start | bytes 393220
  85.4 1.2 %copy-start.4 = (f32[4,2,4096]{2,1,0:T(2,128)S(1)}, f32[4,2,4096]{2,1,0:T(2,128)}, u32[]{:S(2)}) copy-start(f32[4,2,4096]{2,1,0:T(2,128)} %get-tuple-element.17) | copy-start | bytes 393220
  85.4 1.2 %copy-start.5 = (f32[2,2,4096]{2,1,0:T(2,128)S(1)}, f32[2,2,4096]{2,1,0:T(2,128)}, u32[]{:S(2)}) copy-start(f32[2,2,4096]{2,1,0:T(2,128)} %get-tuple-element.13) | copy-start | bytes 196612
  85.4 1.2 %copy-start.6 = (f32[2,2,4096]{2,1,0:T(2,128)S(1)}, f32[2,2,4096]{2,1,0:T(2,128)}, u32[]{:S(2)}) copy-start(f32[2,2,4096]{2,1,0:T(2,128)} %get-tuple-element.15) | copy-start | bytes 196612
  85.4 1.2 %copy-start.7 = (f32[2,2,4096]{2,1,0:T(2,128)S(1)}, f32[2,2,4096]{2,1,0:T(2,128)}, u32[]{:S(2)}) copy-start(f32[2,2,4096]{2,1,0:T(2,128)} %get-tuple-element.18) | copy-start | bytes 196612
  85.4 1.2 %copy-start.8 = (f32[2,2,4096]{2,1,0:T(2,128)S(1)}, f32[2,2,4096]{2,1,0:T(2,128)}, u32[]{:S(2)}) copy-start(f32[2,2,4096]{2,1,0:T(2,128)} %get-tuple-element.20) | copy-start | bytes 196612

commit v11 on v10

--- a/solution.py
+++ b/solution.py
@@ -133,14 +133,16 @@
 STEPS = ((1, 1), (1, 0), (1, -1), (0, 1), (0, -1), (-1, 1), (-1, 0), (-1, -1))
 
 
-def halo_kernel(count, width, cells_ref, *refs):
+def halo_kernel(count, width, cells_ref, extended_ref, send_sem, recv_sem, own_sem):
     pieces = len(STEPS)
-    targets = refs[:pieces]
-    send_sem, recv_sem = refs[pieces], refs[pieces + 1]
     row_count, depth_count = count
     rows, depth = cells_ref.shape[0], cells_ref.shape[1]
     row_parts = {1: pl.ds(rows - width, width), 0: pl.ds(0, rows), -1: pl.ds(0, width)}
     depth_parts = {1: pl.ds(depth - width, width), 0: pl.ds(0, depth), -1: pl.ds(0, width)}
+    row_places = {1: pl.ds(0, width), 0: pl.ds(width, rows), -1: pl.ds(width + rows, width)}
+    depth_places = {
+        1: pl.ds(depth - width, width), 0: pl.ds(depth, depth), -1: pl.ds(2 * depth, width)
+    }
     row_me = lax.axis_index("gy")
     depth_me = lax.axis_index("gz")
     peers = [
@@ -151,13 +153,17 @@
     barrier = pltpu.get_barrier_semaphore()
     for peer in peers:
         pl.semaphore_signal(barrier, inc=1, device_id=peer, device_id_type=pl.DeviceIdType.MESH)
+    own = pltpu.make_async_copy(
+        cells_ref, extended_ref.at[row_places[0], depth_places[0]], own_sem
+    )
+    own.start()
     pl.semaphore_wait(barrier, pieces)
     copies = []
     for k, peer in enumerate(peers):
         row_step, depth_step = STEPS[k]
         copy = pltpu.make_async_remote_copy(
             src_ref=cells_ref.at[row_parts[row_step], depth_parts[depth_step]],
-            dst_ref=targets[k],
+            dst_ref=extended_ref.at[row_places[row_step], depth_places[depth_step]],
             send_sem=send_sem.at[k],
             recv_sem=recv_sem.at[k],
             device_id=peer,
@@ -165,33 +171,26 @@
         )
         copy.start()
         copies.append(copy)
+    own.wait()
     for copy in copies:
         copy.wait()
 
 
 def with_wide_halo(cells, width):
-    rows, depth = cells.shape[0], cells.shape[1]
+    rows, depth, cols = cells.shape
     count = (lax.axis_size("gy"), lax.axis_size("gz"))
-    row_parts = {1: slice(rows - width, rows), 0: slice(None), -1: slice(0, width)}
-    depth_parts = {1: slice(depth - width, depth), 0: slice(None), -1: slice(0, width)}
-    sent = [cells[row_parts[r], depth_parts[d]] for r, d in STEPS]
-    received = pl.pallas_call(
+    return pl.pallas_call(
         functools.partial(halo_kernel, count, width),
-        out_shape=[jax.ShapeDtypeStruct(piece.shape, piece.dtype) for piece in sent],
+        out_shape=jax.ShapeDtypeStruct((rows + 2 * width, 3 * depth, cols), cells.dtype),
         in_specs=[pl.BlockSpec(memory_space=pl.ANY)],
-        out_specs=[pl.BlockSpec(memory_space=pl.ANY)] * len(STEPS),
+        out_specs=pl.BlockSpec(memory_space=pl.ANY),
         scratch_shapes=[
             pltpu.SemaphoreType.DMA((len(STEPS),)),
             pltpu.SemaphoreType.DMA((len(STEPS),)),
+            pltpu.SemaphoreType.DMA(()),
         ],
         compiler_params=pltpu.CompilerParams(collective_id=1, has_side_effects=True),
-    )(cells)
-    parts = dict(zip(STEPS, received))
-    parts[(0, 0)] = cells
-    bands = [
-        jnp.concatenate([parts[(r, 1)], parts[(r, 0)], parts[(r, -1)]], axis=1) for r in (1, 0, -1)
-    ]
-    return jnp.concatenate(bands, axis=0)
+    )(cells)[:, depth - width:2 * depth + width]
 
 
 def geometry(angle_value):

time: 92.8 us -> 93.1 us (level)
  other arithmetic: 14.8 us -> 16.2 us
  local copies, waits for them, and re-layouts: 4.19 us -> 3.23 us
    sub x2, other arithmetic: 1.08 us -> 4.07 us  [smooth_update(): current[:, :, 1:] - current[:, :, :-1]]
    concatenate x1 -> x0, other arithmetic: 1.72 us -> none  [with_wide_halo(): return jnp.concatenate(bands, axis=0)]
    unnamed x21 -> x5, local copies, waits for them, and re-layouts: 1.19 us -> 0.24 us
where the time goes in v11:
time: 93.1 us; the launch traced here: 92.5 us
  Pallas kernels  69 us (74%)
  other arithmetic  16.2 us (17%)
  local copies, waits for them, and re-layouts  3.23 us (3%)
  starting transfers between devices  3.03 us (3%)
    pallas_call x1, Pallas kernels, with_wide_halo(): pl.pallas_call(functools.partial(halo_kernel, count, width), out_shape=ja...  30.6 us
    pallas_call x1, Pallas kernels, gather_columns(): pl.pallas_call(functools.partial(gather_kernel, count), out_shape=jax.Sha...  25.9 us
    pallas_call x1, Pallas kernels, backproject(): pl.pallas_call(backproject_kernel, out_shape=jax.ShapeDtypeStruct((rows,...  12.5 us
    sub x2, other arithmetic, smooth_update(): current[:, :, 1:] - current[:, :, :-1]  4.07 us
    add x2, other arithmetic, smooth_update(): current + step_length * (smooth_weight * divergence - (current - fidelity))  3.14 us
    convert_element_type x1, other arithmetic, footprint_mats(): return weights.astype(jnp.bfloat16)  2.38 us
    mul x2, other arithmetic, smooth_update(): normal_rows = forward_rows * inverse  1.94 us
  transfers between devices with their start and end apart: 2, of which 0 were waited for; matrix products, arithmetic and copies ran while one was open for 8% of the time, Pallas kernels for 0%

profile of v11, /device:TPU:56, one launch (start us, length us, event | category | flops | bytes accessed | tf_op | source)
XLA Modules:
  0.0 92.5 jit_solution(5119856168181380201)
XLA Ops:
  0.0 1.0 %fusion.22 = (bf16[16,4,256]{2,1,0:T(4,128)(2,1)S(1)}, bf16[16,4,256]{2,1,0:T(4,128)(2,1)S(1)}) fusion(bf16[16,8,256]{2,1,0:T(8,128)(2,1)} %param.5), kind=kLoop, calls=%fused_computation.67 | loop fusion | bytes 131072 | tf_op jit(solution)/shard_map/slice | solution.py:30
  1.0 1.7 %collective-permute-start = (bf16[16,4,256]{2,1,0:T(4,128)(2,1)S(1)}, bf16[16,4,256]{2,1,0:T(4,128)(2,1)S(1)}, u32[]{:S(2)}, u32[]{:S(2)}) collective-permute-start(bf16[16,4,256]{2,1,0:T(4,128)(2,1)S(1)} %get-tuple-element.11), channel_id=1, source_target_pairs={{0,16},{16,32},{32,48},{48,64},{64,80},{80,96},{96,112},{112,128},... | collective-permute-start | bytes 98312 | tf_op jit(solution)/shard_map/ppermute | solution.py:33
  2.7 1.3 %collective-permute-start.1 = (bf16[16,4,256]{2,1,0:T(4,128)(2,1)S(1)}, bf16[16,4,256]{2,1,0:T(4,128)(2,1)S(1)}, u32[]{:S(2)}, u32[]{:S(2)}) collective-permute-start(bf16[16,4,256]{2,1,0:T(4,128)(2,1)S(1)} %get-tuple-element.12), channel_id=1, source_target_pairs={{16,0},{32,16},{48,32},{64,48},{80,64},{96,80},{112,96},{128,112},... | collective-permute-start | bytes 98312 | tf_op jit(solution)/shard_map/ppermute | solution.py:35
  4.1 0.7 convert_bitcast_fusion
  4.7 0.7 bitcast_add_fusion
  5.4 0.7 multiply_add_fusion.3
  6.5 0.8 slice.88
  7.5 0.7 fusion.18
  8.2 2.4 %divide_convert_fusion.mats_ref = bf16[16,4,128,128]{3,2,1,0:T(8,128)(2,1)} fusion(f32[16]{0:T(128)S(1)} %get-tuple-element.14, f32[16,4,128]{2,1,0:T(4,128)S(1)} %pad_maximum_fusion, f32[128]{0:T(128)S(1)} %convert_add_fusion.1), kind=kLoop, calls=%fused_computation | loop fusion | flops 7340032 | bytes 2130496 | tf_op jit(solution)/shard_map/vmap()/convert_element_type | solution.py:281
  10.7 0.7 copy.9.shift_ref
  11.4 0.8 convolution_convert_fusion.local_ref
  12.2 25.9 %shard_map.55.columns_ref = bf16[16,8,4096]{2,1,0:T(8,128)(2,1)} custom-call(bf16[16,8,256]{2,1,0:T(8,128)(2,1)} %convolution_convert_fusion.local_ref), custom_call_target="tpu_custom_call" | custom-call | tf_op jit(solution)/shard_map/pallas_call | solution.py:119
  38.2 12.5 %shard_map.56.cells_ref = f32[4,8,4096]{2,1,0:T(8,128)} custom-call(s32[16,4]{1,0:T(8,128)} %copy.9.shift_ref, bf16[16,8,4096]{2,1,0:T(8,128)(2,1)} %shard_map.55.columns_ref, bf16[16,4,128,128]{3,2,1,0:T(8,128)(2,1)} %divide_convert_fusion.mats_ref), custom_call_target="tpu_custom_call" | custom-call | tf_op jit(solution)/shard_map/pallas_call | solution.py:344
  50.7 30.6 %shard_map.57 = f32[8,24,4096]{2,1,0:T(8,128)} custom-call(f32[4,8,4096]{2,1,0:T(8,128)} %shard_map.56.cells_ref), custom_call_target="tpu_custom_call" | custom-call | tf_op jit(solution)/shard_map/pallas_call | solution.py:182
  81.3 3.6 %slice_subtract_fusion = f32[8,12,4095]{2,1,0:T(8,128)S(1)} fusion(f32[8,24,4096]{2,1,0:T(8,128)} %shard_map.57), kind=kLoop, calls=%fused_computation.3 | loop fusion | flops 393120 | bytes 4717440 | tf_op jit(solution)/shard_map/sub | solution.py:244
  85.0 0.3 slice_subtract_fusion.1
  85.3 0.2 slice_subtract_fusion.2
  85.6 1.1 %fusion = (f32[8,12,4096]{2,1,0:T(8,128)S(1)}, f32[8,12,4096]{2,1,0:T(8,128)S(1)}, f32[8,12,4096]{2,1,0:T(8,128)S(1)}) fusion(f32[7,12,4096]{2,1,0:T(8,128)S(1)} %slice_subtract_fusion.2, f32[8]{0:T(128)S(1)} %and_convert_fusion.3, f32[8,12,4095]{2,1,0:T(8,128)S(1)} %slice_subtract_fusion, f32[12]{0:T(128)S(1)} %and_convert_fusion.2, ...), kind=kLoop, calls=%fused_computation.7 | loop fusion | flops 4325376 | bytes 9109200 | tf_op jit(solution)/shard_map/mul | solution.py:252
  86.8 1.9 %multiply_add_fusion = f32[8,12,4096]{2,1,0:T(8,128)S(1)} fusion(f32[8,12,4095]{2,1,0:T(8,128)S(1)} %bitcast.14, f32[8,12,4096]{2,1,0:T(8,128)S(1)} %get-tuple-element.6, f32[8,11,4096]{2,1,0:T(8,128)S(1)} %bitcast.15, f32[8,12,4096]{2,1,0:T(8,128)S(1)} %get-tuple-element.7, f32[8,12,4096]{2,1,0:T(8,128)S(1)} %get-tuple-element.5, ...), kind=kLoop, calls=%fused_computation.1 | loop fusion | flops 3932160 | bytes 12254848 | tf_op jit(solution)/shard_map/add | solution.py:268
  88.7 0.5 slice_subtract_fusion.3
  89.2 0.3 slice_subtract_fusion.4
  89.9 0.8 fusion.2
  90.9 0.4 pad_subtract_fusion
  91.3 1.2 %fusion.6 = f32[4,8,4096]{2,1,0:T(8,128)} fusion(f32[6,10,4096]{2,1,0:T(8,128)S(1)} %slice.111, f32[6,10,4096]{2,1,0:T(8,128)S(1)} %slice.116, f32[6,10,4095]{2,1,0:T(8,128)S(1)} %bitcast.17, f32[6,10,4096]{2,1,0:T(8,128)S(1)} %get-tuple-element.9, f32[6,10,4096]{2,1,0:T(8,128)S(1)} %pad_subtract_fusion), kind=kLoop, calls=%fused_computation.25 | loop fusion | flops 917504 | bytes 3604240 | tf_op jit(solution)/shard_map/add | solution.py:268
  (27 shorter events, 1.4 us)
Async XLA Ops:
  0.0 11.4 %copy-start.1 = (bf16[16,8,256]{2,1,0:T(8,128)(2,1)S(1)}, bf16[16,8,256]{2,1,0:T(8,128)(2,1)}, u32[]{:S(2)}) copy-start(bf16[16,8,256]{2,1,0:T(8,128)(2,1)} %param.5) | copy-start | bytes 196612
  1.0 10.4 %collective-permute-start = (bf16[16,4,256]{2,1,0:T(4,128)(2,1)S(1)}, bf16[16,4,256]{2,1,0:T(4,128)(2,1)S(1)}, u32[]{:S(2)}, u32[]{:S(2)}) collective-permute-start(bf16[16,4,256]{2,1,0:T(4,128)(2,1)S(1)} %get-tuple-element.11), channel_id=1, source_target_pairs={{0,16},{16,32},{32,48},{48,64},{64,80},{80,96},{96,112},{112,128},... | collective-permute-start | bytes 98312 | tf_op jit(solution)/shard_map/ppermute | solution.py:33
  2.7 8.6 %collective-permute-start.1 = (bf16[16,4,256]{2,1,0:T(4,128)(2,1)S(1)}, bf16[16,4,256]{2,1,0:T(4,128)(2,1)S(1)}, u32[]{:S(2)}, u32[]{:S(2)}) collective-permute-start(bf16[16,4,256]{2,1,0:T(4,128)(2,1)S(1)} %get-tuple-element.12), channel_id=1, source_target_pairs={{16,0},{32,16},{48,32},{64,48},{80,64},{96,80},{112,96},{128,112},... | collective-permute-start | bytes 98312 | tf_op jit(solution)/shard_map/ppermute | solution.py:35
  81.2 3.7 %copy-start = (f32[8,24,4096]{2,1,0:T(8,128)S(1)}, f32[8,24,4096]{2,1,0:T(8,128)}, u32[]{:S(2)}) copy-start(f32[8,24,4096]{2,1,0:T(8,128)} %shard_map.57) | copy-start | bytes 9437188

commit v12 on v10

--- a/solution.py
+++ b/solution.py
@@ -13,6 +13,7 @@
 NANG = 3600
 BLOCK = 64
 LANES = 128
+GATHER_CHUNKS = 2
 ITERS = 2
 
 
@@ -57,57 +58,68 @@
     right = device(half, place + 1)
     left = device(half, place - 1)
 
-    def slot(index):
-        return out_ref.at[:, :, pl.ds(pl.multiple_of(index * width, width), width)]
+    chunks = GATHER_CHUNKS
+    chunk_rows = local_ref.shape[0] // chunks
+
+    def rows_of(chunk):
+        return pl.ds(chunk * chunk_rows, chunk_rows)
+
+    def slot(index, chunk):
+        columns = pl.ds(pl.multiple_of(index * width, width), width)
+        return out_ref.at[rows_of(chunk), :, columns]
 
     barrier = pltpu.get_barrier_semaphore()
     for peer in (partner, right, left):
         pl.semaphore_signal(barrier, inc=1, device_id=(depth_index, peer), device_id_type=mesh_kind)
     pl.semaphore_wait(barrier, 3)
 
-    own = pltpu.make_async_copy(local_ref, slot(me), own_sem)
+    own = pltpu.make_async_copy(local_ref, out_ref.at[:, :, pl.ds(pl.multiple_of(me * width, width), width)], own_sem)
     own.start()
     sends = []
 
-    def send(source, index, peer):
+    def send(source, index, chunk, peer):
         copy = pltpu.make_async_remote_copy(
             src_ref=source,
-            dst_ref=slot(index),
+            dst_ref=slot(index, chunk),
             send_sem=send_sem.at[len(sends)],
-            recv_sem=recv_sem.at[index],
+            recv_sem=recv_sem.at[index, chunk],
             device_id=(depth_index, peer),
             device_id_type=mesh_kind,
         )
         copy.start()
         sends.append(copy)
 
-    def arrived(index):
+    def arrived(index, chunk):
         pltpu.make_async_remote_copy(
-            src_ref=local_ref,
-            dst_ref=slot(index),
+            src_ref=local_ref.at[rows_of(chunk)],
+            dst_ref=slot(index, chunk),
             send_sem=send_sem.at[0],
-            recv_sem=recv_sem.at[index],
+            recv_sem=recv_sem.at[index, chunk],
             device_id=(depth_index, partner),
             device_id_type=mesh_kind,
         ).wait_recv()
 
-    send(local_ref, me, partner)
-    arrived(partner)
+    for chunk in range(chunks):
+        send(local_ref.at[rows_of(chunk)], me, chunk, partner)
     for step in range(1, forward_steps + 1):
-        for direction, peer, limit in ((-1, right, forward_steps), (1, left, backward_steps)):
-            if step > limit:
-                continue
-            if step == 1:
-                send(local_ref, me, peer)
-                send(slot(partner), partner, peer)
-                continue
-            for half_of in (0, 1):
-                index = device(half_of, place + direction * (step - 1))
-                arrived(index)
-                send(slot(index), index, peer)
+        for chunk in range(chunks):
+            for direction, peer, limit in ((-1, right, forward_steps), (1, left, backward_steps)):
+                if step > limit:
+                    continue
+                if step == 1:
+                    send(local_ref.at[rows_of(chunk)], me, chunk, peer)
+                    if direction == -1:
+                        arrived(partner, chunk)
+                    send(slot(partner, chunk), partner, chunk, peer)
+                    continue
+                for half_of in (0, 1):
+                    index = device(half_of, place + direction * (step - 1))
+                    arrived(index, chunk)
+                    send(slot(index, chunk), index, chunk, peer)
     for direction, steps in ((-1, forward_steps), (1, backward_steps)):
         for half_of in (0, 1):
-            arrived(device(half_of, place + direction * steps))
+            for chunk in range(chunks):
+                arrived(device(half_of, place + direction * steps), chunk)
     own.wait()
     for copy in sends:
         copy.wait_send()
@@ -122,8 +134,8 @@
         in_specs=[pl.BlockSpec(memory_space=pl.ANY)],
         out_specs=pl.BlockSpec(memory_space=pl.ANY),
         scratch_shapes=[
-            pltpu.SemaphoreType.DMA((count,)),
-            pltpu.SemaphoreType.DMA((count,)),
+            pltpu.SemaphoreType.DMA((count * GATHER_CHUNKS,)),
+            pltpu.SemaphoreType.DMA((count, GATHER_CHUNKS)),
             pltpu.SemaphoreType.DMA(()),
         ],
         compiler_params=pltpu.CompilerParams(collective_id=0, has_side_effects=True),

time: 92.8 us -> 91.1 us (0.982)
  Pallas kernels: 69 us -> 67.3 us
    pallas_call x1, Pallas kernels: 25.9 us -> 23.8 us  [gather_columns(): pl.pallas_call(functools.partial(gather_kernel, count), out_shape=jax.Sha...]
where the time goes in v12:
time: 91.1 us; the launch traced here: 90.5 us
  Pallas kernels  67.3 us (74%)
  other arithmetic  14.8 us (16%)
  local copies, waits for them, and re-layouts  4.19 us (5%)
  starting transfers between devices  3.03 us (3%)
    pallas_call x1, Pallas kernels, with_wide_halo(): pl.pallas_call(functools.partial(halo_kernel, count, width), out_shape=[j...  30.9 us
    pallas_call x1, Pallas kernels, gather_columns(): pl.pallas_call(functools.partial(gather_kernel, count), out_shape=jax.Sha...  23.8 us
    pallas_call x1, Pallas kernels, backproject(): pl.pallas_call(backproject_kernel, out_shape=jax.ShapeDtypeStruct((rows,...  12.5 us
    add x2, other arithmetic, smooth_update(): current + step_length * (smooth_weight * divergence - (current - fidelity))  3.13 us
    convert_element_type x1, other arithmetic, footprint_mats(): return weights.astype(jnp.bfloat16)  2.38 us
    mul x2, other arithmetic, smooth_update(): normal_rows = forward_rows * inverse  2.02 us
  transfers between devices with their start and end apart: 2, of which 0 were waited for; matrix products, arithmetic and copies ran while one was open for 8% of the time, Pallas kernels for 0%

profile of v12, /device:TPU:56, one launch (start us, length us, event | category | flops | bytes accessed | tf_op | source)
XLA Modules:
  0.0 90.5 jit_solution(8503710559243379987)
XLA Ops:
  0.0 1.0 %fusion.22 = (bf16[16,4,256]{2,1,0:T(4,128)(2,1)S(1)}, bf16[16,4,256]{2,1,0:T(4,128)(2,1)S(1)}) fusion(bf16[16,8,256]{2,1,0:T(8,128)(2,1)} %param.5), kind=kLoop, calls=%fused_computation.68 | loop fusion | bytes 131072 | tf_op jit(solution)/shard_map/slice | solution.py:31
  1.0 1.7 %collective-permute-start = (bf16[16,4,256]{2,1,0:T(4,128)(2,1)S(1)}, bf16[16,4,256]{2,1,0:T(4,128)(2,1)S(1)}, u32[]{:S(2)}, u32[]{:S(2)}) collective-permute-start(bf16[16,4,256]{2,1,0:T(4,128)(2,1)S(1)} %get-tuple-element.27), channel_id=1, source_target_pairs={{0,16},{16,32},{32,48},{48,64},{64,80},{80,96},{96,112},{112,128},... | collective-permute-start | bytes 98312 | tf_op jit(solution)/shard_map/ppermute | solution.py:34
  2.7 1.3 %collective-permute-start.1 = (bf16[16,4,256]{2,1,0:T(4,128)(2,1)S(1)}, bf16[16,4,256]{2,1,0:T(4,128)(2,1)S(1)}, u32[]{:S(2)}, u32[]{:S(2)}) collective-permute-start(bf16[16,4,256]{2,1,0:T(4,128)(2,1)S(1)} %get-tuple-element.28), channel_id=1, source_target_pairs={{16,0},{32,16},{48,32},{64,48},{80,64},{96,80},{112,96},{128,112},... | collective-permute-start | bytes 98312 | tf_op jit(solution)/shard_map/ppermute | solution.py:36
  4.1 0.7 bitcast_add_fusion
  4.8 0.7 convert_bitcast_fusion
  5.5 0.7 multiply_add_fusion.3
  6.6 0.8 slice.78
  7.5 0.7 fusion.18
  8.3 2.4 %divide_convert_fusion.mats_ref = bf16[16,4,128,128]{3,2,1,0:T(8,128)(2,1)} fusion(f32[16]{0:T(128)S(1)} %get-tuple-element.30, f32[16,4,128]{2,1,0:T(4,128)S(1)} %pad_maximum_fusion, f32[128]{0:T(128)S(1)} %convert_add_fusion.1), kind=kLoop, calls=%fused_computation | loop fusion | flops 7340032 | bytes 2130496 | tf_op jit(solution)/shard_map/vmap()/convert_element_type | solution.py:294
  10.7 0.7 copy.9.shift_ref
  11.4 0.8 convolution_convert_fusion.local_ref
  12.2 23.8 %shard_map.55.columns_ref = bf16[16,8,4096]{2,1,0:T(8,128)(2,1)} custom-call(bf16[16,8,256]{2,1,0:T(8,128)(2,1)} %convolution_convert_fusion.local_ref), custom_call_target="tpu_custom_call" | custom-call | tf_op jit(solution)/shard_map/pallas_call | solution.py:131
  36.1 12.5 %shard_map.56.cells_ref = f32[4,8,4096]{2,1,0:T(8,128)} custom-call(s32[16,4]{1,0:T(8,128)} %copy.9.shift_ref, bf16[16,8,4096]{2,1,0:T(8,128)(2,1)} %shard_map.55.columns_ref, bf16[16,4,128,128]{3,2,1,0:T(8,128)(2,1)} %divide_convert_fusion.mats_ref), custom_call_target="tpu_custom_call" | custom-call | tf_op jit(solution)/shard_map/pallas_call | solution.py:357
  48.6 30.9 %shard_map.57 = (f32[2,2,4096]{2,1,0:T(2,128)}, f32[2,8,4096]{2,1,0:T(8,128)}, f32[2,2,4096]{2,1,0:T(2,128)}, f32[4,2,4096]{2,1,0:T(2,128)}, f32[4,2,4096]{2,1,0...) custom-call(f32[4,8,4096]{2,1,0:T(8,128)} %shard_map.56.cells_ref), custom_call_target="tpu_custom_call" | custom-call | tf_op jit(solution)/shard_map/pallas_call | solution.py:190
  79.5 1.7 %maximum_maximum_fusion = f32[8,12,4096]{2,1,0:T(8,128)S(1)} fusion(f32[2,2,4096]{2,1,0:T(2,128)} %get-tuple-element.20, f32[2,8,4096]{2,1,0:T(8,128)} %get-tuple-element.19, f32[2,2,4096]{2,1,0:T(2,128)} %get-tuple-element.18, f32[4,2,4096]{2,1,0:T(2,128)} %get-tuple-element.17, f32[4,8,4096]{2,1,0:T(8,128)} %shard_map.56.cells_ref, ...), kind=kLoop, calls=%fused_computation.3 | loop fusion | flops 3145728 | bytes 3145728 | tf_op jit(solution)/shard_map/concatenate | solution.py:206
  81.5 0.3 slice_subtract_fusion.1
  81.8 0.6 slice_subtract_fusion
  82.4 1.2 %fusion = (f32[8,12,4096]{2,1,0:T(8,128)S(1)}, f32[8,12,4096]{2,1,0:T(8,128)S(1)}, f32[8,12,4096]{2,1,0:T(8,128)S(1)}) fusion(f32[7,12,4096]{2,1,0:T(8,128)S(1)} %slice_subtract_fusion.2, f32[8]{0:T(128)S(1)} %and_convert_fusion.3, f32[8,12,4095]{2,1,0:T(8,128)S(1)} %slice_subtract_fusion, f32[12]{0:T(128)S(1)} %and_convert_fusion.2, ...), kind=kLoop, calls=%fused_computation.8 | loop fusion | flops 4325376 | bytes 9109200 | tf_op jit(solution)/shard_map/mul | solution.py:265
  83.9 0.8 copy-done
  84.9 1.9 %multiply_add_fusion = f32[8,12,4096]{2,1,0:T(8,128)S(1)} fusion(f32[8,12,4095]{2,1,0:T(8,128)S(1)} %bitcast.14, f32[8,12,4096]{2,1,0:T(8,128)S(1)} %get-tuple-element.22, f32[8,11,4096]{2,1,0:T(8,128)S(1)} %bitcast.15, f32[8,12,4096]{2,1,0:T(8,128)S(1)} %get-tuple-element.23, f32[8,12,4096]{2,1,0:T(8,128)S(1)} %get-tuple-element.21, ...), kind=kLoop, calls=%fused_computation.4 | loop fusion | flops 7077888 | bytes 12254848 | tf_op jit(solution)/shard_map/add | solution.py:281
  87.0 0.5 slice_subtract_fusion.3
  87.9 0.8 fusion.2
  88.8 0.4 pad_subtract_fusion
  89.2 1.2 %fusion.6 = f32[4,8,4096]{2,1,0:T(8,128)} fusion(f32[6,10,4096]{2,1,0:T(8,128)S(1)} %slice.121, f32[6,10,4096]{2,1,0:T(8,128)S(1)} %slice.111, f32[6,10,4095]{2,1,0:T(8,128)S(1)} %bitcast.17, f32[6,10,4096]{2,1,0:T(8,128)S(1)} %get-tuple-element.25, f32[6,10,4096]{2,1,0:T(8,128)S(1)} %pad_subtract_fusion), kind=kLoop, calls=%fused_computation.26 | loop fusion | flops 917504 | bytes 3604240 | tf_op jit(solution)/shard_map/add | solution.py:281
  (44 shorter events, 1.9 us)
Async XLA Ops:
  0.0 11.4 %copy-start.9 = (bf16[16,8,256]{2,1,0:T(8,128)(2,1)S(1)}, bf16[16,8,256]{2,1,0:T(8,128)(2,1)}, u32[]{:S(2)}) copy-start(bf16[16,8,256]{2,1,0:T(8,128)(2,1)} %param.5) | copy-start | bytes 196612
  1.0 10.4 %collective-permute-start = (bf16[16,4,256]{2,1,0:T(4,128)(2,1)S(1)}, bf16[16,4,256]{2,1,0:T(4,128)(2,1)S(1)}, u32[]{:S(2)}, u32[]{:S(2)}) collective-permute-start(bf16[16,4,256]{2,1,0:T(4,128)(2,1)S(1)} %get-tuple-element.27), channel_id=1, source_target_pairs={{0,16},{16,32},{32,48},{48,64},{64,80},{80,96},{96,112},{112,128},... | collective-permute-start | bytes 98312 | tf_op jit(solution)/shard_map/ppermute | solution.py:34
  2.7 8.6 %collective-permute-start.1 = (bf16[16,4,256]{2,1,0:T(4,128)(2,1)S(1)}, bf16[16,4,256]{2,1,0:T(4,128)(2,1)S(1)}, u32[]{:S(2)}, u32[]{:S(2)}) collective-permute-start(bf16[16,4,256]{2,1,0:T(4,128)(2,1)S(1)} %get-tuple-element.28), channel_id=1, source_target_pairs={{16,0},{32,16},{48,32},{64,48},{80,64},{96,80},{112,96},{128,112},... | collective-permute-start | bytes 98312 | tf_op jit(solution)/shard_map/ppermute | solution.py:36
  83.6 1.0 %copy-start = (f32[4,8,4096]{2,1,0:T(8,128)S(1)}, f32[4,8,4096]{2,1,0:T(8,128)}, u32[]{:S(2)}) copy-start(f32[4,8,4096]{2,1,0:T(8,128)} %shard_map.56.cells_ref) | copy-start | bytes 1572868
  83.6 1.1 %copy-start.1 = (f32[2,8,4096]{2,1,0:T(8,128)S(1)}, f32[2,8,4096]{2,1,0:T(8,128)}, u32[]{:S(2)}) copy-start(f32[2,8,4096]{2,1,0:T(8,128)} %get-tuple-element.14) | copy-start | bytes 786436
  83.6 1.2 %copy-start.2 = (f32[2,8,4096]{2,1,0:T(8,128)S(1)}, f32[2,8,4096]{2,1,0:T(8,128)}, u32[]{:S(2)}) copy-start(f32[2,8,4096]{2,1,0:T(8,128)} %get-tuple-element.19) | copy-start | bytes 786436
  83.7 1.2 %copy-start.3 = (f32[4,2,4096]{2,1,0:T(2,128)S(1)}, f32[4,2,4096]{2,1,0:T(2,128)}, u32[]{:S(2)}) copy-start(f32[4,2,4096]{2,1,0:T(2,128)} %get-tuple-element.16) | copy-start | bytes 393220
  83.7 1.2 %copy-start.4 = (f32[4,2,4096]{2,1,0:T(2,128)S(1)}, f32[4,2,4096]{2,1,0:T(2,128)}, u32[]{:S(2)}) copy-start(f32[4,2,4096]{2,1,0:T(2,128)} %get-tuple-element.17) | copy-start | bytes 393220
  83.7 1.2 %copy-start.5 = (f32[2,2,4096]{2,1,0:T(2,128)S(1)}, f32[2,2,4096]{2,1,0:T(2,128)}, u32[]{:S(2)}) copy-start(f32[2,2,4096]{2,1,0:T(2,128)} %get-tuple-element.13) | copy-start | bytes 196612
  83.7 1.2 %copy-start.6 = (f32[2,2,4096]{2,1,0:T(2,128)S(1)}, f32[2,2,4096]{2,1,0:T(2,128)}, u32[]{:S(2)}) copy-start(f32[2,2,4096]{2,1,0:T(2,128)} %get-tuple-element.15) | copy-start | bytes 196612
  83.7 1.2 %copy-start.7 = (f32[2,2,4096]{2,1,0:T(2,128)S(1)}, f32[2,2,4096]{2,1,0:T(2,128)}, u32[]{:S(2)}) copy-start(f32[2,2,4096]{2,1,0:T(2,128)} %get-tuple-element.18) | copy-start | bytes 196612
  83.7 1.2 %copy-start.8 = (f32[2,2,4096]{2,1,0:T(2,128)S(1)}, f32[2,2,4096]{2,1,0:T(2,128)}, u32[]{:S(2)}) copy-start(f32[2,2,4096]{2,1,0:T(2,128)} %get-tuple-element.20) | copy-start | bytes 196612

commit v13 on v12

--- a/solution.py
+++ b/solution.py
@@ -13,7 +13,7 @@
 NANG = 3600
 BLOCK = 64
 LANES = 128
-GATHER_CHUNKS = 2
+GATHER_CHUNKS = 4
 ITERS = 2
 
 

time: 91.1 us -> 91.5 us (level)
  no operation moved by 1% of the time
where the time goes in v13:
time: 91.5 us; the launch traced here: 90.9 us
  Pallas kernels  67.7 us (74%)
  other arithmetic  14.8 us (16%)
  local copies, waits for them, and re-layouts  4.19 us (5%)
  starting transfers between devices  3.03 us (3%)
    pallas_call x1, Pallas kernels, with_wide_halo(): pl.pallas_call(functools.partial(halo_kernel, count, width), out_shape=[j...  31.2 us
    pallas_call x1, Pallas kernels, gather_columns(): pl.pallas_call(functools.partial(gather_kernel, count), out_shape=jax.Sha...  24 us
    pallas_call x1, Pallas kernels, backproject(): pl.pallas_call(backproject_kernel, out_shape=jax.ShapeDtypeStruct((rows,...  12.5 us
    add x2, other arithmetic, smooth_update(): current + step_length * (smooth_weight * divergence - (current - fidelity))  3.13 us
    convert_element_type x1, other arithmetic, footprint_mats(): return weights.astype(jnp.bfloat16)  2.38 us
    mul x2, other arithmetic, smooth_update(): normal_rows = forward_rows * inverse  2.02 us
  transfers between devices with their start and end apart: 2, of which 0 were waited for; matrix products, arithmetic and copies ran while one was open for 8% of the time, Pallas kernels for 0%

profile of v13, /device:TPU:56, one launch (start us, length us, event | category | flops | bytes accessed | tf_op | source)
XLA Modules:
  0.0 90.9 jit_solution(1048640816182246537)
XLA Ops:
  0.0 1.0 %fusion.22 = (bf16[16,4,256]{2,1,0:T(4,128)(2,1)S(1)}, bf16[16,4,256]{2,1,0:T(4,128)(2,1)S(1)}) fusion(bf16[16,8,256]{2,1,0:T(8,128)(2,1)} %param.5), kind=kLoop, calls=%fused_computation.68 | loop fusion | bytes 131072 | tf_op jit(solution)/shard_map/slice | solution.py:31
  1.0 1.7 %collective-permute-start = (bf16[16,4,256]{2,1,0:T(4,128)(2,1)S(1)}, bf16[16,4,256]{2,1,0:T(4,128)(2,1)S(1)}, u32[]{:S(2)}, u32[]{:S(2)}) collective-permute-start(bf16[16,4,256]{2,1,0:T(4,128)(2,1)S(1)} %get-tuple-element.27), channel_id=1, source_target_pairs={{0,16},{16,32},{32,48},{48,64},{64,80},{80,96},{96,112},{112,128},... | collective-permute-start | bytes 98312 | tf_op jit(solution)/shard_map/ppermute | solution.py:34
  2.7 1.3 %collective-permute-start.1 = (bf16[16,4,256]{2,1,0:T(4,128)(2,1)S(1)}, bf16[16,4,256]{2,1,0:T(4,128)(2,1)S(1)}, u32[]{:S(2)}, u32[]{:S(2)}) collective-permute-start(bf16[16,4,256]{2,1,0:T(4,128)(2,1)S(1)} %get-tuple-element.28), channel_id=1, source_target_pairs={{16,0},{32,16},{48,32},{64,48},{80,64},{96,80},{112,96},{128,112},... | collective-permute-start | bytes 98312 | tf_op jit(solution)/shard_map/ppermute | solution.py:36
  4.1 0.7 bitcast_add_fusion
  4.8 0.7 convert_bitcast_fusion
  5.5 0.7 multiply_add_fusion.3
  6.6 0.8 slice.78
  7.5 0.7 fusion.18
  8.3 2.4 %divide_convert_fusion.mats_ref = bf16[16,4,128,128]{3,2,1,0:T(8,128)(2,1)} fusion(f32[16]{0:T(128)S(1)} %get-tuple-element.30, f32[16,4,128]{2,1,0:T(4,128)S(1)} %pad_maximum_fusion, f32[128]{0:T(128)S(1)} %convert_add_fusion.1), kind=kLoop, calls=%fused_computation | loop fusion | flops 7340032 | bytes 2130496 | tf_op jit(solution)/shard_map/vmap()/convert_element_type | solution.py:294
  10.7 0.7 copy.9.shift_ref
  11.4 0.8 convolution_convert_fusion.local_ref
  12.2 24.0 %shard_map.55.columns_ref = bf16[16,8,4096]{2,1,0:T(8,128)(2,1)} custom-call(bf16[16,8,256]{2,1,0:T(8,128)(2,1)} %convolution_convert_fusion.local_ref), custom_call_target="tpu_custom_call" | custom-call | tf_op jit(solution)/shard_map/pallas_call | solution.py:131
  36.2 12.5 %shard_map.56.cells_ref = f32[4,8,4096]{2,1,0:T(8,128)} custom-call(s32[16,4]{1,0:T(8,128)} %copy.9.shift_ref, bf16[16,8,4096]{2,1,0:T(8,128)(2,1)} %shard_map.55.columns_ref, bf16[16,4,128,128]{3,2,1,0:T(8,128)(2,1)} %divide_convert_fusion.mats_ref), custom_call_target="tpu_custom_call" | custom-call | tf_op jit(solution)/shard_map/pallas_call | solution.py:357
  48.7 31.2 %shard_map.57 = (f32[2,2,4096]{2,1,0:T(2,128)}, f32[2,8,4096]{2,1,0:T(8,128)}, f32[2,2,4096]{2,1,0:T(2,128)}, f32[4,2,4096]{2,1,0:T(2,128)}, f32[4,2,4096]{2,1,0...) custom-call(f32[4,8,4096]{2,1,0:T(8,128)} %shard_map.56.cells_ref), custom_call_target="tpu_custom_call" | custom-call | tf_op jit(solution)/shard_map/pallas_call | solution.py:190
  79.9 1.7 %maximum_maximum_fusion = f32[8,12,4096]{2,1,0:T(8,128)S(1)} fusion(f32[2,2,4096]{2,1,0:T(2,128)} %get-tuple-element.20, f32[2,8,4096]{2,1,0:T(8,128)} %get-tuple-element.19, f32[2,2,4096]{2,1,0:T(2,128)} %get-tuple-element.18, f32[4,2,4096]{2,1,0:T(2,128)} %get-tuple-element.17, f32[4,8,4096]{2,1,0:T(8,128)} %shard_map.56.cells_ref, ...), kind=kLoop, calls=%fused_computation.3 | loop fusion | flops 3145728 | bytes 3145728 | tf_op jit(solution)/shard_map/concatenate | solution.py:206
  81.9 0.3 slice_subtract_fusion.1
  82.2 0.6 slice_subtract_fusion
  82.8 1.2 %fusion = (f32[8,12,4096]{2,1,0:T(8,128)S(1)}, f32[8,12,4096]{2,1,0:T(8,128)S(1)}, f32[8,12,4096]{2,1,0:T(8,128)S(1)}) fusion(f32[7,12,4096]{2,1,0:T(8,128)S(1)} %slice_subtract_fusion.2, f32[8]{0:T(128)S(1)} %and_convert_fusion.3, f32[8,12,4095]{2,1,0:T(8,128)S(1)} %slice_subtract_fusion, f32[12]{0:T(128)S(1)} %and_convert_fusion.2, ...), kind=kLoop, calls=%fused_computation.8 | loop fusion | flops 4325376 | bytes 9109200 | tf_op jit(solution)/shard_map/mul | solution.py:265
  84.2 0.8 copy-done
  85.3 1.9 %multiply_add_fusion = f32[8,12,4096]{2,1,0:T(8,128)S(1)} fusion(f32[8,12,4095]{2,1,0:T(8,128)S(1)} %bitcast.14, f32[8,12,4096]{2,1,0:T(8,128)S(1)} %get-tuple-element.22, f32[8,11,4096]{2,1,0:T(8,128)S(1)} %bitcast.15, f32[8,12,4096]{2,1,0:T(8,128)S(1)} %get-tuple-element.23, f32[8,12,4096]{2,1,0:T(8,128)S(1)} %get-tuple-element.21, ...), kind=kLoop, calls=%fused_computation.4 | loop fusion | flops 7077888 | bytes 12254848 | tf_op jit(solution)/shard_map/add | solution.py:281
  87.4 0.5 slice_subtract_fusion.3
  88.3 0.8 fusion.2
  89.2 0.4 pad_subtract_fusion
  89.6 1.2 %fusion.6 = f32[4,8,4096]{2,1,0:T(8,128)} fusion(f32[6,10,4096]{2,1,0:T(8,128)S(1)} %slice.121, f32[6,10,4096]{2,1,0:T(8,128)S(1)} %slice.111, f32[6,10,4095]{2,1,0:T(8,128)S(1)} %bitcast.17, f32[6,10,4096]{2,1,0:T(8,128)S(1)} %get-tuple-element.25, f32[6,10,4096]{2,1,0:T(8,128)S(1)} %pad_subtract_fusion), kind=kLoop, calls=%fused_computation.26 | loop fusion | flops 917504 | bytes 3604240 | tf_op jit(solution)/shard_map/add | solution.py:281
  (44 shorter events, 1.9 us)
Async XLA Ops:
  0.0 11.4 %copy-start.9 = (bf16[16,8,256]{2,1,0:T(8,128)(2,1)S(1)}, bf16[16,8,256]{2,1,0:T(8,128)(2,1)}, u32[]{:S(2)}) copy-start(bf16[16,8,256]{2,1,0:T(8,128)(2,1)} %param.5) | copy-start | bytes 196612
  1.0 10.4 %collective-permute-start = (bf16[16,4,256]{2,1,0:T(4,128)(2,1)S(1)}, bf16[16,4,256]{2,1,0:T(4,128)(2,1)S(1)}, u32[]{:S(2)}, u32[]{:S(2)}) collective-permute-start(bf16[16,4,256]{2,1,0:T(4,128)(2,1)S(1)} %get-tuple-element.27), channel_id=1, source_target_pairs={{0,16},{16,32},{32,48},{48,64},{64,80},{80,96},{96,112},{112,128},... | collective-permute-start | bytes 98312 | tf_op jit(solution)/shard_map/ppermute | solution.py:34
  2.7 8.6 %collective-permute-start.1 = (bf16[16,4,256]{2,1,0:T(4,128)(2,1)S(1)}, bf16[16,4,256]{2,1,0:T(4,128)(2,1)S(1)}, u32[]{:S(2)}, u32[]{:S(2)}) collective-permute-start(bf16[16,4,256]{2,1,0:T(4,128)(2,1)S(1)} %get-tuple-element.28), channel_id=1, source_target_pairs={{16,0},{32,16},{48,32},{64,48},{80,64},{96,80},{112,96},{128,112},... | collective-permute-start | bytes 98312 | tf_op jit(solution)/shard_map/ppermute | solution.py:36
  84.0 1.0 %copy-start = (f32[4,8,4096]{2,1,0:T(8,128)S(1)}, f32[4,8,4096]{2,1,0:T(8,128)}, u32[]{:S(2)}) copy-start(f32[4,8,4096]{2,1,0:T(8,128)} %shard_map.56.cells_ref) | copy-start | bytes 1572868
  84.0 1.1 %copy-start.1 = (f32[2,8,4096]{2,1,0:T(8,128)S(1)}, f32[2,8,4096]{2,1,0:T(8,128)}, u32[]{:S(2)}) copy-start(f32[2,8,4096]{2,1,0:T(8,128)} %get-tuple-element.14) | copy-start | bytes 786436
  84.0 1.2 %copy-start.2 = (f32[2,8,4096]{2,1,0:T(8,128)S(1)}, f32[2,8,4096]{2,1,0:T(8,128)}, u32[]{:S(2)}) copy-start(f32[2,8,4096]{2,1,0:T(8,128)} %get-tuple-element.19) | copy-start | bytes 786436
  84.0 1.2 %copy-start.3 = (f32[4,2,4096]{2,1,0:T(2,128)S(1)}, f32[4,2,4096]{2,1,0:T(2,128)}, u32[]{:S(2)}) copy-start(f32[4,2,4096]{2,1,0:T(2,128)} %get-tuple-element.16) | copy-start | bytes 393220
  84.1 1.2 %copy-start.4 = (f32[4,2,4096]{2,1,0:T(2,128)S(1)}, f32[4,2,4096]{2,1,0:T(2,128)}, u32[]{:S(2)}) copy-start(f32[4,2,4096]{2,1,0:T(2,128)} %get-tuple-element.17) | copy-start | bytes 393220
  84.1 1.2 %copy-start.5 = (f32[2,2,4096]{2,1,0:T(2,128)S(1)}, f32[2,2,4096]{2,1,0:T(2,128)}, u32[]{:S(2)}) copy-start(f32[2,2,4096]{2,1,0:T(2,128)} %get-tuple-element.13) | copy-start | bytes 196612
  84.1 1.2 %copy-start.6 = (f32[2,2,4096]{2,1,0:T(2,128)S(1)}, f32[2,2,4096]{2,1,0:T(2,128)}, u32[]{:S(2)}) copy-start(f32[2,2,4096]{2,1,0:T(2,128)} %get-tuple-element.15) | copy-start | bytes 196612
  84.1 1.2 %copy-start.7 = (f32[2,2,4096]{2,1,0:T(2,128)S(1)}, f32[2,2,4096]{2,1,0:T(2,128)}, u32[]{:S(2)}) copy-start(f32[2,2,4096]{2,1,0:T(2,128)} %get-tuple-element.18) | copy-start | bytes 196612
  84.1 1.2 %copy-start.8 = (f32[2,2,4096]{2,1,0:T(2,128)S(1)}, f32[2,2,4096]{2,1,0:T(2,128)}, u32[]{:S(2)}) copy-start(f32[2,2,4096]{2,1,0:T(2,128)} %get-tuple-element.20) | copy-start | bytes 196612

commit v14 on v12

--- a/solution.py
+++ b/solution.py
@@ -43,7 +43,7 @@
 def gather_kernel(count, local_ref, out_ref, send_sem, recv_sem, own_sem):
     ring = count // 2
     forward_steps = ring // 2
-    backward_steps = ring - 1 - forward_steps
+    backward_steps = (ring - 1) // 2
     me = lax.axis_index("gy")
     depth_index = lax.axis_index("gz")
     half = me // ring
@@ -101,10 +101,19 @@
 
     for chunk in range(chunks):
         send(local_ref.at[rows_of(chunk)], me, chunk, partner)
+    shared = ring - 1 - 2 * backward_steps
+
+    def carried(direction, step, chunk):
+        if step <= backward_steps:
+            return True
+        if shared and step == backward_steps + 1:
+            return chunk == (0 if direction == -1 else chunks - 1)
+        return False
+
     for step in range(1, forward_steps + 1):
         for chunk in range(chunks):
-            for direction, peer, limit in ((-1, right, forward_steps), (1, left, backward_steps)):
-                if step > limit:
+            for direction, peer in ((-1, right), (1, left)):
+                if not carried(direction, step, chunk):
                     continue
                 if step == 1:
                     send(local_ref.at[rows_of(chunk)], me, chunk, peer)
@@ -116,10 +125,15 @@
                     index = device(half_of, place + direction * (step - 1))
                     arrived(index, chunk)
                     send(slot(index, chunk), index, chunk, peer)
-    for direction, steps in ((-1, forward_steps), (1, backward_steps)):
-        for half_of in (0, 1):
+    for direction in (-1, 1):
+        for step in range(1, forward_steps + 1):
             for chunk in range(chunks):
-                arrived(device(half_of, place + direction * steps), chunk)
+                if not carried(direction, step, chunk):
+                    continue
+                if step < forward_steps and carried(direction, step + 1, chunk):
+                    continue
+                for half_of in (0, 1):
+                    arrived(device(half_of, place + direction * step), chunk)
     own.wait()
     for copy in sends:
         copy.wait_send()

time: 91.1 us -> 91.3 us (level)
  no operation moved by 1% of the time
where the time goes in v14:
time: 91.3 us; the launch traced here: 90.7 us
  Pallas kernels  67.5 us (74%)
  other arithmetic  14.8 us (16%)
  local copies, waits for them, and re-layouts  4.19 us (5%)
  starting transfers between devices  3.03 us (3%)
    pallas_call x1, Pallas kernels, with_wide_halo(): pl.pallas_call(functools.partial(halo_kernel, count, width), out_shape=[j...  30.6 us
    pallas_call x1, Pallas kernels, gather_columns(): pl.pallas_call(functools.partial(gather_kernel, count), out_shape=jax.Sha...  24.4 us
    pallas_call x1, Pallas kernels, backproject(): pl.pallas_call(backproject_kernel, out_shape=jax.ShapeDtypeStruct((rows,...  12.5 us
    add x2, other arithmetic, smooth_update(): current + step_length * (smooth_weight * divergence - (current - fidelity))  3.13 us
    convert_element_type x1, other arithmetic, footprint_mats(): return weights.astype(jnp.bfloat16)  2.38 us
    mul x2, other arithmetic, smooth_update(): normal_rows = forward_rows * inverse  2.02 us
  transfers between devices with their start and end apart: 2, of which 0 were waited for; matrix products, arithmetic and copies ran while one was open for 8% of the time, Pallas kernels for 0%

profile of v14, /device:TPU:56, one launch (start us, length us, event | category | flops | bytes accessed | tf_op | source)
XLA Modules:
  0.0 90.7 jit_solution(12330453514720753606)
XLA Ops:
  0.0 1.0 %fusion.22 = (bf16[16,4,256]{2,1,0:T(4,128)(2,1)S(1)}, bf16[16,4,256]{2,1,0:T(4,128)(2,1)S(1)}) fusion(bf16[16,8,256]{2,1,0:T(8,128)(2,1)} %param.5), kind=kLoop, calls=%fused_computation.68 | loop fusion | bytes 131072 | tf_op jit(solution)/shard_map/slice | solution.py:31
  1.0 1.7 %collective-permute-start = (bf16[16,4,256]{2,1,0:T(4,128)(2,1)S(1)}, bf16[16,4,256]{2,1,0:T(4,128)(2,1)S(1)}, u32[]{:S(2)}, u32[]{:S(2)}) collective-permute-start(bf16[16,4,256]{2,1,0:T(4,128)(2,1)S(1)} %get-tuple-element.27), channel_id=1, source_target_pairs={{0,16},{16,32},{32,48},{48,64},{64,80},{80,96},{96,112},{112,128},... | collective-permute-start | bytes 98312 | tf_op jit(solution)/shard_map/ppermute | solution.py:34
  2.7 1.3 %collective-permute-start.1 = (bf16[16,4,256]{2,1,0:T(4,128)(2,1)S(1)}, bf16[16,4,256]{2,1,0:T(4,128)(2,1)S(1)}, u32[]{:S(2)}, u32[]{:S(2)}) collective-permute-start(bf16[16,4,256]{2,1,0:T(4,128)(2,1)S(1)} %get-tuple-element.28), channel_id=1, source_target_pairs={{16,0},{32,16},{48,32},{64,48},{80,64},{96,80},{112,96},{128,112},... | collective-permute-start | bytes 98312 | tf_op jit(solution)/shard_map/ppermute | solution.py:36
  4.1 0.7 bitcast_add_fusion
  4.8 0.7 convert_bitcast_fusion
  5.5 0.7 multiply_add_fusion.3
  6.6 0.8 slice.78
  7.5 0.7 fusion.18
  8.3 2.4 %divide_convert_fusion.mats_ref = bf16[16,4,128,128]{3,2,1,0:T(8,128)(2,1)} fusion(f32[16]{0:T(128)S(1)} %get-tuple-element.30, f32[16,4,128]{2,1,0:T(4,128)S(1)} %pad_maximum_fusion, f32[128]{0:T(128)S(1)} %convert_add_fusion.1), kind=kLoop, calls=%fused_computation | loop fusion | flops 7340032 | bytes 2130496 | tf_op jit(solution)/shard_map/vmap()/convert_element_type | solution.py:308
  10.7 0.7 copy.9.shift_ref
  11.4 0.8 convolution_convert_fusion.local_ref
  12.2 24.4 %shard_map.55.columns_ref = bf16[16,8,4096]{2,1,0:T(8,128)(2,1)} custom-call(bf16[16,8,256]{2,1,0:T(8,128)(2,1)} %convolution_convert_fusion.local_ref), custom_call_target="tpu_custom_call" | custom-call | tf_op jit(solution)/shard_map/pallas_call | solution.py:145
  36.6 12.5 %shard_map.56.cells_ref = f32[4,8,4096]{2,1,0:T(8,128)} custom-call(s32[16,4]{1,0:T(8,128)} %copy.9.shift_ref, bf16[16,8,4096]{2,1,0:T(8,128)(2,1)} %shard_map.55.columns_ref, bf16[16,4,128,128]{3,2,1,0:T(8,128)(2,1)} %divide_convert_fusion.mats_ref), custom_call_target="tpu_custom_call" | custom-call | tf_op jit(solution)/shard_map/pallas_call | solution.py:371
  49.2 30.6 %shard_map.57 = (f32[2,2,4096]{2,1,0:T(2,128)}, f32[2,8,4096]{2,1,0:T(8,128)}, f32[2,2,4096]{2,1,0:T(2,128)}, f32[4,2,4096]{2,1,0:T(2,128)}, f32[4,2,4096]{2,1,0...) custom-call(f32[4,8,4096]{2,1,0:T(8,128)} %shard_map.56.cells_ref), custom_call_target="tpu_custom_call" | custom-call | tf_op jit(solution)/shard_map/pallas_call | solution.py:204
  79.7 1.7 %maximum_maximum_fusion = f32[8,12,4096]{2,1,0:T(8,128)S(1)} fusion(f32[2,2,4096]{2,1,0:T(2,128)} %get-tuple-element.20, f32[2,8,4096]{2,1,0:T(8,128)} %get-tuple-element.19, f32[2,2,4096]{2,1,0:T(2,128)} %get-tuple-element.18, f32[4,2,4096]{2,1,0:T(2,128)} %get-tuple-element.17, f32[4,8,4096]{2,1,0:T(8,128)} %shard_map.56.cells_ref, ...), kind=kLoop, calls=%fused_computation.3 | loop fusion | flops 3145728 | bytes 3145728 | tf_op jit(solution)/shard_map/concatenate | solution.py:220
  81.8 0.3 slice_subtract_fusion.1
  82.0 0.6 slice_subtract_fusion
  82.6 1.2 %fusion = (f32[8,12,4096]{2,1,0:T(8,128)S(1)}, f32[8,12,4096]{2,1,0:T(8,128)S(1)}, f32[8,12,4096]{2,1,0:T(8,128)S(1)}) fusion(f32[7,12,4096]{2,1,0:T(8,128)S(1)} %slice_subtract_fusion.2, f32[8]{0:T(128)S(1)} %and_convert_fusion.3, f32[8,12,4095]{2,1,0:T(8,128)S(1)} %slice_subtract_fusion, f32[12]{0:T(128)S(1)} %and_convert_fusion.2, ...), kind=kLoop, calls=%fused_computation.8 | loop fusion | flops 4325376 | bytes 9109200 | tf_op jit(solution)/shard_map/mul | solution.py:279
  84.1 0.8 copy-done
  85.1 1.9 %multiply_add_fusion = f32[8,12,4096]{2,1,0:T(8,128)S(1)} fusion(f32[8,12,4095]{2,1,0:T(8,128)S(1)} %bitcast.14, f32[8,12,4096]{2,1,0:T(8,128)S(1)} %get-tuple-element.22, f32[8,11,4096]{2,1,0:T(8,128)S(1)} %bitcast.15, f32[8,12,4096]{2,1,0:T(8,128)S(1)} %get-tuple-element.23, f32[8,12,4096]{2,1,0:T(8,128)S(1)} %get-tuple-element.21, ...), kind=kLoop, calls=%fused_computation.4 | loop fusion | flops 7077888 | bytes 12254848 | tf_op jit(solution)/shard_map/add | solution.py:295
  87.2 0.5 slice_subtract_fusion.3
  88.1 0.8 fusion.2
  89.0 0.4 pad_subtract_fusion
  89.4 1.2 %fusion.6 = f32[4,8,4096]{2,1,0:T(8,128)} fusion(f32[6,10,4096]{2,1,0:T(8,128)S(1)} %slice.121, f32[6,10,4096]{2,1,0:T(8,128)S(1)} %slice.111, f32[6,10,4095]{2,1,0:T(8,128)S(1)} %bitcast.17, f32[6,10,4096]{2,1,0:T(8,128)S(1)} %get-tuple-element.25, f32[6,10,4096]{2,1,0:T(8,128)S(1)} %pad_subtract_fusion), kind=kLoop, calls=%fused_computation.26 | loop fusion | flops 917504 | bytes 3604240 | tf_op jit(solution)/shard_map/add | solution.py:295
  (44 shorter events, 1.9 us)
Async XLA Ops:
  0.0 11.4 %copy-start.9 = (bf16[16,8,256]{2,1,0:T(8,128)(2,1)S(1)}, bf16[16,8,256]{2,1,0:T(8,128)(2,1)}, u32[]{:S(2)}) copy-start(bf16[16,8,256]{2,1,0:T(8,128)(2,1)} %param.5) | copy-start | bytes 196612
  1.0 10.4 %collective-permute-start = (bf16[16,4,256]{2,1,0:T(4,128)(2,1)S(1)}, bf16[16,4,256]{2,1,0:T(4,128)(2,1)S(1)}, u32[]{:S(2)}, u32[]{:S(2)}) collective-permute-start(bf16[16,4,256]{2,1,0:T(4,128)(2,1)S(1)} %get-tuple-element.27), channel_id=1, source_target_pairs={{0,16},{16,32},{32,48},{48,64},{64,80},{80,96},{96,112},{112,128},... | collective-permute-start | bytes 98312 | tf_op jit(solution)/shard_map/ppermute | solution.py:34
  2.7 8.6 %collective-permute-start.1 = (bf16[16,4,256]{2,1,0:T(4,128)(2,1)S(1)}, bf16[16,4,256]{2,1,0:T(4,128)(2,1)S(1)}, u32[]{:S(2)}, u32[]{:S(2)}) collective-permute-start(bf16[16,4,256]{2,1,0:T(4,128)(2,1)S(1)} %get-tuple-element.28), channel_id=1, source_target_pairs={{16,0},{32,16},{48,32},{64,48},{80,64},{96,80},{112,96},{128,112},... | collective-permute-start | bytes 98312 | tf_op jit(solution)/shard_map/ppermute | solution.py:36
  83.8 1.0 %copy-start = (f32[4,8,4096]{2,1,0:T(8,128)S(1)}, f32[4,8,4096]{2,1,0:T(8,128)}, u32[]{:S(2)}) copy-start(f32[4,8,4096]{2,1,0:T(8,128)} %shard_map.56.cells_ref) | copy-start | bytes 1572868
  83.9 1.1 %copy-start.1 = (f32[2,8,4096]{2,1,0:T(8,128)S(1)}, f32[2,8,4096]{2,1,0:T(8,128)}, u32[]{:S(2)}) copy-start(f32[2,8,4096]{2,1,0:T(8,128)} %get-tuple-element.14) | copy-start | bytes 786436
  83.9 1.2 %copy-start.2 = (f32[2,8,4096]{2,1,0:T(8,128)S(1)}, f32[2,8,4096]{2,1,0:T(8,128)}, u32[]{:S(2)}) copy-start(f32[2,8,4096]{2,1,0:T(8,128)} %get-tuple-element.19) | copy-start | bytes 786436
  83.9 1.2 %copy-start.3 = (f32[4,2,4096]{2,1,0:T(2,128)S(1)}, f32[4,2,4096]{2,1,0:T(2,128)}, u32[]{:S(2)}) copy-start(f32[4,2,4096]{2,1,0:T(2,128)} %get-tuple-element.16) | copy-start | bytes 393220
  83.9 1.2 %copy-start.4 = (f32[4,2,4096]{2,1,0:T(2,128)S(1)}, f32[4,2,4096]{2,1,0:T(2,128)}, u32[]{:S(2)}) copy-start(f32[4,2,4096]{2,1,0:T(2,128)} %get-tuple-element.17) | copy-start | bytes 393220
  83.9 1.2 %copy-start.5 = (f32[2,2,4096]{2,1,0:T(2,128)S(1)}, f32[2,2,4096]{2,1,0:T(2,128)}, u32[]{:S(2)}) copy-start(f32[2,2,4096]{2,1,0:T(2,128)} %get-tuple-element.13) | copy-start | bytes 196612
  83.9 1.2 %copy-start.6 = (f32[2,2,4096]{2,1,0:T(2,128)S(1)}, f32[2,2,4096]{2,1,0:T(2,128)}, u32[]{:S(2)}) copy-start(f32[2,2,4096]{2,1,0:T(2,128)} %get-tuple-element.15) | copy-start | bytes 196612
  83.9 1.2 %copy-start.7 = (f32[2,2,4096]{2,1,0:T(2,128)S(1)}, f32[2,2,4096]{2,1,0:T(2,128)}, u32[]{:S(2)}) copy-start(f32[2,2,4096]{2,1,0:T(2,128)} %get-tuple-element.18) | copy-start | bytes 196612
  83.9 1.2 %copy-start.8 = (f32[2,2,4096]{2,1,0:T(2,128)S(1)}, f32[2,2,4096]{2,1,0:T(2,128)}, u32[]{:S(2)}) copy-start(f32[2,2,4096]{2,1,0:T(2,128)} %get-tuple-element.20) | copy-start | bytes 196612

commit v15 on v12

--- a/solution.py
+++ b/solution.py
@@ -313,7 +313,7 @@
     second_half = lax.broadcasted_iota(jnp.int32, (LANES, LANES), 1) >= BLOCK
     empty = jnp.zeros((BLOCK, LANES), jnp.bfloat16)
     for row in range(out_ref.shape[0]):
-        shift = shift_ref[p, row]
+        shift = shift_ref[p, row, 2] - 2
         start = (shift + 2) // 2
         odd = jnp.full((LANES, LANES), shift - 2 * (start - 1), jnp.int32) == 1
         whole = mats_ref[0, row]
@@ -351,7 +351,7 @@
 
 
 def backproject(shifts, columns, mats):
-    count, rows = shifts.shape
+    count, rows = shifts.shape[0], shifts.shape[1]
     depth_count, column_count = columns.shape[1], columns.shape[2]
     tile_count = column_count // LANES
     return pl.pallas_call(
@@ -389,9 +389,8 @@
     rows_total = lax.axis_size("gy") * row_count
     depth_total = lax.axis_size("gz") * depth_count
     row_global = (row_base + jnp.arange(row_count)).astype(jnp.float32)
-    shifts = foot_block[:, :, 2] - 2
     mats = jax.vmap(footprint_mats, in_axes=(0, None, None))(angle_index, row_global, rows_total)
-    backprojection = backproject(shifts, columns, mats)
+    backprojection = backproject(foot_block, columns, mats)
     current = backprojection
     extended = with_wide_halo(backprojection, ITERS)
     fidelity = extended

time: 91.1 us -> 89.9 us (0.987)
  local copies, waits for them, and re-layouts: 4.19 us -> 2.58 us
  transfers between devices with their start and end apart: 2 -> 2, of which waited for: 0 -> 0; matrix products, arithmetic and copies ran while one was open for 8% -> 6% of each run, Pallas kernels for 0% -> 0%
where the time goes in v15:
time: 89.9 us; the launch traced here: 89.3 us
  Pallas kernels  67.7 us (75%)
  other arithmetic  14.8 us (16%)
  starting transfers between devices  3.03 us (3%)
  local copies, waits for them, and re-layouts  2.58 us (3%)
    pallas_call x1, Pallas kernels, with_wide_halo(): pl.pallas_call(functools.partial(halo_kernel, count, width), out_shape=[j...  30.9 us
    pallas_call x1, Pallas kernels, gather_columns(): pl.pallas_call(functools.partial(gather_kernel, count), out_shape=jax.Sha...  23.8 us
    pallas_call x1, Pallas kernels, backproject(): pl.pallas_call(backproject_kernel, out_shape=jax.ShapeDtypeStruct((rows,...  12.9 us
    add x2, other arithmetic, smooth_update(): current + step_length * (smooth_weight * divergence - (current - fidelity))  3.13 us
    convert_element_type x1, other arithmetic, footprint_mats(): return weights.astype(jnp.bfloat16)  2.38 us
    mul x2, other arithmetic, smooth_update(): normal_rows = forward_rows * inverse  2.02 us
  transfers between devices with their start and end apart: 2, of which 0 were waited for; matrix products, arithmetic and copies ran while one was open for 6% of the time, Pallas kernels for 0%

profile of v15, /device:TPU:56, one launch (start us, length us, event | category | flops | bytes accessed | tf_op | source)
XLA Modules:
  0.0 89.3 jit_solution(9647170152254980674)
XLA Ops:
  0.0 1.0 %fusion.22 = (bf16[16,4,256]{2,1,0:T(4,128)(2,1)S(1)}, bf16[16,4,256]{2,1,0:T(4,128)(2,1)S(1)}) fusion(bf16[16,8,256]{2,1,0:T(8,128)(2,1)} %param.5), kind=kLoop, calls=%fused_computation.67 | loop fusion | bytes 131072 | tf_op jit(solution)/shard_map/slice | solution.py:31
  1.0 1.7 %collective-permute-start = (bf16[16,4,256]{2,1,0:T(4,128)(2,1)S(1)}, bf16[16,4,256]{2,1,0:T(4,128)(2,1)S(1)}, u32[]{:S(2)}, u32[]{:S(2)}) collective-permute-start(bf16[16,4,256]{2,1,0:T(4,128)(2,1)S(1)} %get-tuple-element.27), channel_id=1, source_target_pairs={{0,16},{16,32},{32,48},{48,64},{64,80},{80,96},{96,112},{112,128},... | collective-permute-start | bytes 98312 | tf_op jit(solution)/shard_map/ppermute | solution.py:34
  2.7 1.3 %collective-permute-start.1 = (bf16[16,4,256]{2,1,0:T(4,128)(2,1)S(1)}, bf16[16,4,256]{2,1,0:T(4,128)(2,1)S(1)}, u32[]{:S(2)}, u32[]{:S(2)}) collective-permute-start(bf16[16,4,256]{2,1,0:T(4,128)(2,1)S(1)} %get-tuple-element.28), channel_id=1, source_target_pairs={{16,0},{32,16},{48,32},{64,48},{80,64},{96,80},{112,96},{128,112},... | collective-permute-start | bytes 98312 | tf_op jit(solution)/shard_map/ppermute | solution.py:36
  4.1 0.7 bitcast_add_fusion
  4.8 0.7 convert_bitcast_fusion
  5.5 0.7 multiply_add_fusion.3
  6.6 0.7 fusion.18
  7.4 2.4 %divide_convert_fusion.mats_ref = bf16[16,4,128,128]{3,2,1,0:T(8,128)(2,1)} fusion(f32[16]{0:T(128)S(1)} %get-tuple-element.30, f32[16,4,128]{2,1,0:T(4,128)S(1)} %pad_maximum_fusion, f32[128]{0:T(128)S(1)} %convert_add_fusion.1), kind=kLoop, calls=%fused_computation | loop fusion | flops 7340032 | bytes 2130496 | tf_op jit(solution)/shard_map/vmap()/convert_element_type | solution.py:294
  9.8 0.8 convolution_convert_fusion.local_ref
  10.6 23.8 %shard_map.55.columns_ref = bf16[16,8,4096]{2,1,0:T(8,128)(2,1)} custom-call(bf16[16,8,256]{2,1,0:T(8,128)(2,1)} %convolution_convert_fusion.local_ref), custom_call_target="tpu_custom_call" | custom-call | tf_op jit(solution)/shard_map/pallas_call | solution.py:131
  34.4 12.9 %shard_map.56.cells_ref = f32[4,8,4096]{2,1,0:T(8,128)} custom-call(s32[16,4,64]{2,1,0:T(4,128)} %shift_ref.1, bf16[16,8,4096]{2,1,0:T(8,128)(2,1)} %shard_map.55.columns_ref, bf16[16,4,128,128]{3,2,1,0:T(8,128)(2,1)} %divide_convert_fusion.mats_ref), custom_call_target="tpu_custom_call" | custom-call | tf_op jit(solution)/shard_map/pallas_call | solution.py:357
  47.4 30.9 %shard_map.57 = (f32[2,2,4096]{2,1,0:T(2,128)}, f32[2,8,4096]{2,1,0:T(8,128)}, f32[2,2,4096]{2,1,0:T(2,128)}, f32[4,2,4096]{2,1,0:T(2,128)}, f32[4,2,4096]{2,1,0...) custom-call(f32[4,8,4096]{2,1,0:T(8,128)} %shard_map.56.cells_ref), custom_call_target="tpu_custom_call" | custom-call | tf_op jit(solution)/shard_map/pallas_call | solution.py:190
  78.3 1.7 %maximum_maximum_fusion = f32[8,12,4096]{2,1,0:T(8,128)S(1)} fusion(f32[2,2,4096]{2,1,0:T(2,128)} %get-tuple-element.20, f32[2,8,4096]{2,1,0:T(8,128)} %get-tuple-element.19, f32[2,2,4096]{2,1,0:T(2,128)} %get-tuple-element.18, f32[4,2,4096]{2,1,0:T(2,128)} %get-tuple-element.17, f32[4,8,4096]{2,1,0:T(8,128)} %shard_map.56.cells_ref, ...), kind=kLoop, calls=%fused_computation.3 | loop fusion | flops 3145728 | bytes 3145728 | tf_op jit(solution)/shard_map/concatenate | solution.py:206
  80.3 0.3 slice_subtract_fusion.1
  80.6 0.6 slice_subtract_fusion
  81.2 1.2 %fusion = (f32[8,12,4096]{2,1,0:T(8,128)S(1)}, f32[8,12,4096]{2,1,0:T(8,128)S(1)}, f32[8,12,4096]{2,1,0:T(8,128)S(1)}) fusion(f32[7,12,4096]{2,1,0:T(8,128)S(1)} %slice_subtract_fusion.2, f32[8]{0:T(128)S(1)} %and_convert_fusion.3, f32[8,12,4095]{2,1,0:T(8,128)S(1)} %slice_subtract_fusion, f32[12]{0:T(128)S(1)} %and_convert_fusion.2, ...), kind=kLoop, calls=%fused_computation.8 | loop fusion | flops 4325376 | bytes 9109200 | tf_op jit(solution)/shard_map/mul | solution.py:265
  82.6 0.8 copy-done
  83.7 1.9 %multiply_add_fusion = f32[8,12,4096]{2,1,0:T(8,128)S(1)} fusion(f32[8,12,4095]{2,1,0:T(8,128)S(1)} %bitcast.12, f32[8,12,4096]{2,1,0:T(8,128)S(1)} %get-tuple-element.22, f32[8,11,4096]{2,1,0:T(8,128)S(1)} %bitcast.13, f32[8,12,4096]{2,1,0:T(8,128)S(1)} %get-tuple-element.23, f32[8,12,4096]{2,1,0:T(8,128)S(1)} %get-tuple-element.21, ...), kind=kLoop, calls=%fused_computation.4 | loop fusion | flops 7077888 | bytes 12254848 | tf_op jit(solution)/shard_map/add | solution.py:281
  85.6 0.2 slice_subtract_fusion.5
  85.8 0.5 slice_subtract_fusion.3
  86.2 0.3 slice_subtract_fusion.4
  86.7 0.8 fusion.2
  87.6 0.4 pad_subtract_fusion
  88.0 1.2 %fusion.6 = f32[4,8,4096]{2,1,0:T(8,128)} fusion(f32[6,10,4096]{2,1,0:T(8,128)S(1)} %slice.117, f32[6,10,4096]{2,1,0:T(8,128)S(1)} %slice.107, f32[6,10,4095]{2,1,0:T(8,128)S(1)} %bitcast.15, f32[6,10,4096]{2,1,0:T(8,128)S(1)} %get-tuple-element.25, f32[6,10,4096]{2,1,0:T(8,128)S(1)} %pad_subtract_fusion), kind=kLoop, calls=%fused_computation.26 | loop fusion | flops 917504 | bytes 3604240 | tf_op jit(solution)/shard_map/add | solution.py:281
  (40 shorter events, 1.4 us)
Async XLA Ops:
  0.0 9.8 %copy-start.9 = (bf16[16,8,256]{2,1,0:T(8,128)(2,1)S(1)}, bf16[16,8,256]{2,1,0:T(8,128)(2,1)}, u32[]{:S(2)}) copy-start(bf16[16,8,256]{2,1,0:T(8,128)(2,1)} %param.5) | copy-start | bytes 196612
  1.0 8.8 %collective-permute-start = (bf16[16,4,256]{2,1,0:T(4,128)(2,1)S(1)}, bf16[16,4,256]{2,1,0:T(4,128)(2,1)S(1)}, u32[]{:S(2)}, u32[]{:S(2)}) collective-permute-start(bf16[16,4,256]{2,1,0:T(4,128)(2,1)S(1)} %get-tuple-element.27), channel_id=1, source_target_pairs={{0,16},{16,32},{32,48},{48,64},{64,80},{80,96},{96,112},{112,128},... | collective-permute-start | bytes 98312 | tf_op jit(solution)/shard_map/ppermute | solution.py:34
  2.7 7.0 %collective-permute-start.1 = (bf16[16,4,256]{2,1,0:T(4,128)(2,1)S(1)}, bf16[16,4,256]{2,1,0:T(4,128)(2,1)S(1)}, u32[]{:S(2)}, u32[]{:S(2)}) collective-permute-start(bf16[16,4,256]{2,1,0:T(4,128)(2,1)S(1)} %get-tuple-element.28), channel_id=1, source_target_pairs={{16,0},{32,16},{48,32},{64,48},{80,64},{96,80},{112,96},{128,112},... | collective-permute-start | bytes 98312 | tf_op jit(solution)/shard_map/ppermute | solution.py:36
  82.4 1.0 %copy-start = (f32[4,8,4096]{2,1,0:T(8,128)S(1)}, f32[4,8,4096]{2,1,0:T(8,128)}, u32[]{:S(2)}) copy-start(f32[4,8,4096]{2,1,0:T(8,128)} %shard_map.56.cells_ref) | copy-start | bytes 1572868
  82.4 1.1 %copy-start.1 = (f32[2,8,4096]{2,1,0:T(8,128)S(1)}, f32[2,8,4096]{2,1,0:T(8,128)}, u32[]{:S(2)}) copy-start(f32[2,8,4096]{2,1,0:T(8,128)} %get-tuple-element.14) | copy-start | bytes 786436
  82.4 1.2 %copy-start.2 = (f32[2,8,4096]{2,1,0:T(8,128)S(1)}, f32[2,8,4096]{2,1,0:T(8,128)}, u32[]{:S(2)}) copy-start(f32[2,8,4096]{2,1,0:T(8,128)} %get-tuple-element.19) | copy-start | bytes 786436
  82.4 1.2 %copy-start.3 = (f32[4,2,4096]{2,1,0:T(2,128)S(1)}, f32[4,2,4096]{2,1,0:T(2,128)}, u32[]{:S(2)}) copy-start(f32[4,2,4096]{2,1,0:T(2,128)} %get-tuple-element.16) | copy-start | bytes 393220
  82.4 1.2 %copy-start.4 = (f32[4,2,4096]{2,1,0:T(2,128)S(1)}, f32[4,2,4096]{2,1,0:T(2,128)}, u32[]{:S(2)}) copy-start(f32[4,2,4096]{2,1,0:T(2,128)} %get-tuple-element.17) | copy-start | bytes 393220
  82.5 1.2 %copy-start.5 = (f32[2,2,4096]{2,1,0:T(2,128)S(1)}, f32[2,2,4096]{2,1,0:T(2,128)}, u32[]{:S(2)}) copy-start(f32[2,2,4096]{2,1,0:T(2,128)} %get-tuple-element.13) | copy-start | bytes 196612
  82.5 1.2 %copy-start.6 = (f32[2,2,4096]{2,1,0:T(2,128)S(1)}, f32[2,2,4096]{2,1,0:T(2,128)}, u32[]{:S(2)}) copy-start(f32[2,2,4096]{2,1,0:T(2,128)} %get-tuple-element.15) | copy-start | bytes 196612
  82.5 1.2 %copy-start.7 = (f32[2,2,4096]{2,1,0:T(2,128)S(1)}, f32[2,2,4096]{2,1,0:T(2,128)}, u32[]{:S(2)}) copy-start(f32[2,2,4096]{2,1,0:T(2,128)} %get-tuple-element.18) | copy-start | bytes 196612
  82.5 1.2 %copy-start.8 = (f32[2,2,4096]{2,1,0:T(2,128)S(1)}, f32[2,2,4096]{2,1,0:T(2,128)}, u32[]{:S(2)}) copy-start(f32[2,2,4096]{2,1,0:T(2,128)} %get-tuple-element.20) | copy-start | bytes 196612

commit v16 on v15

--- a/solution.py
+++ b/solution.py
@@ -140,6 +140,56 @@
         ],
         compiler_params=pltpu.CompilerParams(collective_id=0, has_side_effects=True),
     )(local)
+
+
+def band_kernel(count, width, band_ref, before_ref, after_ref, send_sem, recv_sem):
+    me = lax.axis_index("gz")
+    row_index = lax.axis_index("gy")
+    depth = band_ref.shape[1]
+    mesh_kind = pl.DeviceIdType.MESH
+    below = (lax.rem(me + count - 1, count), row_index)
+    above = (lax.rem(me + 1, count), row_index)
+    barrier = pltpu.get_barrier_semaphore()
+    for peer in (below, above):
+        pl.semaphore_signal(barrier, inc=1, device_id=peer, device_id_type=mesh_kind)
+    pl.semaphore_wait(barrier, 2)
+    up = pltpu.make_async_remote_copy(
+        src_ref=band_ref.at[:, pl.ds(depth - width, width)],
+        dst_ref=before_ref,
+        send_sem=send_sem.at[0],
+        recv_sem=recv_sem.at[0],
+        device_id=above,
+        device_id_type=mesh_kind,
+    )
+    down = pltpu.make_async_remote_copy(
+        src_ref=band_ref.at[:, pl.ds(0, width)],
+        dst_ref=after_ref,
+        send_sem=send_sem.at[1],
+        recv_sem=recv_sem.at[1],
+        device_id=below,
+        device_id_type=mesh_kind,
+    )
+    up.start()
+    down.start()
+    up.wait()
+    down.wait()
+
+
+def with_band_halo(band, width):
+    count = lax.axis_size("gz")
+    me = lax.axis_index("gz")
+    piece = jax.ShapeDtypeStruct((band.shape[0], width, band.shape[2]), band.dtype)
+    before, after = pl.pallas_call(
+        functools.partial(band_kernel, count, width),
+        out_shape=[piece, piece],
+        in_specs=[pl.BlockSpec(memory_space=pl.ANY)],
+        out_specs=[pl.BlockSpec(memory_space=pl.ANY)] * 2,
+        scratch_shapes=[pltpu.SemaphoreType.DMA((2,)), pltpu.SemaphoreType.DMA((2,))],
+        compiler_params=pltpu.CompilerParams(collective_id=2, has_side_effects=True),
+    )(band)
+    before = jnp.where(me > 0, before, jnp.zeros_like(before))
+    after = jnp.where(me < count - 1, after, jnp.zeros_like(after))
+    return jnp.concatenate([before, band, after], axis=1)
 
 
 STEPS = ((1, 1), (1, 0), (1, -1), (0, 1), (0, -1), (-1, 1), (-1, 0), (-1, -1))
@@ -374,7 +424,7 @@
 def per_device(filtered, angle_index, band_offset, band_length, foot_block):
     depth_count = filtered.shape[1]
     row_count = foot_block.shape[1]
-    extended_band = with_halo(filtered, (("gz", 1),), depth_count // 2)
+    extended_band = with_band_halo(filtered, depth_count // 2)
     axial_weights = axial_table(band_offset[:, 0], band_length[:, 0], depth_count)
     summed_rows = jnp.einsum(
         "pzv,pvu->pzu",

time: 89.9 us -> 90.5 us (level)
  starting transfers between devices: 3.03 us -> 0 us
  Pallas kernels: 67.7 us -> 70.6 us
  local copies, waits for them, and re-layouts: 2.58 us -> 1.6 us
    pallas_call x0 -> x1, Pallas kernels: none -> 14 us  [with_band_halo(): pl.pallas_call(functools.partial(band_kernel, count, width), out_shape=[p...]
    pallas_call x1, Pallas kernels: 30.9 us -> 21 us  [with_wide_halo(): pl.pallas_call(functools.partial(halo_kernel, count, width), out_shape=[j...]
    ppermute x2 -> x0, starting transfers between devices: 3.03 us -> none  [the longest x1 1.74 us: with_halo(): lax.ppermute(tail, axis, [(i, (i + 1) % count) for i in range(ends)])]
    pallas_call x1, Pallas kernels: 23.8 us -> 22.7 us  [gather_columns(): pl.pallas_call(functools.partial(gather_kernel, count), out_shape=jax.Sha...]
    slice x1 -> x0, local copies, waits for them, and re-layouts: 0.98 us -> none  [with_halo(): lax.slice_in_dim(cells, cells.shape[dim] - width, cells.shape[dim], axis=...]
  transfers between devices with their start and end apart: 2 -> 0, of which waited for: 0 -> 0; matrix products, arithmetic and copies ran while one was open for 6% -> 0% of each run, Pallas kernels for 0% -> 0%
where the time goes in v16:
time: 90.5 us; the launch traced here: 89.8 us
  Pallas kernels  70.6 us (78%)
  other arithmetic  15.6 us (17%)
  matrix products  1.69 us (2%)
  local copies, waits for them, and re-layouts  1.6 us (2%)
    pallas_call x1, Pallas kernels, gather_columns(): pl.pallas_call(functools.partial(gather_kernel, count), out_shape=jax.Sha...  22.7 us
    pallas_call x1, Pallas kernels, with_wide_halo(): pl.pallas_call(functools.partial(halo_kernel, count, width), out_shape=[j...  21 us
    pallas_call x1, Pallas kernels, with_band_halo(): pl.pallas_call(functools.partial(band_kernel, count, width), out_shape=[p...  14 us
    pallas_call x1, Pallas kernels, backproject(): pl.pallas_call(backproject_kernel, out_shape=jax.ShapeDtypeStruct((rows,...  12.9 us
    add x2, other arithmetic, smooth_update(): current + step_length * (smooth_weight * divergence - (current - fidelity))  3.13 us
    convert_element_type x1, other arithmetic, footprint_mats(): return weights.astype(jnp.bfloat16)  2.37 us
    mul x2, other arithmetic, smooth_update(): normal_rows = forward_rows * inverse  2.02 us

profile of v16, /device:TPU:56, one launch (start us, length us, event | category | flops | bytes accessed | tf_op | source)
XLA Modules:
  0.0 89.8 jit_solution(8401671602814757296)
XLA Ops:
  0.1 0.7 bitcast_add_fusion
  0.8 0.7 convert_bitcast_fusion
  1.4 0.7 fusion.18
  2.2 0.7 multiply_add_fusion.3
  3.3 14.0 %shard_map.55 = (bf16[16,4,256]{2,1,0:T(4,128)(2,1)}, bf16[16,4,256]{2,1,0:T(4,128)(2,1)}) custom-call(bf16[16,8,256]{2,1,0:T(8,128)(2,1)} %band_ref.1), custom_call_target="tpu_custom_call" | custom-call | tf_op jit(solution)/shard_map/pallas_call | solution.py:182
  17.4 0.8 broadcast_select_fusion
  18.2 1.7 %convolution_convert_fusion.local_ref = bf16[16,8,256]{2,1,0:T(8,128)(2,1)} fusion(bf16[16,4,256]{2,1,0:T(4,128)(2,1)S(1)} %get-tuple-element.34, bf16[16,8,256]{2,1,0:T(8,128)(2,1)} %band_ref.1, bf16[16,4,256]{2,1,0:T(4,128)(2,1)S(1)} %get-tuple-element.35, f32[16,8]{1,0:T(8,128)S(1)} %multiply_add_fusion.2, f32[16]{0:T(128)S(1)} %convert_add_fusion.3, ...), kind=kOutput, calls=%fused_computation.22 | convolution fusion | flops 1486848 | bytes 197440 | tf_op jit(solution)/shard_map/pzv,pvu->pzu/dot_general | solution.py:429
  19.8 22.7 %shard_map.56.columns_ref = bf16[16,8,4096]{2,1,0:T(8,128)(2,1)} custom-call(bf16[16,8,256]{2,1,0:T(8,128)(2,1)} %convolution_convert_fusion.local_ref), custom_call_target="tpu_custom_call" | custom-call | tf_op jit(solution)/shard_map/pallas_call | solution.py:131
  42.6 2.4 %divide_convert_fusion.mats_ref = bf16[16,4,128,128]{3,2,1,0:T(8,128)(2,1)} fusion(f32[16]{0:T(128)S(1)} %get-tuple-element.32, f32[16,4,128]{2,1,0:T(4,128)S(1)} %pad_maximum_fusion, f32[128]{0:T(128)S(1)} %convert_add_fusion.1), kind=kLoop, calls=%fused_computation | loop fusion | flops 7340032 | bytes 2130496 | tf_op jit(solution)/shard_map/vmap()/convert_element_type | solution.py:344
  45.0 12.9 %shard_map.57.cells_ref = f32[4,8,4096]{2,1,0:T(8,128)} custom-call(s32[16,4,64]{2,1,0:T(4,128)} %shift_ref.1, bf16[16,8,4096]{2,1,0:T(8,128)(2,1)} %shard_map.56.columns_ref, bf16[16,4,128,128]{3,2,1,0:T(8,128)(2,1)} %divide_convert_fusion.mats_ref), custom_call_target="tpu_custom_call" | custom-call | tf_op jit(solution)/shard_map/pallas_call | solution.py:407
  57.9 21.0 %shard_map.58 = (f32[2,2,4096]{2,1,0:T(2,128)}, f32[2,8,4096]{2,1,0:T(8,128)}, f32[2,2,4096]{2,1,0:T(2,128)}, f32[4,2,4096]{2,1,0:T(2,128)}, f32[4,2,4096]{2,1,0...) custom-call(f32[4,8,4096]{2,1,0:T(8,128)} %shard_map.57.cells_ref), custom_call_target="tpu_custom_call" | custom-call | tf_op jit(solution)/shard_map/pallas_call | solution.py:240
  78.8 1.7 %maximum_maximum_fusion = f32[8,12,4096]{2,1,0:T(8,128)S(1)} fusion(f32[2,2,4096]{2,1,0:T(2,128)} %get-tuple-element.24, f32[2,8,4096]{2,1,0:T(8,128)} %get-tuple-element.23, f32[2,2,4096]{2,1,0:T(2,128)} %get-tuple-element.22, f32[4,2,4096]{2,1,0:T(2,128)} %get-tuple-element.21, f32[4,8,4096]{2,1,0:T(8,128)} %shard_map.57.cells_ref, ...), kind=kLoop, calls=%fused_computation.3 | loop fusion | flops 3145728 | bytes 3145728 | tf_op jit(solution)/shard_map/concatenate | solution.py:256
  80.6 0.1 slice.109
  80.9 0.3 slice_subtract_fusion.1
  81.1 0.6 slice_subtract_fusion
  81.8 1.2 %fusion = (f32[8,12,4096]{2,1,0:T(8,128)S(1)}, f32[8,12,4096]{2,1,0:T(8,128)S(1)}, f32[8,12,4096]{2,1,0:T(8,128)S(1)}) fusion(f32[7,12,4096]{2,1,0:T(8,128)S(1)} %slice_subtract_fusion.2, f32[8]{0:T(128)S(1)} %and_convert_fusion.3, f32[8,12,4095]{2,1,0:T(8,128)S(1)} %slice_subtract_fusion, f32[12]{0:T(128)S(1)} %and_convert_fusion.2, ...), kind=kLoop, calls=%fused_computation.8 | loop fusion | flops 4325376 | bytes 9109200 | tf_op jit(solution)/shard_map/mul | solution.py:315
  83.2 0.8 copy-done
  84.2 1.9 %multiply_add_fusion = f32[8,12,4096]{2,1,0:T(8,128)S(1)} fusion(f32[8,12,4095]{2,1,0:T(8,128)S(1)} %bitcast.12, f32[8,12,4096]{2,1,0:T(8,128)S(1)} %get-tuple-element.26, f32[8,11,4096]{2,1,0:T(8,128)S(1)} %bitcast.13, f32[8,12,4096]{2,1,0:T(8,128)S(1)} %get-tuple-element.27, f32[8,12,4096]{2,1,0:T(8,128)S(1)} %get-tuple-element.25, ...), kind=kLoop, calls=%fused_computation.4 | loop fusion | flops 7077888 | bytes 12254848 | tf_op jit(solution)/shard_map/add | solution.py:331
  86.1 0.2 slice_subtract_fusion.5
  86.3 0.5 slice_subtract_fusion.3
  86.8 0.3 slice_subtract_fusion.4
  87.2 0.8 fusion.2
  88.1 0.4 pad_subtract_fusion
  88.6 1.2 %fusion.6 = f32[4,8,4096]{2,1,0:T(8,128)} fusion(f32[6,10,4096]{2,1,0:T(8,128)S(1)} %slice.109, f32[6,10,4096]{2,1,0:T(8,128)S(1)} %slice.99, f32[6,10,4095]{2,1,0:T(8,128)S(1)} %bitcast.15, f32[6,10,4096]{2,1,0:T(8,128)S(1)} %get-tuple-element.29, f32[6,10,4096]{2,1,0:T(8,128)S(1)} %pad_subtract_fusion), kind=kLoop, calls=%fused_computation.26 | loop fusion | flops 917504 | bytes 3604240 | tf_op jit(solution)/shard_map/add | solution.py:331
  (35 shorter events, 1.2 us)
Async XLA Ops:
  82.9 1.0 %copy-start = (f32[4,8,4096]{2,1,0:T(8,128)S(1)}, f32[4,8,4096]{2,1,0:T(8,128)}, u32[]{:S(2)}) copy-start(f32[4,8,4096]{2,1,0:T(8,128)} %shard_map.57.cells_ref) | copy-start | bytes 1572868
  83.0 1.1 %copy-start.1 = (f32[2,8,4096]{2,1,0:T(8,128)S(1)}, f32[2,8,4096]{2,1,0:T(8,128)}, u32[]{:S(2)}) copy-start(f32[2,8,4096]{2,1,0:T(8,128)} %get-tuple-element.18) | copy-start | bytes 786436
  83.0 1.2 %copy-start.2 = (f32[2,8,4096]{2,1,0:T(8,128)S(1)}, f32[2,8,4096]{2,1,0:T(8,128)}, u32[]{:S(2)}) copy-start(f32[2,8,4096]{2,1,0:T(8,128)} %get-tuple-element.23) | copy-start | bytes 786436
  83.0 1.2 %copy-start.3 = (f32[4,2,4096]{2,1,0:T(2,128)S(1)}, f32[4,2,4096]{2,1,0:T(2,128)}, u32[]{:S(2)}) copy-start(f32[4,2,4096]{2,1,0:T(2,128)} %get-tuple-element.20) | copy-start | bytes 393220
  83.0 1.2 %copy-start.4 = (f32[4,2,4096]{2,1,0:T(2,128)S(1)}, f32[4,2,4096]{2,1,0:T(2,128)}, u32[]{:S(2)}) copy-start(f32[4,2,4096]{2,1,0:T(2,128)} %get-tuple-element.21) | copy-start | bytes 393220
  83.0 1.2 %copy-start.5 = (f32[2,2,4096]{2,1,0:T(2,128)S(1)}, f32[2,2,4096]{2,1,0:T(2,128)}, u32[]{:S(2)}) copy-start(f32[2,2,4096]{2,1,0:T(2,128)} %get-tuple-element.17) | copy-start | bytes 196612
  83.0 1.2 %copy-start.6 = (f32[2,2,4096]{2,1,0:T(2,128)S(1)}, f32[2,2,4096]{2,1,0:T(2,128)}, u32[]{:S(2)}) copy-start(f32[2,2,4096]{2,1,0:T(2,128)} %get-tuple-element.19) | copy-start | bytes 196612
  83.0 1.2 %copy-start.7 = (f32[2,2,4096]{2,1,0:T(2,128)S(1)}, f32[2,2,4096]{2,1,0:T(2,128)}, u32[]{:S(2)}) copy-start(f32[2,2,4096]{2,1,0:T(2,128)} %get-tuple-element.22) | copy-start | bytes 196612
  83.0 1.2 %copy-start.8 = (f32[2,2,4096]{2,1,0:T(2,128)S(1)}, f32[2,2,4096]{2,1,0:T(2,128)}, u32[]{:S(2)}) copy-start(f32[2,2,4096]{2,1,0:T(2,128)} %get-tuple-element.24) | copy-start | bytes 196612

commit v17 on v15

--- a/solution.py
+++ b/solution.py
@@ -371,6 +371,47 @@
     )(shifts, columns, mats)
 
 
+def smooth_inner(current, fidelity, row_first, depth_first, rows_total, depth_total):
+    row_index = row_first + jnp.arange(current.shape[0])
+    depth_index = depth_first + jnp.arange(current.shape[1])
+    keep_rows = ((row_index >= 0) & (row_index < rows_total - 1)).astype(jnp.float32)[:, None, None]
+    keep_depth = ((depth_index >= 0) & (depth_index < depth_total - 1)).astype(jnp.float32)[
+        None, :, None
+    ]
+    rows_here, rows_before = keep_rows[1:-1], keep_rows[:-2]
+    depth_here, depth_before = keep_depth[:, 1:-1], keep_depth[:, :-2]
+
+    def across(cells):
+        return jnp.concatenate([cells[:, :, 1:] - cells[:, :, :-1], jnp.zeros_like(cells[:, :, :1])], 2)
+
+    centre = current[1:-1, 1:-1]
+    row_next, row_prev = current[2:, 1:-1], current[:-2, 1:-1]
+    depth_next, depth_prev = current[1:-1, 2:], current[1:-1, :-2]
+    prev_row_next_depth = current[:-2, 2:]
+    next_row_prev_depth = current[2:, :-2]
+
+    def inverse(a, b, c):
+        return lax.rsqrt(a * a + b * b + c * c + gradient_floor)
+
+    rows_d = (row_next - centre) * rows_here
+    depth_d = (depth_next - centre) * depth_here
+    width_d = across(centre)
+    scale = inverse(rows_d, depth_d, width_d)
+    prev_rows_d = (centre - row_prev) * rows_before
+    prev_scale = inverse(prev_rows_d, (prev_row_next_depth - row_prev) * depth_here, across(row_prev))
+    prev_depth_d = (centre - depth_prev) * depth_before
+    low_scale = inverse(
+        (next_row_prev_depth - depth_prev) * rows_here, prev_depth_d, across(depth_prev)
+    )
+    width_n = width_d * scale
+    divergence = rows_d * scale - prev_rows_d * prev_scale
+    divergence = divergence + depth_d * scale - prev_depth_d * low_scale
+    divergence = divergence + width_n - jnp.concatenate(
+        [jnp.zeros_like(width_n[:, :, :1]), width_n[:, :, :-1]], 2
+    )
+    return centre + step_length * (smooth_weight * divergence - (centre - fidelity[1:-1, 1:-1]))
+
+
 def per_device(filtered, angle_index, band_offset, band_length, foot_block):
     depth_count = filtered.shape[1]
     row_count = foot_block.shape[1]
@@ -397,9 +438,9 @@
     current = extended
     for turn_index in range(ITERS):
         reach = ITERS - turn_index
-        current = smooth_update(
+        current = smooth_inner(
             current, fidelity, row_base - reach, depth_base - reach, rows_total, depth_total
-        )[1:-1, 1:-1]
+        )
         fidelity = fidelity[1:-1, 1:-1]
     return current
 

time: 89.9 us -> 89.6 us (level)
  local copies, waits for them, and re-layouts: 2.58 us -> 1.32 us
  other arithmetic: 14.8 us -> 15.9 us
    add x2, other arithmetic: 3.13 us -> 4.94 us  [smooth_inner(): centre + step_length * (smooth_weight * divergence - (centre - fidelity[1...]
    unnamed x20, local copies, waits for them, and re-layouts: 1.09 us -> 0.04 us
    concatenate x1 -> x2, other arithmetic: 1.72 us -> 2.26 us  [with_wide_halo(): return jnp.concatenate(bands, axis=0)]
    sub x7 -> x3, other arithmetic: 2.3 us -> 1.82 us  [across(): cells[:, :, 1:] - cells[:, :, :-1]]
  transfers between devices with their start and end apart: 2 -> 2, of which waited for: 0 -> 0; matrix products, arithmetic and copies ran while one was open for 6% -> 7% of each run, Pallas kernels for 0% -> 0%
where the time goes in v17:
time: 89.6 us; the launch traced here: 89 us
  Pallas kernels  67.6 us (75%)
  other arithmetic  15.9 us (18%)
  starting transfers between devices  3.03 us (3%)
  local copies, waits for them, and re-layouts  1.32 us (1%)
    pallas_call x1, Pallas kernels, with_wide_halo(): pl.pallas_call(functools.partial(halo_kernel, count, width), out_shape=[j...  30.9 us
    pallas_call x1, Pallas kernels, gather_columns(): pl.pallas_call(functools.partial(gather_kernel, count), out_shape=jax.Sha...  23.8 us
    pallas_call x1, Pallas kernels, backproject(): pl.pallas_call(backproject_kernel, out_shape=jax.ShapeDtypeStruct((rows,...  12.9 us
    add x2, other arithmetic, smooth_inner(): centre + step_length * (smooth_weight * divergence - (centre - fidelity[1...  4.94 us
    convert_element_type x1, other arithmetic, footprint_mats(): return weights.astype(jnp.bfloat16)  2.36 us
    concatenate x2, other arithmetic, with_wide_halo(): return jnp.concatenate(bands, axis=0)  2.26 us
    sub x3, other arithmetic, across(): cells[:, :, 1:] - cells[:, :, :-1]  1.82 us
  transfers between devices with their start and end apart: 2, of which 0 were waited for; matrix products, arithmetic and copies ran while one was open for 7% of the time, Pallas kernels for 0%

profile of v17, /device:TPU:56, one launch (start us, length us, event | category | flops | bytes accessed | tf_op | source)
XLA Modules:
  0.0 89.0 jit_solution(13735763595002706899)
XLA Ops:
  0.0 1.0 %fusion.66 = (bf16[16,4,256]{2,1,0:T(4,128)(2,1)S(1)}, bf16[16,4,256]{2,1,0:T(4,128)(2,1)S(1)}) fusion(bf16[16,8,256]{2,1,0:T(8,128)(2,1)} %param.5), kind=kLoop, calls=%fused_computation.114 | loop fusion | bytes 131072 | tf_op jit(solution)/shard_map/slice | solution.py:31
  1.0 1.7 %collective-permute-start = (bf16[16,4,256]{2,1,0:T(4,128)(2,1)S(1)}, bf16[16,4,256]{2,1,0:T(4,128)(2,1)S(1)}, u32[]{:S(2)}, u32[]{:S(2)}) collective-permute-start(bf16[16,4,256]{2,1,0:T(4,128)(2,1)S(1)} %get-tuple-element.28), channel_id=1, source_target_pairs={{0,16},{16,32},{32,48},{48,64},{64,80},{80,96},{96,112},{112,128},... | collective-permute-start | bytes 98312 | tf_op jit(solution)/shard_map/ppermute | solution.py:34
  2.7 1.3 %collective-permute-start.1 = (bf16[16,4,256]{2,1,0:T(4,128)(2,1)S(1)}, bf16[16,4,256]{2,1,0:T(4,128)(2,1)S(1)}, u32[]{:S(2)}, u32[]{:S(2)}) collective-permute-start(bf16[16,4,256]{2,1,0:T(4,128)(2,1)S(1)} %get-tuple-element.29), channel_id=1, source_target_pairs={{16,0},{32,16},{48,32},{64,48},{80,64},{96,80},{112,96},{128,112},... | collective-permute-start | bytes 98312 | tf_op jit(solution)/shard_map/ppermute | solution.py:36
  4.1 0.7 convert_bitcast_fusion
  4.7 0.7 bitcast_add_fusion
  5.4 0.7 multiply_add_fusion.2
  6.1 0.1 sine_multiply_fusion
  6.3 0.1 broadcast_add_fusion
  6.4 0.1 pad_maximum_fusion
  6.8 0.7 fusion.62
  7.6 2.4 %divide_convert_fusion.mats_ref = bf16[16,4,128,128]{3,2,1,0:T(8,128)(2,1)} fusion(f32[16]{0:T(128)S(1)} %get-tuple-element.39, f32[16,4,128]{2,1,0:T(4,128)S(1)} %pad_maximum_fusion, f32[128]{0:T(128)S(1)} %convert_add_fusion.1), kind=kLoop, calls=%fused_computation | loop fusion | flops 7340032 | bytes 2130496 | tf_op jit(solution)/shard_map/vmap()/convert_element_type | solution.py:294
  10.0 0.8 convolution_convert_fusion.local_ref
  10.9 23.8 %shard_map.55.columns_ref = bf16[16,8,4096]{2,1,0:T(8,128)(2,1)} custom-call(bf16[16,8,256]{2,1,0:T(8,128)(2,1)} %convolution_convert_fusion.local_ref), custom_call_target="tpu_custom_call" | custom-call | tf_op jit(solution)/shard_map/pallas_call | solution.py:131
  34.7 12.9 %shard_map.56.cells_ref = f32[4,8,4096]{2,1,0:T(8,128)} custom-call(s32[16,4,64]{2,1,0:T(4,128)} %shift_ref.1, bf16[16,8,4096]{2,1,0:T(8,128)(2,1)} %shard_map.55.columns_ref, bf16[16,4,128,128]{3,2,1,0:T(8,128)(2,1)} %divide_convert_fusion.mats_ref), custom_call_target="tpu_custom_call" | custom-call | tf_op jit(solution)/shard_map/pallas_call | solution.py:357
  47.6 30.9 %shard_map.57 = (f32[2,2,4096]{2,1,0:T(2,128)}, f32[2,8,4096]{2,1,0:T(8,128)}, f32[2,2,4096]{2,1,0:T(2,128)}, f32[4,2,4096]{2,1,0:T(2,128)}, f32[4,2,4096]{2,1,0...) custom-call(f32[4,8,4096]{2,1,0:T(8,128)} %shard_map.56.cells_ref), custom_call_target="tpu_custom_call" | custom-call | tf_op jit(solution)/shard_map/pallas_call | solution.py:190
  78.6 1.8 %maximum_maximum_fusion = f32[8,12,4096]{2,1,0:T(8,128)S(1)} fusion(f32[2,2,4096]{2,1,0:T(2,128)} %get-tuple-element.20, f32[2,8,4096]{2,1,0:T(8,128)} %get-tuple-element.19, f32[2,2,4096]{2,1,0:T(2,128)} %get-tuple-element.18, f32[4,2,4096]{2,1,0:T(2,128)} %get-tuple-element.17, f32[4,8,4096]{2,1,0:T(8,128)} %shard_map.56.cells_ref, ...), kind=kLoop, calls=%fused_computation.1 | loop fusion | flops 3145728 | bytes 3145728 | tf_op jit(solution)/shard_map/concatenate | solution.py:206
  80.5 0.4 maximum_maximum_fusion.2
  81.0 0.9 slice_subtract_fusion
  81.9 0.5 slice_subtract_fusion.2
  82.3 1.0 %fusion.25 = f32[6,10,4096]{2,1,0:T(8,128)S(1)} fusion(f32[6,10,4095]{2,1,0:T(8,128)S(1)} %get-tuple-element.22, f32[6]{0:T(128)S(1)} %get-tuple-element.35, f32[8,12,4096]{2,1,0:T(8,128)S(1)} %maximum_maximum_fusion, f32[6,12,4096]{2,1,0:T(8,128)S(1)} %get-tuple-element.27, f32[10]{0:T(128)S(1)} %get-tuple-element.37), kind=kLoop, calls=%fused_computation.37 | loop fusion | flops 2703360 | bytes 4915024 | tf_op jit(solution)/shard_map/mul | solution.py:406
  83.3 3.2 %fusion.13 = f32[6,10,4096]{2,1,0:T(8,128)S(1)} fusion(f32[6,12,4096]{2,1,0:T(8,128)S(1)} %get-tuple-element.27, f32[6,12,4096]{2,1,0:T(8,128)S(1)} %get-tuple-element.26, f32[6,10,4095]{2,1,0:T(8,128)S(1)} %bitcast.18, f32[6,10,4095]{2,1,0:T(8,128)S(1)} %get-tuple-element.21, f32[8,12,4096]{2,1,0:T(8,128)S(1)} %maximum_maximum_fusion, ...), kind=kLoop, calls=%fused_computation.17 | loop fusion | flops 11059200 | bytes 11795648 | tf_op jit(solution)/shard_map/add | solution.py:412
  86.5 0.5 slice_subtract_fusion.9
  87.0 0.3 fusion.51
  87.3 1.7 %fusion.39 = f32[4,8,4096]{2,1,0:T(8,128)} fusion(f32[6,10,4096]{2,1,0:T(8,128)S(1)} %fusion.13, f32[4,8,4096]{2,1,0:T(8,128)S(1)} %copy-done, f32[4,8,4095]{2,1,0:T(8,128)S(1)} %bitcast.19, f32[4,8,4095]{2,1,0:T(8,128)S(1)} %get-tuple-element.25, f32[4,8,4095]{2,1,0:T(8,128)S(1)} %get-tuple-element.23, f32[4,8,4095]{2,1,0:T(8,128)S(1)} %get-tuple-element.24, ...), kind=kLoop, calls=%fused_computation.54 | loop fusion | flops 5898240 | bytes 6815328 | tf_op jit(solution)/shard_map/add | solution.py:412
  (37 shorter events, 0.5 us)
Async XLA Ops:
  0.0 10.0 %copy-start.9 = (bf16[16,8,256]{2,1,0:T(8,128)(2,1)S(1)}, bf16[16,8,256]{2,1,0:T(8,128)(2,1)}, u32[]{:S(2)}) copy-start(bf16[16,8,256]{2,1,0:T(8,128)(2,1)} %param.5) | copy-start | bytes 196612
  1.0 9.0 %collective-permute-start = (bf16[16,4,256]{2,1,0:T(4,128)(2,1)S(1)}, bf16[16,4,256]{2,1,0:T(4,128)(2,1)S(1)}, u32[]{:S(2)}, u32[]{:S(2)}) collective-permute-start(bf16[16,4,256]{2,1,0:T(4,128)(2,1)S(1)} %get-tuple-element.28), channel_id=1, source_target_pairs={{0,16},{16,32},{32,48},{48,64},{64,80},{80,96},{96,112},{112,128},... | collective-permute-start | bytes 98312 | tf_op jit(solution)/shard_map/ppermute | solution.py:34
  2.7 7.3 %collective-permute-start.1 = (bf16[16,4,256]{2,1,0:T(4,128)(2,1)S(1)}, bf16[16,4,256]{2,1,0:T(4,128)(2,1)S(1)}, u32[]{:S(2)}, u32[]{:S(2)}) collective-permute-start(bf16[16,4,256]{2,1,0:T(4,128)(2,1)S(1)} %get-tuple-element.29), channel_id=1, source_target_pairs={{16,0},{32,16},{48,32},{64,48},{80,64},{96,80},{112,96},{128,112},... | collective-permute-start | bytes 98312 | tf_op jit(solution)/shard_map/ppermute | solution.py:36
  78.5 1.9 %copy-start = (f32[4,8,4096]{2,1,0:T(8,128)S(1)}, f32[4,8,4096]{2,1,0:T(8,128)}, u32[]{:S(2)}) copy-start(f32[4,8,4096]{2,1,0:T(8,128)} %shard_map.56.cells_ref) | copy-start | bytes 1572868
  78.5 1.9 %copy-start.1 = (f32[2,8,4096]{2,1,0:T(8,128)S(1)}, f32[2,8,4096]{2,1,0:T(8,128)}, u32[]{:S(2)}) copy-start(f32[2,8,4096]{2,1,0:T(8,128)} %get-tuple-element.14) | copy-start | bytes 786436
  78.5 1.9 %copy-start.2 = (f32[2,8,4096]{2,1,0:T(8,128)S(1)}, f32[2,8,4096]{2,1,0:T(8,128)}, u32[]{:S(2)}) copy-start(f32[2,8,4096]{2,1,0:T(8,128)} %get-tuple-element.19) | copy-start | bytes 786436
  78.6 1.9 %copy-start.3 = (f32[4,2,4096]{2,1,0:T(2,128)S(1)}, f32[4,2,4096]{2,1,0:T(2,128)}, u32[]{:S(2)}) copy-start(f32[4,2,4096]{2,1,0:T(2,128)} %get-tuple-element.16) | copy-start | bytes 393220
  78.6 1.9 %copy-start.4 = (f32[4,2,4096]{2,1,0:T(2,128)S(1)}, f32[4,2,4096]{2,1,0:T(2,128)}, u32[]{:S(2)}) copy-start(f32[4,2,4096]{2,1,0:T(2,128)} %get-tuple-element.17) | copy-start | bytes 393220
  78.6 1.9 %copy-start.5 = (f32[2,2,4096]{2,1,0:T(2,128)S(1)}, f32[2,2,4096]{2,1,0:T(2,128)}, u32[]{:S(2)}) copy-start(f32[2,2,4096]{2,1,0:T(2,128)} %get-tuple-element.13) | copy-start | bytes 196612
  78.6 1.9 %copy-start.6 = (f32[2,2,4096]{2,1,0:T(2,128)S(1)}, f32[2,2,4096]{2,1,0:T(2,128)}, u32[]{:S(2)}) copy-start(f32[2,2,4096]{2,1,0:T(2,128)} %get-tuple-element.15) | copy-start | bytes 196612
  78.6 1.9 %copy-start.7 = (f32[2,2,4096]{2,1,0:T(2,128)S(1)}, f32[2,2,4096]{2,1,0:T(2,128)}, u32[]{:S(2)}) copy-start(f32[2,2,4096]{2,1,0:T(2,128)} %get-tuple-element.18) | copy-start | bytes 196612
  78.6 1.9 %copy-start.8 = (f32[2,2,4096]{2,1,0:T(2,128)S(1)}, f32[2,2,4096]{2,1,0:T(2,128)}, u32[]{:S(2)}) copy-start(f32[2,2,4096]{2,1,0:T(2,128)} %get-tuple-element.20) | copy-start | bytes 196612

commit v18 on v17

--- a/solution.py
+++ b/solution.py
@@ -14,6 +14,7 @@
 BLOCK = 64
 LANES = 128
 GATHER_CHUNKS = 2
+PER_STEP = 2
 ITERS = 2
 
 
@@ -304,46 +305,47 @@
         out_ref[...] = jnp.zeros_like(out_ref)
         tiles_ref[...] = jnp.zeros_like(tiles_ref)
 
-    for tile in range(tile_count):
-        tiles_ref[0, tile + 1] = columns_ref[0, :, tile * LANES:(tile + 1) * LANES].astype(
-            jnp.float32
-        )
-
-    ends = jnp.concatenate([tiles_ref[0, 1], tiles_ref[0, tile_count]], axis=0).astype(jnp.bfloat16)
-    second_half = lax.broadcasted_iota(jnp.int32, (LANES, LANES), 1) >= BLOCK
-    empty = jnp.zeros((BLOCK, LANES), jnp.bfloat16)
-    for row in range(out_ref.shape[0]):
-        shift = shift_ref[p, row, 2] - 2
-        start = (shift + 2) // 2
-        odd = jnp.full((LANES, LANES), shift - 2 * (start - 1), jnp.int32) == 1
-        whole = mats_ref[0, row]
-        down = jnp.concatenate([empty, whole[:BLOCK]], axis=0)
-        up = jnp.concatenate([whole[BLOCK:], empty], axis=0)
-        nothing = jnp.zeros_like(whole)
-        first = jnp.where(
-            second_half, jnp.where(odd, nothing, down), jnp.where(odd, down, whole)
-        )
-        second = jnp.where(
-            second_half, jnp.where(odd, whole, up), jnp.where(odd, up, nothing)
-        )
-        low = tiles_ref[0, pl.ds(start, tile_count)].reshape(tile_count * depth_count, LANES)
-        high = tiles_ref[0, pl.ds(start + 1, tile_count)].reshape(tile_count * depth_count, LANES)
-        taps = jnp.concatenate([low, high], axis=1).astype(jnp.bfloat16)
-        result = jnp.dot(
-            taps, jnp.concatenate([first, second], axis=0), preferred_element_type=jnp.float32
-        )
-        edge = jnp.dot(ends, whole, preferred_element_type=jnp.float32)
-        shift_vec = jnp.full((depth_count, LANES), shift, jnp.int32)
+    for step in range(PER_STEP):
         for tile in range(tile_count):
-            part = result[tile * depth_count:(tile + 1) * depth_count]
-            if tile == 0:
-                part = jnp.where(shift_vec < 0, edge[:depth_count], part)
-            elif tile == tile_count - 2:
-                part = jnp.where(shift_vec >= 2, edge[depth_count:], part)
-            elif tile == tile_count - 1:
-                part = jnp.where(shift_vec >= 0, edge[depth_count:], part)
-            lanes = pl.ds(tile * LANES, LANES)
-            out_ref[row, :, lanes] = out_ref[row, :, lanes] + part
+            tiles_ref[0, tile + 1] = columns_ref[step, :, tile * LANES:(tile + 1) * LANES].astype(
+                jnp.float32
+            )
+
+        ends = jnp.concatenate([tiles_ref[0, 1], tiles_ref[0, tile_count]], axis=0).astype(jnp.bfloat16)
+        second_half = lax.broadcasted_iota(jnp.int32, (LANES, LANES), 1) >= BLOCK
+        empty = jnp.zeros((BLOCK, LANES), jnp.bfloat16)
+        for row in range(out_ref.shape[0]):
+            shift = shift_ref[p * PER_STEP + step, row, 2] - 2
+            start = (shift + 2) // 2
+            odd = jnp.full((LANES, LANES), shift - 2 * (start - 1), jnp.int32) == 1
+            whole = mats_ref[step, row]
+            down = jnp.concatenate([empty, whole[:BLOCK]], axis=0)
+            up = jnp.concatenate([whole[BLOCK:], empty], axis=0)
+            nothing = jnp.zeros_like(whole)
+            first = jnp.where(
+                second_half, jnp.where(odd, nothing, down), jnp.where(odd, down, whole)
+            )
+            second = jnp.where(
+                second_half, jnp.where(odd, whole, up), jnp.where(odd, up, nothing)
+            )
+            low = tiles_ref[0, pl.ds(start, tile_count)].reshape(tile_count * depth_count, LANES)
+            high = tiles_ref[0, pl.ds(start + 1, tile_count)].reshape(tile_count * depth_count, LANES)
+            taps = jnp.concatenate([low, high], axis=1).astype(jnp.bfloat16)
+            result = jnp.dot(
+                taps, jnp.concatenate([first, second], axis=0), preferred_element_type=jnp.float32
+            )
+            edge = jnp.dot(ends, whole, preferred_element_type=jnp.float32)
+            shift_vec = jnp.full((depth_count, LANES), shift, jnp.int32)
+            for tile in range(tile_count):
+                part = result[tile * depth_count:(tile + 1) * depth_count]
+                if tile == 0:
+                    part = jnp.where(shift_vec < 0, edge[:depth_count], part)
+                elif tile == tile_count - 2:
+                    part = jnp.where(shift_vec >= 2, edge[depth_count:], part)
+                elif tile == tile_count - 1:
+                    part = jnp.where(shift_vec >= 0, edge[depth_count:], part)
+                lanes = pl.ds(tile * LANES, LANES)
+                out_ref[row, :, lanes] = out_ref[row, :, lanes] + part
 
     @pl.when(p == pl.num_programs(0) - 1)
     def _():
@@ -359,10 +361,10 @@
         out_shape=jax.ShapeDtypeStruct((rows, depth_count, column_count), jnp.float32),
         grid_spec=pltpu.PrefetchScalarGridSpec(
             num_scalar_prefetch=1,
-            grid=(count,),
+            grid=(count // PER_STEP,),
             in_specs=[
-                pl.BlockSpec((1,) + columns.shape[1:], lambda p, s: (p, 0, 0)),
-                pl.BlockSpec((1,) + mats.shape[1:], lambda p, s: (p, 0, 0, 0)),
+                pl.BlockSpec((PER_STEP,) + columns.shape[1:], lambda p, s: (p, 0, 0)),
+                pl.BlockSpec((PER_STEP,) + mats.shape[1:], lambda p, s: (p, 0, 0, 0)),
             ],
             out_specs=pl.BlockSpec((rows, depth_count, column_count), lambda p, s: (0, 0, 0)),
             scratch_shapes=[pltpu.VMEM((1, tile_count + 3, depth_count, LANES), jnp.float32)],

time: 89.6 us -> 85.7 us (0.956)
  Pallas kernels: 67.6 us -> 63.8 us
    pallas_call x1, Pallas kernels: 12.9 us -> 9.1 us  [backproject(): pl.pallas_call(backproject_kernel, out_shape=jax.ShapeDtypeStruct((rows,...]
where the time goes in v18:
time: 85.7 us; the launch traced here: 85.2 us
  Pallas kernels  63.8 us (74%)
  other arithmetic  15.9 us (19%)
  starting transfers between devices  3.03 us (4%)
  local copies, waits for them, and re-layouts  1.32 us (2%)
    pallas_call x1, Pallas kernels, with_wide_halo(): pl.pallas_call(functools.partial(halo_kernel, count, width), out_shape=[j...  30.9 us
    pallas_call x1, Pallas kernels, gather_columns(): pl.pallas_call(functools.partial(gather_kernel, count), out_shape=jax.Sha...  23.8 us
    pallas_call x1, Pallas kernels, backproject(): pl.pallas_call(backproject_kernel, out_shape=jax.ShapeDtypeStruct((rows,...  9.1 us
    add x2, other arithmetic, smooth_inner(): centre + step_length * (smooth_weight * divergence - (centre - fidelity[1...  4.94 us
    convert_element_type x1, other arithmetic, footprint_mats(): return weights.astype(jnp.bfloat16)  2.36 us
    concatenate x2, other arithmetic, with_wide_halo(): return jnp.concatenate(bands, axis=0)  2.26 us
    sub x3, other arithmetic, across(): cells[:, :, 1:] - cells[:, :, :-1]  1.82 us
    ppermute x1, starting transfers between devices, with_halo(): lax.ppermute(tail, axis, [(i, (i + 1) % count) for i in range(ends)])  1.74 us
  transfers between devices with their start and end apart: 2, of which 0 were waited for; matrix products, arithmetic and copies ran while one was open for 7% of the time, Pallas kernels for 0%

profile of v18, /device:TPU:56, one launch (start us, length us, event | category | flops | bytes accessed | tf_op | source)
XLA Modules:
  0.0 85.2 jit_solution(16532757135825101765)
XLA Ops:
  0.0 1.0 %fusion.66 = (bf16[16,4,256]{2,1,0:T(4,128)(2,1)S(1)}, bf16[16,4,256]{2,1,0:T(4,128)(2,1)S(1)}) fusion(bf16[16,8,256]{2,1,0:T(8,128)(2,1)} %param.5), kind=kLoop, calls=%fused_computation.114 | loop fusion | bytes 131072 | tf_op jit(solution)/shard_map/slice | solution.py:32
  1.0 1.7 %collective-permute-start = (bf16[16,4,256]{2,1,0:T(4,128)(2,1)S(1)}, bf16[16,4,256]{2,1,0:T(4,128)(2,1)S(1)}, u32[]{:S(2)}, u32[]{:S(2)}) collective-permute-start(bf16[16,4,256]{2,1,0:T(4,128)(2,1)S(1)} %get-tuple-element.28), channel_id=1, source_target_pairs={{0,16},{16,32},{32,48},{48,64},{64,80},{80,96},{96,112},{112,128},... | collective-permute-start | bytes 98312 | tf_op jit(solution)/shard_map/ppermute | solution.py:35
  2.7 1.3 %collective-permute-start.1 = (bf16[16,4,256]{2,1,0:T(4,128)(2,1)S(1)}, bf16[16,4,256]{2,1,0:T(4,128)(2,1)S(1)}, u32[]{:S(2)}, u32[]{:S(2)}) collective-permute-start(bf16[16,4,256]{2,1,0:T(4,128)(2,1)S(1)} %get-tuple-element.29), channel_id=1, source_target_pairs={{16,0},{32,16},{48,32},{64,48},{80,64},{96,80},{112,96},{128,112},... | collective-permute-start | bytes 98312 | tf_op jit(solution)/shard_map/ppermute | solution.py:37
  4.1 0.7 convert_bitcast_fusion
  4.7 0.7 bitcast_add_fusion
  5.4 0.7 multiply_add_fusion.2
  6.1 0.1 sine_multiply_fusion
  6.3 0.1 broadcast_add_fusion
  6.4 0.1 pad_maximum_fusion
  6.8 0.7 fusion.62
  7.6 2.4 %divide_convert_fusion.mats_ref = bf16[16,4,128,128]{3,2,1,0:T(8,128)(2,1)} fusion(f32[16]{0:T(128)S(1)} %get-tuple-element.39, f32[16,4,128]{2,1,0:T(4,128)S(1)} %pad_maximum_fusion, f32[128]{0:T(128)S(1)} %convert_add_fusion.1), kind=kLoop, calls=%fused_computation | loop fusion | flops 7340032 | bytes 2130496 | tf_op jit(solution)/shard_map/vmap()/convert_element_type | solution.py:295
  10.0 0.8 convolution_convert_fusion.local_ref
  10.9 23.8 %shard_map.55.columns_ref = bf16[16,8,4096]{2,1,0:T(8,128)(2,1)} custom-call(bf16[16,8,256]{2,1,0:T(8,128)(2,1)} %convolution_convert_fusion.local_ref), custom_call_target="tpu_custom_call" | custom-call | tf_op jit(solution)/shard_map/pallas_call | solution.py:132
  34.7 9.1 %shard_map.56.cells_ref = f32[4,8,4096]{2,1,0:T(8,128)} custom-call(s32[16,4,64]{2,1,0:T(4,128)} %shift_ref.1, bf16[16,8,4096]{2,1,0:T(8,128)(2,1)} %shard_map.55.columns_ref, bf16[16,4,128,128]{3,2,1,0:T(8,128)(2,1)} %divide_convert_fusion.mats_ref), custom_call_target="tpu_custom_call" | custom-call | tf_op jit(solution)/shard_map/pallas_call | solution.py:359
  43.8 30.9 %shard_map.57 = (f32[2,2,4096]{2,1,0:T(2,128)}, f32[2,8,4096]{2,1,0:T(8,128)}, f32[2,2,4096]{2,1,0:T(2,128)}, f32[4,2,4096]{2,1,0:T(2,128)}, f32[4,2,4096]{2,1,0...) custom-call(f32[4,8,4096]{2,1,0:T(8,128)} %shard_map.56.cells_ref), custom_call_target="tpu_custom_call" | custom-call | tf_op jit(solution)/shard_map/pallas_call | solution.py:191
  74.8 1.8 %maximum_maximum_fusion = f32[8,12,4096]{2,1,0:T(8,128)S(1)} fusion(f32[2,2,4096]{2,1,0:T(2,128)} %get-tuple-element.20, f32[2,8,4096]{2,1,0:T(8,128)} %get-tuple-element.19, f32[2,2,4096]{2,1,0:T(2,128)} %get-tuple-element.18, f32[4,2,4096]{2,1,0:T(2,128)} %get-tuple-element.17, f32[4,8,4096]{2,1,0:T(8,128)} %shard_map.56.cells_ref, ...), kind=kLoop, calls=%fused_computation.1 | loop fusion | flops 3145728 | bytes 3145728 | tf_op jit(solution)/shard_map/concatenate | solution.py:207
  76.7 0.4 maximum_maximum_fusion.2
  77.1 0.9 %slice_subtract_fusion = (f32[6,10,4095]{2,1,0:T(8,128)S(1)}, f32[6,10,4095]{2,1,0:T(8,128)S(1)}) fusion(f32[8,12,4096]{2,1,0:T(8,128)S(1)} %maximum_maximum_fusion), kind=kLoop, calls=%fused_computation.2 | loop fusion | flops 491400 | bytes 5896800 | tf_op jit(solution)/shard_map/sub | solution.py:387
  78.0 0.5 slice_subtract_fusion.2
  78.5 1.0 %fusion.25 = f32[6,10,4096]{2,1,0:T(8,128)S(1)} fusion(f32[6,10,4095]{2,1,0:T(8,128)S(1)} %get-tuple-element.22, f32[6]{0:T(128)S(1)} %get-tuple-element.35, f32[8,12,4096]{2,1,0:T(8,128)S(1)} %maximum_maximum_fusion, f32[6,12,4096]{2,1,0:T(8,128)S(1)} %get-tuple-element.27, f32[10]{0:T(128)S(1)} %get-tuple-element.37), kind=kLoop, calls=%fused_computation.37 | loop fusion | flops 2703360 | bytes 4915024 | tf_op jit(solution)/shard_map/mul | solution.py:408
  79.5 3.2 %fusion.13 = f32[6,10,4096]{2,1,0:T(8,128)S(1)} fusion(f32[6,12,4096]{2,1,0:T(8,128)S(1)} %get-tuple-element.27, f32[6,12,4096]{2,1,0:T(8,128)S(1)} %get-tuple-element.26, f32[6,10,4095]{2,1,0:T(8,128)S(1)} %bitcast.18, f32[6,10,4095]{2,1,0:T(8,128)S(1)} %get-tuple-element.21, f32[8,12,4096]{2,1,0:T(8,128)S(1)} %maximum_maximum_fusion, ...), kind=kLoop, calls=%fused_computation.17 | loop fusion | flops 11059200 | bytes 11795648 | tf_op jit(solution)/shard_map/add | solution.py:414
  82.7 0.5 slice_subtract_fusion.9
  83.2 0.3 fusion.51
  83.5 1.7 %fusion.39 = f32[4,8,4096]{2,1,0:T(8,128)} fusion(f32[6,10,4096]{2,1,0:T(8,128)S(1)} %fusion.13, f32[4,8,4096]{2,1,0:T(8,128)S(1)} %copy-done, f32[4,8,4095]{2,1,0:T(8,128)S(1)} %bitcast.19, f32[4,8,4095]{2,1,0:T(8,128)S(1)} %get-tuple-element.25, f32[4,8,4095]{2,1,0:T(8,128)S(1)} %get-tuple-element.23, f32[4,8,4095]{2,1,0:T(8,128)S(1)} %get-tuple-element.24, ...), kind=kLoop, calls=%fused_computation.54 | loop fusion | flops 5898240 | bytes 6815328 | tf_op jit(solution)/shard_map/add | solution.py:414
  (37 shorter events, 0.5 us)
Async XLA Ops:
  0.0 10.0 %copy-start.9 = (bf16[16,8,256]{2,1,0:T(8,128)(2,1)S(1)}, bf16[16,8,256]{2,1,0:T(8,128)(2,1)}, u32[]{:S(2)}) copy-start(bf16[16,8,256]{2,1,0:T(8,128)(2,1)} %param.5) | copy-start | bytes 196612
  1.0 9.0 %collective-permute-start = (bf16[16,4,256]{2,1,0:T(4,128)(2,1)S(1)}, bf16[16,4,256]{2,1,0:T(4,128)(2,1)S(1)}, u32[]{:S(2)}, u32[]{:S(2)}) collective-permute-start(bf16[16,4,256]{2,1,0:T(4,128)(2,1)S(1)} %get-tuple-element.28), channel_id=1, source_target_pairs={{0,16},{16,32},{32,48},{48,64},{64,80},{80,96},{96,112},{112,128},... | collective-permute-start | bytes 98312 | tf_op jit(solution)/shard_map/ppermute | solution.py:35
  2.7 7.3 %collective-permute-start.1 = (bf16[16,4,256]{2,1,0:T(4,128)(2,1)S(1)}, bf16[16,4,256]{2,1,0:T(4,128)(2,1)S(1)}, u32[]{:S(2)}, u32[]{:S(2)}) collective-permute-start(bf16[16,4,256]{2,1,0:T(4,128)(2,1)S(1)} %get-tuple-element.29), channel_id=1, source_target_pairs={{16,0},{32,16},{48,32},{64,48},{80,64},{96,80},{112,96},{128,112},... | collective-permute-start | bytes 98312 | tf_op jit(solution)/shard_map/ppermute | solution.py:37
  74.7 1.9 %copy-start = (f32[4,8,4096]{2,1,0:T(8,128)S(1)}, f32[4,8,4096]{2,1,0:T(8,128)}, u32[]{:S(2)}) copy-start(f32[4,8,4096]{2,1,0:T(8,128)} %shard_map.56.cells_ref) | copy-start | bytes 1572868
  74.7 1.9 %copy-start.1 = (f32[2,8,4096]{2,1,0:T(8,128)S(1)}, f32[2,8,4096]{2,1,0:T(8,128)}, u32[]{:S(2)}) copy-start(f32[2,8,4096]{2,1,0:T(8,128)} %get-tuple-element.14) | copy-start | bytes 786436
  74.7 1.9 %copy-start.2 = (f32[2,8,4096]{2,1,0:T(8,128)S(1)}, f32[2,8,4096]{2,1,0:T(8,128)}, u32[]{:S(2)}) copy-start(f32[2,8,4096]{2,1,0:T(8,128)} %get-tuple-element.19) | copy-start | bytes 786436
  74.7 1.9 %copy-start.3 = (f32[4,2,4096]{2,1,0:T(2,128)S(1)}, f32[4,2,4096]{2,1,0:T(2,128)}, u32[]{:S(2)}) copy-start(f32[4,2,4096]{2,1,0:T(2,128)} %get-tuple-element.16) | copy-start | bytes 393220
  74.7 1.9 %copy-start.4 = (f32[4,2,4096]{2,1,0:T(2,128)S(1)}, f32[4,2,4096]{2,1,0:T(2,128)}, u32[]{:S(2)}) copy-start(f32[4,2,4096]{2,1,0:T(2,128)} %get-tuple-element.17) | copy-start | bytes 393220
  74.7 1.9 %copy-start.5 = (f32[2,2,4096]{2,1,0:T(2,128)S(1)}, f32[2,2,4096]{2,1,0:T(2,128)}, u32[]{:S(2)}) copy-start(f32[2,2,4096]{2,1,0:T(2,128)} %get-tuple-element.13) | copy-start | bytes 196612
  74.8 1.9 %copy-start.6 = (f32[2,2,4096]{2,1,0:T(2,128)S(1)}, f32[2,2,4096]{2,1,0:T(2,128)}, u32[]{:S(2)}) copy-start(f32[2,2,4096]{2,1,0:T(2,128)} %get-tuple-element.15) | copy-start | bytes 196612
  74.8 1.9 %copy-start.7 = (f32[2,2,4096]{2,1,0:T(2,128)S(1)}, f32[2,2,4096]{2,1,0:T(2,128)}, u32[]{:S(2)}) copy-start(f32[2,2,4096]{2,1,0:T(2,128)} %get-tuple-element.18) | copy-start | bytes 196612
  74.8 1.9 %copy-start.8 = (f32[2,2,4096]{2,1,0:T(2,128)S(1)}, f32[2,2,4096]{2,1,0:T(2,128)}, u32[]{:S(2)}) copy-start(f32[2,2,4096]{2,1,0:T(2,128)} %get-tuple-element.20) | copy-start | bytes 196612

commit v19 on v18

--- a/solution.py
+++ b/solution.py
@@ -14,7 +14,7 @@
 BLOCK = 64
 LANES = 128
 GATHER_CHUNKS = 2
-PER_STEP = 2
+PER_STEP = 4
 ITERS = 2
 
 

time: 85.7 us -> 83.9 us (0.979)
  Pallas kernels: 63.8 us -> 62 us
    pallas_call x1, Pallas kernels: 9.1 us -> 7.24 us  [backproject(): pl.pallas_call(backproject_kernel, out_shape=jax.ShapeDtypeStruct((rows,...]
where the time goes in v19:
time: 83.9 us; the launch traced here: 83.4 us
  Pallas kernels  62 us (74%)
  other arithmetic  15.9 us (19%)
  starting transfers between devices  3.03 us (4%)
  local copies, waits for them, and re-layouts  1.32 us (2%)
  matrix products  0.85 us (1%)
    pallas_call x1, Pallas kernels, with_wide_halo(): pl.pallas_call(functools.partial(halo_kernel, count, width), out_shape=[j...  30.9 us
    pallas_call x1, Pallas kernels, gather_columns(): pl.pallas_call(functools.partial(gather_kernel, count), out_shape=jax.Sha...  23.8 us
    pallas_call x1, Pallas kernels, backproject(): pl.pallas_call(backproject_kernel, out_shape=jax.ShapeDtypeStruct((rows,...  7.24 us
    add x2, other arithmetic, smooth_inner(): centre + step_length * (smooth_weight * divergence - (centre - fidelity[1...  4.94 us
    convert_element_type x1, other arithmetic, footprint_mats(): return weights.astype(jnp.bfloat16)  2.36 us
    concatenate x2, other arithmetic, with_wide_halo(): return jnp.concatenate(bands, axis=0)  2.26 us
    sub x3, other arithmetic, across(): cells[:, :, 1:] - cells[:, :, :-1]  1.82 us
    ppermute x1, starting transfers between devices, with_halo(): lax.ppermute(tail, axis, [(i, (i + 1) % count) for i in range(ends)])  1.74 us
  transfers between devices with their start and end apart: 2, of which 0 were waited for; matrix products, arithmetic and copies ran while one was open for 7% of the time, Pallas kernels for 0%

profile of v19, /device:TPU:56, one launch (start us, length us, event | category | flops | bytes accessed | tf_op | source)
XLA Modules:
  0.0 83.4 jit_solution(3577410327354935848)
XLA Ops:
  0.0 1.0 %fusion.66 = (bf16[16,4,256]{2,1,0:T(4,128)(2,1)S(1)}, bf16[16,4,256]{2,1,0:T(4,128)(2,1)S(1)}) fusion(bf16[16,8,256]{2,1,0:T(8,128)(2,1)} %param.5), kind=kLoop, calls=%fused_computation.114 | loop fusion | bytes 131072 | tf_op jit(solution)/shard_map/slice | solution.py:32
  1.0 1.7 %collective-permute-start = (bf16[16,4,256]{2,1,0:T(4,128)(2,1)S(1)}, bf16[16,4,256]{2,1,0:T(4,128)(2,1)S(1)}, u32[]{:S(2)}, u32[]{:S(2)}) collective-permute-start(bf16[16,4,256]{2,1,0:T(4,128)(2,1)S(1)} %get-tuple-element.28), channel_id=1, source_target_pairs={{0,16},{16,32},{32,48},{48,64},{64,80},{80,96},{96,112},{112,128},... | collective-permute-start | bytes 98312 | tf_op jit(solution)/shard_map/ppermute | solution.py:35
  2.7 1.3 %collective-permute-start.1 = (bf16[16,4,256]{2,1,0:T(4,128)(2,1)S(1)}, bf16[16,4,256]{2,1,0:T(4,128)(2,1)S(1)}, u32[]{:S(2)}, u32[]{:S(2)}) collective-permute-start(bf16[16,4,256]{2,1,0:T(4,128)(2,1)S(1)} %get-tuple-element.29), channel_id=1, source_target_pairs={{16,0},{32,16},{48,32},{64,48},{80,64},{96,80},{112,96},{128,112},... | collective-permute-start | bytes 98312 | tf_op jit(solution)/shard_map/ppermute | solution.py:37
  4.1 0.7 convert_bitcast_fusion
  4.7 0.7 bitcast_add_fusion
  5.4 0.7 multiply_add_fusion.2
  6.1 0.1 sine_multiply_fusion
  6.3 0.1 broadcast_add_fusion
  6.4 0.1 pad_maximum_fusion
  6.8 0.7 fusion.62
  7.6 2.4 %divide_convert_fusion.mats_ref = bf16[16,4,128,128]{3,2,1,0:T(8,128)(2,1)} fusion(f32[16]{0:T(128)S(1)} %get-tuple-element.39, f32[16,4,128]{2,1,0:T(4,128)S(1)} %pad_maximum_fusion, f32[128]{0:T(128)S(1)} %convert_add_fusion.1), kind=kLoop, calls=%fused_computation | loop fusion | flops 7340032 | bytes 2130496 | tf_op jit(solution)/shard_map/vmap()/convert_element_type | solution.py:295
  10.0 0.8 %convolution_convert_fusion.local_ref = bf16[16,8,256]{2,1,0:T(8,128)(2,1)} fusion(bf16[16,4,256]{2,1,0:T(4,128)(2,1)S(1)} %collective-permute-done.1, bf16[16,8,256]{2,1,0:T(8,128)(2,1)S(1)} %copy-done.9, bf16[16,4,256]{2,1,0:T(4,128)(2,1)S(1)} %collective-permute-done, f32[16,8]{1,0:T(8,128)S(1)} %multiply_add_fusion.1, f32[16]{0:T(128)S(1)} %convert_add_fusion.3, ...), kind=kOutput, calls=%fused_computation.38 | convolution fusion | flops 1486848 | bytes 197440 | tf_op jit(solution)/shard_map/pzv,pvu->pzu/dot_general | solution.py:422
  10.9 23.8 %shard_map.55.columns_ref = bf16[16,8,4096]{2,1,0:T(8,128)(2,1)} custom-call(bf16[16,8,256]{2,1,0:T(8,128)(2,1)} %convolution_convert_fusion.local_ref), custom_call_target="tpu_custom_call" | custom-call | tf_op jit(solution)/shard_map/pallas_call | solution.py:132
  34.7 7.2 %shard_map.56.cells_ref = f32[4,8,4096]{2,1,0:T(8,128)} custom-call(s32[16,4,64]{2,1,0:T(4,128)} %shift_ref.1, bf16[16,8,4096]{2,1,0:T(8,128)(2,1)} %shard_map.55.columns_ref, bf16[16,4,128,128]{3,2,1,0:T(8,128)(2,1)} %divide_convert_fusion.mats_ref), custom_call_target="tpu_custom_call" | custom-call | tf_op jit(solution)/shard_map/pallas_call | solution.py:359
  41.9 30.9 %shard_map.57 = (f32[2,2,4096]{2,1,0:T(2,128)}, f32[2,8,4096]{2,1,0:T(8,128)}, f32[2,2,4096]{2,1,0:T(2,128)}, f32[4,2,4096]{2,1,0:T(2,128)}, f32[4,2,4096]{2,1,0...) custom-call(f32[4,8,4096]{2,1,0:T(8,128)} %shard_map.56.cells_ref), custom_call_target="tpu_custom_call" | custom-call | tf_op jit(solution)/shard_map/pallas_call | solution.py:191
  73.0 1.8 %maximum_maximum_fusion = f32[8,12,4096]{2,1,0:T(8,128)S(1)} fusion(f32[2,2,4096]{2,1,0:T(2,128)} %get-tuple-element.20, f32[2,8,4096]{2,1,0:T(8,128)} %get-tuple-element.19, f32[2,2,4096]{2,1,0:T(2,128)} %get-tuple-element.18, f32[4,2,4096]{2,1,0:T(2,128)} %get-tuple-element.17, f32[4,8,4096]{2,1,0:T(8,128)} %shard_map.56.cells_ref, ...), kind=kLoop, calls=%fused_computation.1 | loop fusion | flops 3145728 | bytes 3145728 | tf_op jit(solution)/shard_map/concatenate | solution.py:207
  74.9 0.4 maximum_maximum_fusion.2
  75.3 0.9 %slice_subtract_fusion = (f32[6,10,4095]{2,1,0:T(8,128)S(1)}, f32[6,10,4095]{2,1,0:T(8,128)S(1)}) fusion(f32[8,12,4096]{2,1,0:T(8,128)S(1)} %maximum_maximum_fusion), kind=kLoop, calls=%fused_computation.2 | loop fusion | flops 491400 | bytes 5896800 | tf_op jit(solution)/shard_map/sub | solution.py:387
  76.2 0.5 slice_subtract_fusion.2
  76.7 1.0 %fusion.25 = f32[6,10,4096]{2,1,0:T(8,128)S(1)} fusion(f32[6,10,4095]{2,1,0:T(8,128)S(1)} %get-tuple-element.22, f32[6]{0:T(128)S(1)} %get-tuple-element.35, f32[8,12,4096]{2,1,0:T(8,128)S(1)} %maximum_maximum_fusion, f32[6,12,4096]{2,1,0:T(8,128)S(1)} %get-tuple-element.27, f32[10]{0:T(128)S(1)} %get-tuple-element.37), kind=kLoop, calls=%fused_computation.37 | loop fusion | flops 2703360 | bytes 4915024 | tf_op jit(solution)/shard_map/mul | solution.py:408
  77.7 3.2 %fusion.13 = f32[6,10,4096]{2,1,0:T(8,128)S(1)} fusion(f32[6,12,4096]{2,1,0:T(8,128)S(1)} %get-tuple-element.27, f32[6,12,4096]{2,1,0:T(8,128)S(1)} %get-tuple-element.26, f32[6,10,4095]{2,1,0:T(8,128)S(1)} %bitcast.18, f32[6,10,4095]{2,1,0:T(8,128)S(1)} %get-tuple-element.21, f32[8,12,4096]{2,1,0:T(8,128)S(1)} %maximum_maximum_fusion, ...), kind=kLoop, calls=%fused_computation.17 | loop fusion | flops 11059200 | bytes 11795648 | tf_op jit(solution)/shard_map/add | solution.py:414
  80.9 0.5 slice_subtract_fusion.9
  81.4 0.3 fusion.51
  81.7 1.7 %fusion.39 = f32[4,8,4096]{2,1,0:T(8,128)} fusion(f32[6,10,4096]{2,1,0:T(8,128)S(1)} %fusion.13, f32[4,8,4096]{2,1,0:T(8,128)S(1)} %copy-done, f32[4,8,4095]{2,1,0:T(8,128)S(1)} %bitcast.19, f32[4,8,4095]{2,1,0:T(8,128)S(1)} %get-tuple-element.25, f32[4,8,4095]{2,1,0:T(8,128)S(1)} %get-tuple-element.23, f32[4,8,4095]{2,1,0:T(8,128)S(1)} %get-tuple-element.24, ...), kind=kLoop, calls=%fused_computation.54 | loop fusion | flops 5898240 | bytes 6815328 | tf_op jit(solution)/shard_map/add | solution.py:414
  (37 shorter events, 0.5 us)
Async XLA Ops:
  0.0 10.0 %copy-start.9 = (bf16[16,8,256]{2,1,0:T(8,128)(2,1)S(1)}, bf16[16,8,256]{2,1,0:T(8,128)(2,1)}, u32[]{:S(2)}) copy-start(bf16[16,8,256]{2,1,0:T(8,128)(2,1)} %param.5) | copy-start | bytes 196612
  1.0 9.0 %collective-permute-start = (bf16[16,4,256]{2,1,0:T(4,128)(2,1)S(1)}, bf16[16,4,256]{2,1,0:T(4,128)(2,1)S(1)}, u32[]{:S(2)}, u32[]{:S(2)}) collective-permute-start(bf16[16,4,256]{2,1,0:T(4,128)(2,1)S(1)} %get-tuple-element.28), channel_id=1, source_target_pairs={{0,16},{16,32},{32,48},{48,64},{64,80},{80,96},{96,112},{112,128},... | collective-permute-start | bytes 98312 | tf_op jit(solution)/shard_map/ppermute | solution.py:35
  2.7 7.3 %collective-permute-start.1 = (bf16[16,4,256]{2,1,0:T(4,128)(2,1)S(1)}, bf16[16,4,256]{2,1,0:T(4,128)(2,1)S(1)}, u32[]{:S(2)}, u32[]{:S(2)}) collective-permute-start(bf16[16,4,256]{2,1,0:T(4,128)(2,1)S(1)} %get-tuple-element.29), channel_id=1, source_target_pairs={{16,0},{32,16},{48,32},{64,48},{80,64},{96,80},{112,96},{128,112},... | collective-permute-start | bytes 98312 | tf_op jit(solution)/shard_map/ppermute | solution.py:37
  72.9 1.9 %copy-start = (f32[4,8,4096]{2,1,0:T(8,128)S(1)}, f32[4,8,4096]{2,1,0:T(8,128)}, u32[]{:S(2)}) copy-start(f32[4,8,4096]{2,1,0:T(8,128)} %shard_map.56.cells_ref) | copy-start | bytes 1572868
  72.9 1.9 %copy-start.1 = (f32[2,8,4096]{2,1,0:T(8,128)S(1)}, f32[2,8,4096]{2,1,0:T(8,128)}, u32[]{:S(2)}) copy-start(f32[2,8,4096]{2,1,0:T(8,128)} %get-tuple-element.14) | copy-start | bytes 786436
  72.9 1.9 %copy-start.2 = (f32[2,8,4096]{2,1,0:T(8,128)S(1)}, f32[2,8,4096]{2,1,0:T(8,128)}, u32[]{:S(2)}) copy-start(f32[2,8,4096]{2,1,0:T(8,128)} %get-tuple-element.19) | copy-start | bytes 786436
  72.9 1.9 %copy-start.3 = (f32[4,2,4096]{2,1,0:T(2,128)S(1)}, f32[4,2,4096]{2,1,0:T(2,128)}, u32[]{:S(2)}) copy-start(f32[4,2,4096]{2,1,0:T(2,128)} %get-tuple-element.16) | copy-start | bytes 393220
  72.9 1.9 %copy-start.4 = (f32[4,2,4096]{2,1,0:T(2,128)S(1)}, f32[4,2,4096]{2,1,0:T(2,128)}, u32[]{:S(2)}) copy-start(f32[4,2,4096]{2,1,0:T(2,128)} %get-tuple-element.17) | copy-start | bytes 393220
  72.9 1.9 %copy-start.5 = (f32[2,2,4096]{2,1,0:T(2,128)S(1)}, f32[2,2,4096]{2,1,0:T(2,128)}, u32[]{:S(2)}) copy-start(f32[2,2,4096]{2,1,0:T(2,128)} %get-tuple-element.13) | copy-start | bytes 196612
  73.0 1.9 %copy-start.6 = (f32[2,2,4096]{2,1,0:T(2,128)S(1)}, f32[2,2,4096]{2,1,0:T(2,128)}, u32[]{:S(2)}) copy-start(f32[2,2,4096]{2,1,0:T(2,128)} %get-tuple-element.15) | copy-start | bytes 196612
  73.0 1.9 %copy-start.7 = (f32[2,2,4096]{2,1,0:T(2,128)S(1)}, f32[2,2,4096]{2,1,0:T(2,128)}, u32[]{:S(2)}) copy-start(f32[2,2,4096]{2,1,0:T(2,128)} %get-tuple-element.18) | copy-start | bytes 196612
  73.0 1.9 %copy-start.8 = (f32[2,2,4096]{2,1,0:T(2,128)S(1)}, f32[2,2,4096]{2,1,0:T(2,128)}, u32[]{:S(2)}) copy-start(f32[2,2,4096]{2,1,0:T(2,128)} %get-tuple-element.20) | copy-start | bytes 196612

commit v20 on v19

--- a/solution.py
+++ b/solution.py
@@ -14,7 +14,7 @@
 BLOCK = 64
 LANES = 128
 GATHER_CHUNKS = 2
-PER_STEP = 4
+PER_STEP = 8
 ITERS = 2
 
 

time: 83.9 us -> 83.6 us (level)
  no operation moved by 1% of the time
where the time goes in v20:
time: 83.6 us; the launch traced here: 83.3 us
  Pallas kernels  61.8 us (74%)
  other arithmetic  15.9 us (19%)
  starting transfers between devices  3.03 us (4%)
  local copies, waits for them, and re-layouts  1.32 us (2%)
  matrix products  0.85 us (1%)
    pallas_call x1, Pallas kernels, with_wide_halo(): pl.pallas_call(functools.partial(halo_kernel, count, width), out_shape=[j...  31 us
    pallas_call x1, Pallas kernels, gather_columns(): pl.pallas_call(functools.partial(gather_kernel, count), out_shape=jax.Sha...  23.8 us
    pallas_call x1, Pallas kernels, backproject(): pl.pallas_call(backproject_kernel, out_shape=jax.ShapeDtypeStruct((rows,...  7.06 us
    add x2, other arithmetic, smooth_inner(): centre + step_length * (smooth_weight * divergence - (centre - fidelity[1...  4.94 us
    convert_element_type x1, other arithmetic, footprint_mats(): return weights.astype(jnp.bfloat16)  2.36 us
    concatenate x2, other arithmetic, with_wide_halo(): return jnp.concatenate(bands, axis=0)  2.26 us
    sub x3, other arithmetic, across(): cells[:, :, 1:] - cells[:, :, :-1]  1.82 us
    ppermute x1, starting transfers between devices, with_halo(): lax.ppermute(tail, axis, [(i, (i + 1) % count) for i in range(ends)])  1.74 us
  transfers between devices with their start and end apart: 2, of which 0 were waited for; matrix products, arithmetic and copies ran while one was open for 7% of the time, Pallas kernels for 0%

profile of v20, /device:TPU:56, one launch (start us, length us, event | category | flops | bytes accessed | tf_op | source)
XLA Modules:
  0.0 83.3 jit_solution(18395669996375695339)
XLA Ops:
  0.0 1.0 %fusion.66 = (bf16[16,4,256]{2,1,0:T(4,128)(2,1)S(1)}, bf16[16,4,256]{2,1,0:T(4,128)(2,1)S(1)}) fusion(bf16[16,8,256]{2,1,0:T(8,128)(2,1)} %param.5), kind=kLoop, calls=%fused_computation.114 | loop fusion | bytes 131072 | tf_op jit(solution)/shard_map/slice | solution.py:32
  1.0 1.7 %collective-permute-start = (bf16[16,4,256]{2,1,0:T(4,128)(2,1)S(1)}, bf16[16,4,256]{2,1,0:T(4,128)(2,1)S(1)}, u32[]{:S(2)}, u32[]{:S(2)}) collective-permute-start(bf16[16,4,256]{2,1,0:T(4,128)(2,1)S(1)} %get-tuple-element.28), channel_id=1, source_target_pairs={{0,16},{16,32},{32,48},{48,64},{64,80},{80,96},{96,112},{112,128},... | collective-permute-start | bytes 98312 | tf_op jit(solution)/shard_map/ppermute | solution.py:35
  2.7 1.3 %collective-permute-start.1 = (bf16[16,4,256]{2,1,0:T(4,128)(2,1)S(1)}, bf16[16,4,256]{2,1,0:T(4,128)(2,1)S(1)}, u32[]{:S(2)}, u32[]{:S(2)}) collective-permute-start(bf16[16,4,256]{2,1,0:T(4,128)(2,1)S(1)} %get-tuple-element.29), channel_id=1, source_target_pairs={{16,0},{32,16},{48,32},{64,48},{80,64},{96,80},{112,96},{128,112},... | collective-permute-start | bytes 98312 | tf_op jit(solution)/shard_map/ppermute | solution.py:37
  4.1 0.7 convert_bitcast_fusion
  4.7 0.7 bitcast_add_fusion
  5.4 0.7 multiply_add_fusion.2
  6.1 0.1 sine_multiply_fusion
  6.3 0.1 broadcast_add_fusion
  6.4 0.1 pad_maximum_fusion
  6.8 0.7 fusion.62
  7.6 2.4 %divide_convert_fusion.mats_ref = bf16[16,4,128,128]{3,2,1,0:T(8,128)(2,1)} fusion(f32[16]{0:T(128)S(1)} %get-tuple-element.39, f32[16,4,128]{2,1,0:T(4,128)S(1)} %pad_maximum_fusion, f32[128]{0:T(128)S(1)} %convert_add_fusion.1), kind=kLoop, calls=%fused_computation | loop fusion | flops 7340032 | bytes 2130496 | tf_op jit(solution)/shard_map/vmap()/convert_element_type | solution.py:295
  10.0 0.8 %convolution_convert_fusion.local_ref = bf16[16,8,256]{2,1,0:T(8,128)(2,1)} fusion(bf16[16,4,256]{2,1,0:T(4,128)(2,1)S(1)} %collective-permute-done.1, bf16[16,8,256]{2,1,0:T(8,128)(2,1)S(1)} %copy-done.9, bf16[16,4,256]{2,1,0:T(4,128)(2,1)S(1)} %collective-permute-done, f32[16,8]{1,0:T(8,128)S(1)} %multiply_add_fusion.1, f32[16]{0:T(128)S(1)} %convert_add_fusion.3, ...), kind=kOutput, calls=%fused_computation.38 | convolution fusion | flops 1486848 | bytes 197440 | tf_op jit(solution)/shard_map/pzv,pvu->pzu/dot_general | solution.py:422
  10.9 23.8 %shard_map.55.columns_ref = bf16[16,8,4096]{2,1,0:T(8,128)(2,1)} custom-call(bf16[16,8,256]{2,1,0:T(8,128)(2,1)} %convolution_convert_fusion.local_ref), custom_call_target="tpu_custom_call" | custom-call | tf_op jit(solution)/shard_map/pallas_call | solution.py:132
  34.7 7.1 %shard_map.56.cells_ref = f32[4,8,4096]{2,1,0:T(8,128)} custom-call(s32[16,4,64]{2,1,0:T(4,128)} %shift_ref.1, bf16[16,8,4096]{2,1,0:T(8,128)(2,1)} %shard_map.55.columns_ref, bf16[16,4,128,128]{3,2,1,0:T(8,128)(2,1)} %divide_convert_fusion.mats_ref), custom_call_target="tpu_custom_call" | custom-call | tf_op jit(solution)/shard_map/pallas_call | solution.py:359
  41.8 31.0 %shard_map.57 = (f32[2,2,4096]{2,1,0:T(2,128)}, f32[2,8,4096]{2,1,0:T(8,128)}, f32[2,2,4096]{2,1,0:T(2,128)}, f32[4,2,4096]{2,1,0:T(2,128)}, f32[4,2,4096]{2,1,0...) custom-call(f32[4,8,4096]{2,1,0:T(8,128)} %shard_map.56.cells_ref), custom_call_target="tpu_custom_call" | custom-call | tf_op jit(solution)/shard_map/pallas_call | solution.py:191
  72.8 1.8 %maximum_maximum_fusion = f32[8,12,4096]{2,1,0:T(8,128)S(1)} fusion(f32[2,2,4096]{2,1,0:T(2,128)} %get-tuple-element.20, f32[2,8,4096]{2,1,0:T(8,128)} %get-tuple-element.19, f32[2,2,4096]{2,1,0:T(2,128)} %get-tuple-element.18, f32[4,2,4096]{2,1,0:T(2,128)} %get-tuple-element.17, f32[4,8,4096]{2,1,0:T(8,128)} %shard_map.56.cells_ref, ...), kind=kLoop, calls=%fused_computation.1 | loop fusion | flops 3145728 | bytes 3145728 | tf_op jit(solution)/shard_map/concatenate | solution.py:207
  74.7 0.4 maximum_maximum_fusion.2
  75.2 0.9 %slice_subtract_fusion = (f32[6,10,4095]{2,1,0:T(8,128)S(1)}, f32[6,10,4095]{2,1,0:T(8,128)S(1)}) fusion(f32[8,12,4096]{2,1,0:T(8,128)S(1)} %maximum_maximum_fusion), kind=kLoop, calls=%fused_computation.2 | loop fusion | flops 491400 | bytes 5896800 | tf_op jit(solution)/shard_map/sub | solution.py:387
  76.1 0.5 slice_subtract_fusion.2
  76.5 1.0 %fusion.25 = f32[6,10,4096]{2,1,0:T(8,128)S(1)} fusion(f32[6,10,4095]{2,1,0:T(8,128)S(1)} %get-tuple-element.22, f32[6]{0:T(128)S(1)} %get-tuple-element.35, f32[8,12,4096]{2,1,0:T(8,128)S(1)} %maximum_maximum_fusion, f32[6,12,4096]{2,1,0:T(8,128)S(1)} %get-tuple-element.27, f32[10]{0:T(128)S(1)} %get-tuple-element.37), kind=kLoop, calls=%fused_computation.37 | loop fusion | flops 2703360 | bytes 4915024 | tf_op jit(solution)/shard_map/mul | solution.py:408
  77.5 3.2 %fusion.13 = f32[6,10,4096]{2,1,0:T(8,128)S(1)} fusion(f32[6,12,4096]{2,1,0:T(8,128)S(1)} %get-tuple-element.27, f32[6,12,4096]{2,1,0:T(8,128)S(1)} %get-tuple-element.26, f32[6,10,4095]{2,1,0:T(8,128)S(1)} %bitcast.18, f32[6,10,4095]{2,1,0:T(8,128)S(1)} %get-tuple-element.21, f32[8,12,4096]{2,1,0:T(8,128)S(1)} %maximum_maximum_fusion, ...), kind=kLoop, calls=%fused_computation.17 | loop fusion | flops 11059200 | bytes 11795648 | tf_op jit(solution)/shard_map/add | solution.py:414
  80.7 0.5 slice_subtract_fusion.9
  81.2 0.3 fusion.51
  81.5 1.7 %fusion.39 = f32[4,8,4096]{2,1,0:T(8,128)} fusion(f32[6,10,4096]{2,1,0:T(8,128)S(1)} %fusion.13, f32[4,8,4096]{2,1,0:T(8,128)S(1)} %copy-done, f32[4,8,4095]{2,1,0:T(8,128)S(1)} %bitcast.19, f32[4,8,4095]{2,1,0:T(8,128)S(1)} %get-tuple-element.25, f32[4,8,4095]{2,1,0:T(8,128)S(1)} %get-tuple-element.23, f32[4,8,4095]{2,1,0:T(8,128)S(1)} %get-tuple-element.24, ...), kind=kLoop, calls=%fused_computation.54 | loop fusion | flops 5898240 | bytes 6815328 | tf_op jit(solution)/shard_map/add | solution.py:414
  (37 shorter events, 0.5 us)
Async XLA Ops:
  0.0 10.0 %copy-start.9 = (bf16[16,8,256]{2,1,0:T(8,128)(2,1)S(1)}, bf16[16,8,256]{2,1,0:T(8,128)(2,1)}, u32[]{:S(2)}) copy-start(bf16[16,8,256]{2,1,0:T(8,128)(2,1)} %param.5) | copy-start | bytes 196612
  1.0 9.0 %collective-permute-start = (bf16[16,4,256]{2,1,0:T(4,128)(2,1)S(1)}, bf16[16,4,256]{2,1,0:T(4,128)(2,1)S(1)}, u32[]{:S(2)}, u32[]{:S(2)}) collective-permute-start(bf16[16,4,256]{2,1,0:T(4,128)(2,1)S(1)} %get-tuple-element.28), channel_id=1, source_target_pairs={{0,16},{16,32},{32,48},{48,64},{64,80},{80,96},{96,112},{112,128},... | collective-permute-start | bytes 98312 | tf_op jit(solution)/shard_map/ppermute | solution.py:35
  2.7 7.3 %collective-permute-start.1 = (bf16[16,4,256]{2,1,0:T(4,128)(2,1)S(1)}, bf16[16,4,256]{2,1,0:T(4,128)(2,1)S(1)}, u32[]{:S(2)}, u32[]{:S(2)}) collective-permute-start(bf16[16,4,256]{2,1,0:T(4,128)(2,1)S(1)} %get-tuple-element.29), channel_id=1, source_target_pairs={{16,0},{32,16},{48,32},{64,48},{80,64},{96,80},{112,96},{128,112},... | collective-permute-start | bytes 98312 | tf_op jit(solution)/shard_map/ppermute | solution.py:37
  72.7 1.9 %copy-start = (f32[4,8,4096]{2,1,0:T(8,128)S(1)}, f32[4,8,4096]{2,1,0:T(8,128)}, u32[]{:S(2)}) copy-start(f32[4,8,4096]{2,1,0:T(8,128)} %shard_map.56.cells_ref) | copy-start | bytes 1572868
  72.7 1.9 %copy-start.1 = (f32[2,8,4096]{2,1,0:T(8,128)S(1)}, f32[2,8,4096]{2,1,0:T(8,128)}, u32[]{:S(2)}) copy-start(f32[2,8,4096]{2,1,0:T(8,128)} %get-tuple-element.14) | copy-start | bytes 786436
  72.8 1.9 %copy-start.2 = (f32[2,8,4096]{2,1,0:T(8,128)S(1)}, f32[2,8,4096]{2,1,0:T(8,128)}, u32[]{:S(2)}) copy-start(f32[2,8,4096]{2,1,0:T(8,128)} %get-tuple-element.19) | copy-start | bytes 786436
  72.8 1.9 %copy-start.3 = (f32[4,2,4096]{2,1,0:T(2,128)S(1)}, f32[4,2,4096]{2,1,0:T(2,128)}, u32[]{:S(2)}) copy-start(f32[4,2,4096]{2,1,0:T(2,128)} %get-tuple-element.16) | copy-start | bytes 393220
  72.8 1.9 %copy-start.4 = (f32[4,2,4096]{2,1,0:T(2,128)S(1)}, f32[4,2,4096]{2,1,0:T(2,128)}, u32[]{:S(2)}) copy-start(f32[4,2,4096]{2,1,0:T(2,128)} %get-tuple-element.17) | copy-start | bytes 393220
  72.8 1.9 %copy-start.5 = (f32[2,2,4096]{2,1,0:T(2,128)S(1)}, f32[2,2,4096]{2,1,0:T(2,128)}, u32[]{:S(2)}) copy-start(f32[2,2,4096]{2,1,0:T(2,128)} %get-tuple-element.13) | copy-start | bytes 196612
  72.8 1.9 %copy-start.6 = (f32[2,2,4096]{2,1,0:T(2,128)S(1)}, f32[2,2,4096]{2,1,0:T(2,128)}, u32[]{:S(2)}) copy-start(f32[2,2,4096]{2,1,0:T(2,128)} %get-tuple-element.15) | copy-start | bytes 196612
  72.8 1.9 %copy-start.7 = (f32[2,2,4096]{2,1,0:T(2,128)S(1)}, f32[2,2,4096]{2,1,0:T(2,128)}, u32[]{:S(2)}) copy-start(f32[2,2,4096]{2,1,0:T(2,128)} %get-tuple-element.18) | copy-start | bytes 196612
  72.8 1.9 %copy-start.8 = (f32[2,2,4096]{2,1,0:T(2,128)S(1)}, f32[2,2,4096]{2,1,0:T(2,128)}, u32[]{:S(2)}) copy-start(f32[2,2,4096]{2,1,0:T(2,128)} %get-tuple-element.20) | copy-start | bytes 196612

commit v21 on v20

--- a/solution.py
+++ b/solution.py
@@ -14,7 +14,7 @@
 BLOCK = 64
 LANES = 128
 GATHER_CHUNKS = 2
-PER_STEP = 8
+PER_STEP = 16
 ITERS = 2
 
 

time: 83.6 us -> 84 us (level)
  no operation moved by 1% of the time
where the time goes in v21:
time: 84 us; the launch traced here: 83.6 us
  Pallas kernels  62.2 us (74%)
  other arithmetic  15.9 us (19%)
  starting transfers between devices  3.03 us (4%)
  local copies, waits for them, and re-layouts  1.32 us (2%)
  matrix products  0.85 us (1%)
    pallas_call x1, Pallas kernels, with_wide_halo(): pl.pallas_call(functools.partial(halo_kernel, count, width), out_shape=[j...  31 us
    pallas_call x1, Pallas kernels, gather_columns(): pl.pallas_call(functools.partial(gather_kernel, count), out_shape=jax.Sha...  23.8 us
    pallas_call x1, Pallas kernels, backproject(): pl.pallas_call(backproject_kernel, out_shape=jax.ShapeDtypeStruct((rows,...  7.38 us
    add x2, other arithmetic, smooth_inner(): centre + step_length * (smooth_weight * divergence - (centre - fidelity[1...  4.94 us
    convert_element_type x1, other arithmetic, footprint_mats(): return weights.astype(jnp.bfloat16)  2.36 us
    concatenate x2, other arithmetic, with_wide_halo(): return jnp.concatenate(bands, axis=0)  2.26 us
    sub x3, other arithmetic, across(): cells[:, :, 1:] - cells[:, :, :-1]  1.82 us
    ppermute x1, starting transfers between devices, with_halo(): lax.ppermute(tail, axis, [(i, (i + 1) % count) for i in range(ends)])  1.74 us
  transfers between devices with their start and end apart: 2, of which 0 were waited for; matrix products, arithmetic and copies ran while one was open for 7% of the time, Pallas kernels for 0%

profile of v21, /device:TPU:56, one launch (start us, length us, event | category | flops | bytes accessed | tf_op | source)
XLA Modules:
  0.0 83.6 jit_solution(12513244083193172948)
XLA Ops:
  0.0 1.0 %fusion.66 = (bf16[16,4,256]{2,1,0:T(4,128)(2,1)S(1)}, bf16[16,4,256]{2,1,0:T(4,128)(2,1)S(1)}) fusion(bf16[16,8,256]{2,1,0:T(8,128)(2,1)} %param.5), kind=kLoop, calls=%fused_computation.114 | loop fusion | bytes 131072 | tf_op jit(solution)/shard_map/slice | solution.py:32
  1.0 1.7 %collective-permute-start = (bf16[16,4,256]{2,1,0:T(4,128)(2,1)S(1)}, bf16[16,4,256]{2,1,0:T(4,128)(2,1)S(1)}, u32[]{:S(2)}, u32[]{:S(2)}) collective-permute-start(bf16[16,4,256]{2,1,0:T(4,128)(2,1)S(1)} %get-tuple-element.28), channel_id=1, source_target_pairs={{0,16},{16,32},{32,48},{48,64},{64,80},{80,96},{96,112},{112,128},... | collective-permute-start | bytes 98312 | tf_op jit(solution)/shard_map/ppermute | solution.py:35
  2.7 1.3 %collective-permute-start.1 = (bf16[16,4,256]{2,1,0:T(4,128)(2,1)S(1)}, bf16[16,4,256]{2,1,0:T(4,128)(2,1)S(1)}, u32[]{:S(2)}, u32[]{:S(2)}) collective-permute-start(bf16[16,4,256]{2,1,0:T(4,128)(2,1)S(1)} %get-tuple-element.29), channel_id=1, source_target_pairs={{16,0},{32,16},{48,32},{64,48},{80,64},{96,80},{112,96},{128,112},... | collective-permute-start | bytes 98312 | tf_op jit(solution)/shard_map/ppermute | solution.py:37
  4.1 0.7 convert_bitcast_fusion
  4.7 0.7 bitcast_add_fusion
  5.4 0.7 multiply_add_fusion.2
  6.1 0.1 sine_multiply_fusion
  6.3 0.1 broadcast_add_fusion
  6.4 0.1 pad_maximum_fusion
  6.8 0.7 fusion.62
  7.6 2.4 %divide_convert_fusion.mats_ref = bf16[16,4,128,128]{3,2,1,0:T(8,128)(2,1)} fusion(f32[16]{0:T(128)S(1)} %get-tuple-element.39, f32[16,4,128]{2,1,0:T(4,128)S(1)} %pad_maximum_fusion, f32[128]{0:T(128)S(1)} %convert_add_fusion.1), kind=kLoop, calls=%fused_computation | loop fusion | flops 7340032 | bytes 2130496 | tf_op jit(solution)/shard_map/vmap()/convert_element_type | solution.py:295
  10.0 0.8 %convolution_convert_fusion.local_ref = bf16[16,8,256]{2,1,0:T(8,128)(2,1)} fusion(bf16[16,4,256]{2,1,0:T(4,128)(2,1)S(1)} %collective-permute-done.1, bf16[16,8,256]{2,1,0:T(8,128)(2,1)S(1)} %copy-done.9, bf16[16,4,256]{2,1,0:T(4,128)(2,1)S(1)} %collective-permute-done, f32[16,8]{1,0:T(8,128)S(1)} %multiply_add_fusion.1, f32[16]{0:T(128)S(1)} %convert_add_fusion.3, ...), kind=kOutput, calls=%fused_computation.38 | convolution fusion | flops 1486848 | bytes 197440 | tf_op jit(solution)/shard_map/pzv,pvu->pzu/dot_general | solution.py:422
  10.9 23.8 %shard_map.55.columns_ref = bf16[16,8,4096]{2,1,0:T(8,128)(2,1)} custom-call(bf16[16,8,256]{2,1,0:T(8,128)(2,1)} %convolution_convert_fusion.local_ref), custom_call_target="tpu_custom_call" | custom-call | tf_op jit(solution)/shard_map/pallas_call | solution.py:132
  34.7 7.4 %shard_map.56.cells_ref = f32[4,8,4096]{2,1,0:T(8,128)} custom-call(s32[16,4,64]{2,1,0:T(4,128)} %shift_ref.1, bf16[16,8,4096]{2,1,0:T(8,128)(2,1)} %shard_map.55.columns_ref, bf16[16,4,128,128]{3,2,1,0:T(8,128)(2,1)} %divide_convert_fusion.mats_ref), custom_call_target="tpu_custom_call" | custom-call | tf_op jit(solution)/shard_map/pallas_call | solution.py:359
  42.1 31.0 %shard_map.57 = (f32[2,2,4096]{2,1,0:T(2,128)}, f32[2,8,4096]{2,1,0:T(8,128)}, f32[2,2,4096]{2,1,0:T(2,128)}, f32[4,2,4096]{2,1,0:T(2,128)}, f32[4,2,4096]{2,1,0...) custom-call(f32[4,8,4096]{2,1,0:T(8,128)} %shard_map.56.cells_ref), custom_call_target="tpu_custom_call" | custom-call | tf_op jit(solution)/shard_map/pallas_call | solution.py:191
  73.2 1.8 %maximum_maximum_fusion = f32[8,12,4096]{2,1,0:T(8,128)S(1)} fusion(f32[2,2,4096]{2,1,0:T(2,128)} %get-tuple-element.20, f32[2,8,4096]{2,1,0:T(8,128)} %get-tuple-element.19, f32[2,2,4096]{2,1,0:T(2,128)} %get-tuple-element.18, f32[4,2,4096]{2,1,0:T(2,128)} %get-tuple-element.17, f32[4,8,4096]{2,1,0:T(8,128)} %shard_map.56.cells_ref, ...), kind=kLoop, calls=%fused_computation.1 | loop fusion | flops 3145728 | bytes 3145728 | tf_op jit(solution)/shard_map/concatenate | solution.py:207
  75.1 0.4 maximum_maximum_fusion.2
  75.5 0.9 %slice_subtract_fusion = (f32[6,10,4095]{2,1,0:T(8,128)S(1)}, f32[6,10,4095]{2,1,0:T(8,128)S(1)}) fusion(f32[8,12,4096]{2,1,0:T(8,128)S(1)} %maximum_maximum_fusion), kind=kLoop, calls=%fused_computation.2 | loop fusion | flops 491400 | bytes 5896800 | tf_op jit(solution)/shard_map/sub | solution.py:387
  76.4 0.5 slice_subtract_fusion.2
  76.9 1.0 %fusion.25 = f32[6,10,4096]{2,1,0:T(8,128)S(1)} fusion(f32[6,10,4095]{2,1,0:T(8,128)S(1)} %get-tuple-element.22, f32[6]{0:T(128)S(1)} %get-tuple-element.35, f32[8,12,4096]{2,1,0:T(8,128)S(1)} %maximum_maximum_fusion, f32[6,12,4096]{2,1,0:T(8,128)S(1)} %get-tuple-element.27, f32[10]{0:T(128)S(1)} %get-tuple-element.37), kind=kLoop, calls=%fused_computation.37 | loop fusion | flops 2703360 | bytes 4915024 | tf_op jit(solution)/shard_map/mul | solution.py:408
  77.9 3.2 %fusion.13 = f32[6,10,4096]{2,1,0:T(8,128)S(1)} fusion(f32[6,12,4096]{2,1,0:T(8,128)S(1)} %get-tuple-element.27, f32[6,12,4096]{2,1,0:T(8,128)S(1)} %get-tuple-element.26, f32[6,10,4095]{2,1,0:T(8,128)S(1)} %bitcast.18, f32[6,10,4095]{2,1,0:T(8,128)S(1)} %get-tuple-element.21, f32[8,12,4096]{2,1,0:T(8,128)S(1)} %maximum_maximum_fusion, ...), kind=kLoop, calls=%fused_computation.17 | loop fusion | flops 11059200 | bytes 11795648 | tf_op jit(solution)/shard_map/add | solution.py:414
  81.1 0.5 slice_subtract_fusion.9
  81.6 0.3 fusion.51
  81.9 1.7 %fusion.39 = f32[4,8,4096]{2,1,0:T(8,128)} fusion(f32[6,10,4096]{2,1,0:T(8,128)S(1)} %fusion.13, f32[4,8,4096]{2,1,0:T(8,128)S(1)} %copy-done, f32[4,8,4095]{2,1,0:T(8,128)S(1)} %bitcast.19, f32[4,8,4095]{2,1,0:T(8,128)S(1)} %get-tuple-element.25, f32[4,8,4095]{2,1,0:T(8,128)S(1)} %get-tuple-element.23, f32[4,8,4095]{2,1,0:T(8,128)S(1)} %get-tuple-element.24, ...), kind=kLoop, calls=%fused_computation.54 | loop fusion | flops 5898240 | bytes 6815328 | tf_op jit(solution)/shard_map/add | solution.py:414
  (37 shorter events, 0.5 us)
Async XLA Ops:
  0.0 10.0 %copy-start.9 = (bf16[16,8,256]{2,1,0:T(8,128)(2,1)S(1)}, bf16[16,8,256]{2,1,0:T(8,128)(2,1)}, u32[]{:S(2)}) copy-start(bf16[16,8,256]{2,1,0:T(8,128)(2,1)} %param.5) | copy-start | bytes 196612
  1.0 9.0 %collective-permute-start = (bf16[16,4,256]{2,1,0:T(4,128)(2,1)S(1)}, bf16[16,4,256]{2,1,0:T(4,128)(2,1)S(1)}, u32[]{:S(2)}, u32[]{:S(2)}) collective-permute-start(bf16[16,4,256]{2,1,0:T(4,128)(2,1)S(1)} %get-tuple-element.28), channel_id=1, source_target_pairs={{0,16},{16,32},{32,48},{48,64},{64,80},{80,96},{96,112},{112,128},... | collective-permute-start | bytes 98312 | tf_op jit(solution)/shard_map/ppermute | solution.py:35
  2.7 7.3 %collective-permute-start.1 = (bf16[16,4,256]{2,1,0:T(4,128)(2,1)S(1)}, bf16[16,4,256]{2,1,0:T(4,128)(2,1)S(1)}, u32[]{:S(2)}, u32[]{:S(2)}) collective-permute-start(bf16[16,4,256]{2,1,0:T(4,128)(2,1)S(1)} %get-tuple-element.29), channel_id=1, source_target_pairs={{16,0},{32,16},{48,32},{64,48},{80,64},{96,80},{112,96},{128,112},... | collective-permute-start | bytes 98312 | tf_op jit(solution)/shard_map/ppermute | solution.py:37
  73.1 1.9 %copy-start = (f32[4,8,4096]{2,1,0:T(8,128)S(1)}, f32[4,8,4096]{2,1,0:T(8,128)}, u32[]{:S(2)}) copy-start(f32[4,8,4096]{2,1,0:T(8,128)} %shard_map.56.cells_ref) | copy-start | bytes 1572868
  73.1 1.9 %copy-start.1 = (f32[2,8,4096]{2,1,0:T(8,128)S(1)}, f32[2,8,4096]{2,1,0:T(8,128)}, u32[]{:S(2)}) copy-start(f32[2,8,4096]{2,1,0:T(8,128)} %get-tuple-element.14) | copy-start | bytes 786436
  73.1 1.9 %copy-start.2 = (f32[2,8,4096]{2,1,0:T(8,128)S(1)}, f32[2,8,4096]{2,1,0:T(8,128)}, u32[]{:S(2)}) copy-start(f32[2,8,4096]{2,1,0:T(8,128)} %get-tuple-element.19) | copy-start | bytes 786436
  73.1 1.9 %copy-start.3 = (f32[4,2,4096]{2,1,0:T(2,128)S(1)}, f32[4,2,4096]{2,1,0:T(2,128)}, u32[]{:S(2)}) copy-start(f32[4,2,4096]{2,1,0:T(2,128)} %get-tuple-element.16) | copy-start | bytes 393220
  73.1 1.9 %copy-start.4 = (f32[4,2,4096]{2,1,0:T(2,128)S(1)}, f32[4,2,4096]{2,1,0:T(2,128)}, u32[]{:S(2)}) copy-start(f32[4,2,4096]{2,1,0:T(2,128)} %get-tuple-element.17) | copy-start | bytes 393220
  73.1 1.9 %copy-start.5 = (f32[2,2,4096]{2,1,0:T(2,128)S(1)}, f32[2,2,4096]{2,1,0:T(2,128)}, u32[]{:S(2)}) copy-start(f32[2,2,4096]{2,1,0:T(2,128)} %get-tuple-element.13) | copy-start | bytes 196612
  73.1 1.9 %copy-start.6 = (f32[2,2,4096]{2,1,0:T(2,128)S(1)}, f32[2,2,4096]{2,1,0:T(2,128)}, u32[]{:S(2)}) copy-start(f32[2,2,4096]{2,1,0:T(2,128)} %get-tuple-element.15) | copy-start | bytes 196612
  73.2 1.9 %copy-start.7 = (f32[2,2,4096]{2,1,0:T(2,128)S(1)}, f32[2,2,4096]{2,1,0:T(2,128)}, u32[]{:S(2)}) copy-start(f32[2,2,4096]{2,1,0:T(2,128)} %get-tuple-element.18) | copy-start | bytes 196612
  73.2 1.9 %copy-start.8 = (f32[2,2,4096]{2,1,0:T(2,128)S(1)}, f32[2,2,4096]{2,1,0:T(2,128)}, u32[]{:S(2)}) copy-start(f32[2,2,4096]{2,1,0:T(2,128)} %get-tuple-element.20) | copy-start | bytes 196612
